TPU v7x, 32 devices: a whole 2x2x4 slice. The times are simulated.
32 devices in a mesh: row: 8 (over y, x, core), col: 4 (over z).
Axes of the slice: x: 2, y: 2, z: 4, core: 2. Of those that a mesh axis runs over, the one named last changes fastest.
Arguments:
- front_init: float32 [16384, 16384], P('row', 'col'), as said below
- child_tiles: bfloat16 [1024, 256, 256], P(('row', 'col'))
- child_dest: int32 [1024], P(('row', 'col')), may hold values from 0 to 4095, as said below
Outputs:
- panel_factor: float32 [16384, 1024], P('row')
- schur_update: float32 [16384, 16384], P('row', 'col')
Inputs may be any that keep to these rules, and one draw needn't show every extreme that they name: `child_dest`: t = 64 * tile row + tile column. A tile held at col index c has its tile column in c * 16 to (c + 1) * 16 - 1. Of one device's tiles at most 4 have tile rows in one block of 8 tile rows, and in every column of the mesh one such block gets exactly 4 from every device of that column. The leading 1024 x 1024 block of front_init plus any child tiles added to it is strictly diagonally dominant.
All inputs are finite; a program needn't handle non-finite values.
Results may differ from a plain program's by a relative error of at most 0.0003.
Values may be sent and summed in bfloat16 or wider, within the bound.
No kernel may reach another device: no remote copies, remote signals or barrier semaphores. Data moves between devices by JAX's collectives and lax.ppermute only.
A program may use at most 256 MiB of HBM per device.

v0:
```python
import functools

import jax
import jax.numpy as jnp
from jax import lax
from jax.experimental import pallas as pl
from jax.experimental.pallas import tpu as pltpu
from jax.sharding import PartitionSpec as P


PW = 1024
CAP = 4
BLK = 128
KP = 256
GRP = 256
EXT = 16
CODE = 64.0
TOP = 32767.0
HI = lax.Precision.HIGHEST
F32 = jnp.float32
ANY = pl.BlockSpec(memory_space=pl.ANY)
VMEM_CAP = 58 << 20


def params(limit=VMEM_CAP):
    return pltpu.CompilerParams(vmem_limit_bytes=limit)


def dot_t(a, b, precision=HI):
    return lax.dot_general(
        a, b, (((1,), (1,)), ((), ())), precision=precision, preferred_element_type=F32
    )


def pack_kernel(idx_ref, src_ref, out_ref, held, sem_in, sem_out):
    slots = out_ref.shape[0]

    def fetch(s):
        return pltpu.make_async_copy(src_ref.at[idx_ref[s]], held.at[s], sem_in.at[s])

    def flush(s):
        return pltpu.make_async_copy(held.at[s], out_ref.at[s], sem_out.at[s])

    for s in range(slots):
        fetch(s).start()
    for s in range(slots):
        fetch(s).wait()
        flush(s).start()
    for s in range(slots):
        flush(s).wait()


def pack(index, tiles):
    slots = index.shape[0]
    shape = (slots,) + tiles.shape[1:]
    return pl.pallas_call(
        pack_kernel,
        out_shape=jax.ShapeDtypeStruct(shape, tiles.dtype),
        grid_spec=pltpu.PrefetchScalarGridSpec(
            num_scalar_prefetch=1,
            grid=(1,),
            in_specs=[ANY],
            out_specs=ANY,
            scratch_shapes=[
                pltpu.VMEM(shape, tiles.dtype),
                pltpu.SemaphoreType.DMA((slots,)),
                pltpu.SemaphoreType.DMA((slots,)),
            ],
        ),
        compiler_params=params(),
        name="pack",
    )(index, tiles)


PARTS = 4


def pick_kernel(idx_ref, *refs):
    sources, (out_ref, held, sem_in, sem_out) = refs[:-4], refs[-4:]
    step = out_ref.shape[0] // PARTS
    for i, source in enumerate(sources):

        @pl.when(idx_ref[0] == i)
        def _(source=source):
            for p in range(PARTS):
                at = pl.ds(p * step, step)
                pltpu.make_async_copy(source.at[at], held.at[at], sem_in.at[p]).start()

    flushes = []
    for p in range(PARTS):
        at = pl.ds(p * step, step)
        pltpu.make_async_copy(sources[0].at[at], held.at[at], sem_in.at[p]).wait()
        flush = pltpu.make_async_copy(held.at[at], out_ref.at[at], sem_out.at[p])
        flush.start()
        flushes.append(flush)
    for flush in flushes:
        flush.wait()


def pick(which, arrays):
    shape, dtype = arrays[0].shape, arrays[0].dtype
    return pl.pallas_call(
        pick_kernel,
        out_shape=jax.ShapeDtypeStruct(shape, dtype),
        grid_spec=pltpu.PrefetchScalarGridSpec(
            num_scalar_prefetch=1,
            grid=(1,),
            in_specs=[ANY] * len(arrays),
            out_specs=ANY,
            scratch_shapes=[
                pltpu.VMEM(shape, dtype),
                pltpu.SemaphoreType.DMA((PARTS,)),
                pltpu.SemaphoreType.DMA((PARTS,)),
            ],
        ),
        compiler_params=params(),
        name="pick",
    )(which.reshape(1).astype(jnp.int32), *arrays)


def bucket(rows, cols, high, wide, row_blocks, col_blocks):
    count = rows.shape[0]
    inside = (rows >= 0) & (cols < wide * col_blocks)
    key = jnp.where(inside, (rows // high) * col_blocks + cols // wide, row_blocks * col_blocks)
    at = jnp.arange(count)
    before = (key[None, :] < key[:, None]) | ((key[None, :] == key[:, None]) & (at[None, :] < at[:, None]))
    place = jnp.sum(before.astype(jnp.int32), axis=1)
    order = jnp.sum(jnp.where(place[None, :] == at[:, None], at[None, :], 0), axis=1).astype(jnp.int32)
    edges = jnp.arange(row_blocks * col_blocks + 1)
    starts = jnp.sum((key[None, :] < edges[:, None]).astype(jnp.int32), axis=1)
    return order, starts


def add_tiles(scalars, tiles_ref, out_ref, block, row0, col0):
    rows_ref, cols_ref, order_ref, starts_ref = scalars
    tile = tiles_ref.shape[1]

    def step(p, carry):
        t = order_ref[p]
        at = pl.ds(pl.multiple_of((rows_ref[t] - row0) * tile, tile), tile)
        to = pl.ds(pl.multiple_of((cols_ref[t] - col0) * tile, tile), tile)
        out_ref[at, to] += tiles_ref[t].astype(F32)
        return carry

    lax.fori_loop(starts_ref[block], starts_ref[block + 1], step, 0)


def panel_kernel(rows_ref, cols_ref, order_ref, starts_ref, front_ref, tiles_ref, out_ref):
    out_ref[...] = front_ref[...]
    i = pl.program_id(0)
    high = out_ref.shape[0] // tiles_ref.shape[1]
    add_tiles((rows_ref, cols_ref, order_ref, starts_ref), tiles_ref, out_ref, i, i * high, 0)


def panel(place_rows, place_cols, front, tiles):
    rows = front.shape[0]
    tile = tiles.shape[1]
    high = min(rows, 512)
    steps = rows // high
    order, starts = bucket(place_rows, place_cols, high // tile, PW // tile, steps, 1)
    return pl.pallas_call(
        panel_kernel,
        out_shape=jax.ShapeDtypeStruct((rows, PW), F32),
        grid_spec=pltpu.PrefetchScalarGridSpec(
            num_scalar_prefetch=4,
            grid=(steps,),
            in_specs=[
                pl.BlockSpec((high, PW), lambda i, *_: (i, 0)),
                pl.BlockSpec(tiles.shape, lambda i, *_: (0, 0, 0), pipeline_mode=pl.Buffered(1)),
            ],
            out_specs=pl.BlockSpec((high, PW), lambda i, *_: (i, 0)),
        ),
        compiler_params=params(),
        name="panel",
    )(place_rows, place_cols, order, starts, front, tiles)


def spread(x, s):
    return jnp.broadcast_to(x[s : s + 1, :], x.shape)


def factor_block(sym):
    groups = BLK // 8
    rows = [sym[8 * v : 8 * v + 8, :] for v in range(groups)]
    lane = lax.broadcasted_iota(jnp.int32, (8, BLK), 1)
    sub = lax.broadcasted_iota(jnp.int32, (8, BLK), 0)
    for v0 in range(groups):
        first = 8 * v0
        cur = rows[v0]
        cols = [jnp.broadcast_to(cur[:, first + k : first + k + 1], (8, BLK)) for k in range(8)]
        scaled, mults = [], []
        for jj in range(8):
            at = lane == first + jj
            below = sub > jj
            inv = 1.0 / spread(cols[jj], jj)
            rs = jnp.where(at, inv, spread(cur, jj) * inv)
            mult = [None if k <= jj else spread(cols[k], jj) * inv for k in range(8)]
            f = jnp.where(below, cols[jj], 0.0)
            cur = jnp.where(at & below, 0.0, cur) - f * rs
            for k in range(jj + 1, 8):
                cols[k] = cols[k] - f * mult[k]
            scaled.append(jnp.where((lane > first + jj) & (lane < first + 8), 0.0, rs))
            mults.append(mult)
        rows[v0] = cur
        inside = (lane >= first) & (lane < first + 8)
        for v in range(v0 + 1, groups):
            cols = [
                jnp.broadcast_to(rows[v][:, first + k : first + k + 1], (8, BLK))
                for k in range(8)
            ]
            new = jnp.where(inside, 0.0, rows[v])
            for jj in range(8):
                new = new - cols[jj] * scaled[jj]
                for k in range(jj + 1, 8):
                    cols[k] = cols[k] - cols[jj] * mults[jj][k]
            rows[v] = new
    return jnp.concatenate(rows, axis=0)


def inverse_block(sym):
    done = factor_block(sym)
    row = lax.broadcasted_iota(jnp.int32, (BLK, BLK), 0)
    col = lax.broadcasted_iota(jnp.int32, (BLK, BLK), 1)
    diag = jnp.sum(jnp.where(row == col, done, 0.0), axis=1, keepdims=True)
    unit = jnp.where(row > col, done, jnp.where(row == col, 1.0, 0.0))
    return unit * lax.rsqrt(diag)


def first_kernel(rows_ref, cols_ref, front_ref, *refs, sources):
    tiles, (l_ref, trail_ref, pivot, work) = refs[:sources], refs[sources:]
    pivot[...] = front_ref[...]
    tile = tiles[0].shape[1]
    side = PW // tile
    for r, tile_ref in enumerate(tiles):
        for s in range(CAP):
            row, col = rows_ref[r * CAP + s], cols_ref[r * CAP + s]

            @pl.when((row >= 0) & (row < side) & (col < side))
            def _(row=row, col=col, tile_ref=tile_ref, s=s):
                at = pl.ds(pl.multiple_of(row * tile, tile), tile)
                to = pl.ds(pl.multiple_of(col * tile, tile), tile)
                pivot[at, to] += tile_ref[s].astype(F32)

    for i in range(PW // KP):
        for j in range(i + 1):
            si, sj = pl.ds(i * KP, KP), pl.ds(j * KP, KP)
            work[si, sj] = (pivot[si, sj] + pivot[sj, si].T) * 0.5
    eliminate(l_ref, trail_ref, work)


def next_kernel(a_ref, l_ref, *rest):
    work = rest[-1]
    work[...] = a_ref[...]
    eliminate(l_ref, rest[0] if len(rest) == 2 else None, work)


def eliminate(l_ref, trail_ref, work):
    n = work.shape[0]

    def step(b, carry):
        r0 = pl.multiple_of(b * BLK, BLK)
        inv = inverse_block(work[pl.ds(r0, BLK), pl.ds(r0, BLK)])
        l_ref[pl.ds(r0, BLK), pl.ds(r0, BLK)] = inv

        @pl.when(b == 0)
        def _():
            l_ref[0:BLK, BLK:KP] = jnp.zeros((BLK, KP - BLK), F32)
            low = dot_t(work[BLK:n, 0:BLK], inv)
            l_ref[BLK:n, 0:BLK] = low
            work[BLK:n, BLK:KP] -= dot_t(low, low[0:BLK])

        @pl.when(b == 1)
        def _():
            side = jnp.dot(
                l_ref[BLK:KP, 0:BLK], l_ref[0:BLK, 0:BLK], precision=HI, preferred_element_type=F32
            )
            l_ref[BLK:KP, 0:BLK] = -jnp.dot(inv, side, precision=HI, preferred_element_type=F32)
            if n > KP:
                l_ref[KP:n, BLK:KP] = dot_t(work[KP:n, BLK:KP], inv)

        return carry

    lax.fori_loop(0, KP // BLK, step, 0)
    if trail_ref is not None:
        m = n - KP
        for j in range(m // KP):
            rows = slice(j * KP, m)
            cols = slice(j * KP, (j + 1) * KP)
            low = l_ref[KP + j * KP : n, :]
            trail_ref[rows, cols] = work[KP + j * KP : n, KP + j * KP : KP + (j + 1) * KP] - dot_t(
                low, low[0:KP]
            )


def whole(shape):
    return pl.BlockSpec(shape, lambda i, *_: (0,) * len(shape))


def chol_first(place_rows, place_cols, front, gathered):
    shapes = [jax.ShapeDtypeStruct((PW, KP), F32), jax.ShapeDtypeStruct((PW - KP, PW - KP), F32)]
    return pl.pallas_call(
        functools.partial(first_kernel, sources=len(gathered)),
        out_shape=shapes,
        grid_spec=pltpu.PrefetchScalarGridSpec(
            num_scalar_prefetch=2,
            grid=(1,),
            in_specs=[whole((PW, PW))] + [whole(g.shape) for g in gathered],
            out_specs=[whole(s.shape) for s in shapes],
            scratch_shapes=[pltpu.VMEM((PW, PW), F32)] * 2,
        ),
        compiler_params=params(),
        name="chol",
    )(place_rows, place_cols, front, *gathered)


def chol_next(a):
    n = a.shape[0]
    shapes = [jax.ShapeDtypeStruct((n, KP), F32)]
    if n > KP:
        shapes.append(jax.ShapeDtypeStruct((n - KP, n - KP), F32))
    return pl.pallas_call(
        next_kernel,
        out_shape=shapes,
        grid=(1,),
        in_specs=[whole((n, n))],
        out_specs=[whole(s.shape) for s in shapes],
        scratch_shapes=[pltpu.VMEM((n, n), F32)],
        compiler_params=params(),
        name="chol",
    )(a)


def eye(n):
    return lax.broadcasted_iota(jnp.int32, (n, n), 0) == lax.broadcasted_iota(jnp.int32, (n, n), 1)


def solve_kernel(p_ref, *refs, k):
    factors, lowers = refs[:k], refs[k : 2 * k + 1]
    f_ref, q_ref = refs[2 * k + 1 :]
    for g in range(q_ref.shape[0]):
        at = slice(g * GRP, (g + 1) * GRP)
        acc = p_ref[at, :]
        for j in range(k):
            acc = acc - dot_t(factors[j][at, :], lowers[j][(k - j) * KP : (k - j + 1) * KP, :])
        f = dot_t(acc, lowers[k][0:KP, :])
        f_ref[at, :] = f
        peak = jnp.maximum(jnp.max(jnp.abs(f), axis=1, keepdims=True), 1e-30)
        code = jnp.ceil(jnp.log2(peak) * CODE)
        q = jnp.clip(jnp.round(f * (jnp.exp2(code * (-1.0 / CODE)) * TOP)), -TOP, TOP)
        q_ref[g, 0:GRP, :] = q.astype(jnp.int32).astype(jnp.int16)
        codes = jnp.sum(jnp.where(eye(GRP), code, 0.0), axis=0, keepdims=True)
        codes = jnp.broadcast_to(codes, (EXT, GRP))
        q_ref[g, GRP : GRP + EXT, :] = codes.astype(jnp.int32).astype(jnp.int16)


def solve(panel_sum, factors, lowers):
    k = len(factors)
    rows = panel_sum.shape[0]
    high = min(rows, 4 * GRP)
    block = pl.BlockSpec((high, KP), lambda i: (i, 0))
    return pl.pallas_call(
        functools.partial(solve_kernel, k=k),
        out_shape=[
            jax.ShapeDtypeStruct((rows, KP), F32),
            jax.ShapeDtypeStruct((rows // GRP, GRP + EXT, KP), jnp.int16),
        ],
        grid=(rows // high,),
        in_specs=[pl.BlockSpec((high, KP), lambda i: (i, k))]
        + [block] * k
        + [pl.BlockSpec(low.shape, lambda i: (0, 0)) for low in lowers],
        out_specs=[block, pl.BlockSpec((high // GRP, GRP + EXT, KP), lambda i: (i, 0, 0))],
        compiler_params=params(),
        name="solve",
    )(panel_sum, *factors, *lowers)


def decode(q_ref, g):
    codes = q_ref[g, GRP : GRP + EXT, :].astype(jnp.int32).astype(F32)[0:1, :]
    code = jnp.sum(jnp.where(eye(GRP), codes, 0.0), axis=1, keepdims=True)
    scale = jnp.exp2(code * (1.0 / CODE)) * (1.0 / TOP)
    return q_ref[g, 0:GRP, :].astype(jnp.int32).astype(F32) * scale


def halves(x):
    high = x.astype(jnp.bfloat16)
    return high, (x - high.astype(F32)).astype(jnp.bfloat16)


def schur_kernel(rows_ref, cols_ref, order_ref, starts_ref, member_ref, front_ref, tiles_ref, *refs, count):
    own, mine, other = refs[:count], refs[count : 2 * count], refs[2 * count : 3 * count]
    f_ref, out_ref, fh_ref, fl_ref, sh_ref, sl_ref = refs[3 * count :]
    i, j = pl.program_id(0), pl.program_id(1)
    groups = mine[0].shape[0]
    tile = tiles_ref.shape[1]

    @pl.when((i == 0) & (j == 0))
    def _():
        def step(g, carry):
            for e, strip in enumerate((mine, other)):
                member = member_ref[0] if e == 0 else 1 - member_ref[0]
                at = pl.ds(pl.multiple_of((member * groups + g) * GRP, GRP), GRP)
                for k in range(count):
                    high, low = halves(decode(strip[k], g))
                    sh_ref[at, k * KP : (k + 1) * KP] = high
                    sl_ref[at, k * KP : (k + 1) * KP] = low
            return carry

        lax.fori_loop(0, groups, step, 0)

    @pl.when(j == 0)
    def _():
        def step(g, carry):
            at = pl.ds(pl.multiple_of(g * GRP, GRP), GRP)
            for k in range(count):
                f = decode(own[k], g)
                f_ref[at, k * KP : (k + 1) * KP] = f
                high, low = halves(f)
                fh_ref[at, k * KP : (k + 1) * KP] = high
                fl_ref[at, k * KP : (k + 1) * KP] = low
            return carry

        lax.fori_loop(0, own[0].shape[0], step, 0)

    high, wide = out_ref.shape
    at = pl.ds(pl.multiple_of(j * wide, wide), wide)
    fh, fl, sh, sl = fh_ref[...], fl_ref[...], sh_ref[at, :], sl_ref[at, :]
    out_ref[...] = front_ref[...] - (dot_t(fh, sh, None) + (dot_t(fh, sl, None) + dot_t(fl, sh, None)))
    block = i * pl.num_programs(1) + j
    scalars = (rows_ref, cols_ref, order_ref, starts_ref)
    add_tiles(scalars, tiles_ref, out_ref, block, i * (high // tile), j * (wide // tile))


def schur(place_rows, place_cols, member, front, tiles, own, mine, other):
    rows, cols = front.shape
    count = len(own)
    once = pl.Buffered(1)
    high, wide = min(rows, 1024), min(cols, 512)
    depth = count * KP
    tile = tiles.shape[1]
    order, starts = bucket(place_rows, place_cols, high // tile, wide // tile, rows // high, cols // wide)
    block = pl.BlockSpec((high, wide), lambda i, j, *_: (i, j))
    coded = pl.BlockSpec((high // GRP, GRP + EXT, KP), lambda i, j, *_: (i, 0, 0))
    strip = pl.BlockSpec(mine[0].shape, lambda i, j, *_: (0, 0, 0), pipeline_mode=once)
    return pl.pallas_call(
        functools.partial(schur_kernel, count=count),
        out_shape=[jax.ShapeDtypeStruct((rows, PW), F32), jax.ShapeDtypeStruct((rows, cols), F32)],
        grid_spec=pltpu.PrefetchScalarGridSpec(
            num_scalar_prefetch=5,
            grid=(rows // high, cols // wide),
            in_specs=[block, pl.BlockSpec(tiles.shape, lambda i, j, *_: (0, 0, 0), pipeline_mode=once)]
            + [coded] * count
            + [strip] * (2 * count),
            out_specs=[pl.BlockSpec((high, depth), lambda i, j, *_: (i, 0)), block],
            scratch_shapes=[pltpu.VMEM((high, depth), jnp.bfloat16)] * 2
            + [pltpu.VMEM((cols, depth), jnp.bfloat16)] * 2,
        ),
        compiler_params=params(),
        name="schur",
    )(place_rows, place_cols, order, starts, member, front, tiles, *own, *mine, *other)


def gray(n):
    return [i ^ (i >> 1) for i in range(n)]


def ring_pairs(row_count, col_count, hop):
    chips = row_count // 2
    order = gray(chips)
    pairs = []
    for col in range(col_count):
        at = order.index(col)
        for member in range(2):
            way = 1 if member == 0 else -1
            src = order[(at + way * (hop - 1)) % chips] * 2 + member
            dst = order[(at + way * hop) % chips] * 2 + member
            pairs.append((src * col_count + col, dst * col_count + col))
    return pairs


def body(front_init, child_tiles, child_dest):
    row_count = lax.axis_size("row")
    col_count = lax.axis_size("col")
    if row_count != 2 * col_count:
        raise ValueError("mesh shape")
    row_extent, col_extent = front_init.shape
    tile_width = child_tiles.shape[1]
    tile_grid = col_extent * col_count // tile_width
    row_tiles = row_extent // tile_width
    col_tiles = col_extent // tile_width
    tile_count = child_tiles.shape[0]
    row_index = lax.axis_index("row")
    col_index = lax.axis_index("col")

    tile_row = child_dest // tile_grid
    tile_col = child_dest % tile_grid
    owner_row = tile_row // row_tiles
    local_tile = (tile_row - owner_row * row_tiles) * col_tiles + (tile_col - col_index * col_tiles)
    positions = jnp.arange(tile_count)
    earlier = positions[None, :] < positions[:, None]
    same_owner = owner_row[:, None] == owner_row[None, :]
    send_rank = jnp.sum((same_owner & earlier).astype(jnp.int32), axis=1)
    send_slot = owner_row * CAP + send_rank
    slots = jnp.arange(row_count * CAP)
    hit = slots[:, None] == send_slot[None, :]
    index = jnp.sum(jnp.where(hit, positions[None, :], 0), axis=1).astype(jnp.int32)
    targets = jnp.sum(jnp.where(hit, local_tile[None, :] + 1, 0), axis=1).astype(jnp.int32) - 1
    places = lax.all_to_all(targets, "row", split_axis=0, concat_axis=0, tiled=True)
    place_rows = jnp.where(places < 0, -1, places // col_tiles)
    place_cols = places % col_tiles

    both = ("row", "col")
    chips = row_count // 2
    member = row_index % 2
    order = jnp.array(gray(chips))
    here = jnp.argmax(order == row_index // 2)
    there = jnp.argmax(order == col_index)
    distance = jnp.where(member == 0, here - there, there - here) % chips
    swap = [(r * col_count + c, (r ^ 1) * col_count + c) for r in range(row_count) for c in range(col_count)]

    first = pack(index[:CAP], child_tiles)
    gathered = [first]
    for r in range(1, row_count):
        gathered.append(lax.ppermute(first, both, [(r * col_count, 0)]))
    outgoing = pack(index, child_tiles)
    arrived = lax.all_to_all(outgoing, "row", split_axis=0, concat_axis=0, tiled=True)
    panel_sum = panel(place_rows, place_cols, front_init, arrived)

    own, mine, other, factors, lowers = [], [], [], [], []
    pivot = None
    for k in range(PW // KP):
        if k == 0:
            result = chol_first(place_rows, place_cols, front_init, gathered)
        else:
            result = chol_next(pivot)
        pivot = result[-1]
        held = [result[0]]
        for chip in range(1, chips):
            parent = above(chip)
            pair = (2 * parent * col_count, 2 * chip * col_count)
            held.append(lax.ppermute(held[parent], both, [pair]))
        even = pick(row_index // 2, held)
        odd = lax.ppermute(even, both, [(2 * c * col_count, (2 * c + 1) * col_count) for c in range(chips)])
        lowers.append(pick(member, [even, odd]))
        factor, coded = solve(panel_sum, factors, lowers)
        factors.append(factor)
        steps = [coded]
        for hop in range(col_count - 1):
            steps.append(lax.ppermute(steps[-1], "col", [(hop, hop + 1)]))
        own.append(pick(col_index, steps))
        steps = [own[-1]]
        for hop in range(1, chips):
            steps.append(lax.ppermute(steps[-1], both, ring_pairs(row_count, col_count, hop)))
        mine.append(pick(distance, steps))
        other.append(lax.ppermute(mine[-1], both, swap))

    panel_factor, schur_update = schur(
        place_rows, place_cols, member.reshape(1).astype(jnp.int32), front_init, arrived, own, mine, other
    )
    return (panel_factor, schur_update)


def above(chip):
    return chip - (1 << (chip.bit_length() - 1))


def solution(mesh):
    return jax.shard_map(
        body,
        mesh=mesh,
        in_specs=(P("row", "col"), P(("row", "col"), None, None), P(("row", "col"))),
        out_specs=(P("row", None), P("row", "col")),
        check_vma=False,
    )
```

profile of v0, /device:TPU:0, one launch (start us, length us, event | category | flops | bytes accessed | tf_op | source)
XLA Modules:
  0.0 520.0 jit_solution(16264641691377194767)
XLA Ops:
  2.2 2.5 pack.3.refs_0_
  11.2 9.2 %collective-permute-done.6.refs_7_ = bf16[4,256,256]{2,1,0:T(8,128)(2,1)S(1)} collective-permute-done((bf16[4,256,256]{2,1,0:T(8,128)(2,1)}, bf16[4,256,256]{2,1,0:T(8,128)(2,1)S(1)}, u32[]{:S(2)}, u32[]{:S(2)}) %collective-permute-start.6) | collective-permute-done | bytes 524320 | tf_op jit(solution)/shard_map/ppermute | solution.py:523
  24.1 3.7 all-to-all-start
  27.8 5.2 pack.2
  33.4 4.6 all-to-all-start.1
  41.2 18.7 %chol.4 = (f32[1024,256]{1,0:T(8,128)}, f32[768,768]{1,0:T(8,128)}) custom-call(s32[32]{0:T(128)} %get-tuple-element.36.rows_ref, s32[32]{0:T(128)} %get-tuple-element.35.cols_ref, f32[2048,4096]{1,0:T(8,128)} %front_ref.5, bf16[4,256,256]{2,1,0:T(8,128)(2,1)} %pack.3.refs_0_, bf16[4,256,256]{2,1,0:T(8,128)(2,1)} %collective-permute-done.refs_1_, ...), custom_call_target="tpu_custom_call" | custom-call | tf_op jit(solution)/shard_map/chol/pallas_call | solution.py:301
  59.9 4.1 collective-permute-start.7
  64.0 13.7 %chol.5 = (f32[768,256]{1,0:T(8,128)}, f32[512,512]{1,0:T(8,128)}) custom-call(f32[768,768]{1,0:T(8,128)} %get-tuple-element.20.a_ref), custom_call_target="tpu_custom_call" | custom-call | tf_op jit(solution)/shard_map/chol/pallas_call | solution.py:321
  77.7 2.2 collective-permute-start.14
  81.3 14.2 %collective-permute-done.7.refs_1_ = f32[1024,256]{1,0:T(8,128)S(1)} collective-permute-done((f32[1024,256]{1,0:T(8,128)}, f32[1024,256]{1,0:T(8,128)S(1)}, u32[]{:S(2)}, u32[]{:S(2)}) %collective-permute-start.7) | collective-permute-done | bytes 1048608 | tf_op jit(solution)/shard_map/ppermute | solution.py:540
  95.6 1.7 collective-permute-start.9
  97.2 2.2 collective-permute-start.15
  99.4 11.9 %chol.6 = (f32[512,256]{1,0:T(8,128)}, f32[256,256]{1,0:T(8,128)}) custom-call(f32[512,512]{1,0:T(8,128)} %get-tuple-element.24.a_ref), custom_call_target="tpu_custom_call" | custom-call | tf_op jit(solution)/shard_map/chol/pallas_call | solution.py:321
  111.3 5.1 collective-permute-start.21
  116.4 1.5 collective-permute-start.16
  117.9 4.7 collective-permute-done.21.refs_1_
  122.6 2.1 collective-permute-start.22
  126.2 2.0 pick.16.refs_0_
  128.2 1.6 collective-permute-start.10
  129.8 10.8 %chol.7.refs_0_ = f32[256,256]{1,0:T(8,128)} custom-call(f32[256,256]{1,0:T(8,128)} %get-tuple-element.28.a_ref), custom_call_target="tpu_custom_call" | custom-call | tf_op jit(solution)/shard_map/chol/pallas_call | solution.py:321
  140.6 4.5 collective-permute-start.28
  145.1 2.0 pick.19.refs_0_
  151.3 1.8 pick.22.refs_0_
  155.9 1.6 pick.25.refs_0_
  161.1 1.6 pick.26.refs_6_
  163.5 1.8 pick.23.refs_4_.refs_5_
  166.2 2.0 pick.20.refs_2_.refs_3_.refs_4_
  169.2 2.0 pick.17.refs_0_.refs_1_.refs_2_.refs_3_
  171.2 9.2 %panel.1.p_ref = f32[2048,1024]{1,0:T(8,128)} custom-call(s32[32]{0:T(128)} %get-tuple-element.36.rows_ref, s32[32]{0:T(128)} %get-tuple-element.35.cols_ref, s32[32]{0:T(128)} %select_reduce_fusion.order_ref, s32[5]{0:T(128)} %convert_reduce_fusion.4.starts_ref, f32[2048,4096]{1,0:T(8,128)} %front_ref.5, bf16[32,256,256]{2,1,0:T(8,128)(2,1)} %all-to-all-done.1.tiles_ref), custom_call_target="tpu_custom_call" | custom-call | tf_op jit(solution)/shard_map/panel/pallas_call | solution.py:161
  180.4 5.1 solve.4
  186.8 8.2 %solve.5 = (f32[2048,256]{1,0:T(8,128)}, s16[8,272,256]{2,1,0:T(8,128)(2,1)}) custom-call(f32[2048,1024]{1,0:T(8,128)} %panel.1.p_ref, f32[2048,256]{1,0:T(8,128)} %get-tuple-element.19.refs_0_, f32[1024,256]{1,0:T(8,128)} %pick.17.refs_0_.refs_1_.refs_2_.refs_3_, f32[768,256]{1,0:T(8,128)} %pick.20.refs_2_.refs_3_.refs_4_), custom_call_target="tpu_custom_call" | custom-call | tf_op jit(solution)/shard_map/solve/pallas_call | solution.py:361
  195.0 1.6 collective-permute-start.18
  196.6 11.8 %solve.6 = (f32[2048,256]{1,0:T(8,128)}, s16[8,272,256]{2,1,0:T(8,128)(2,1)}) custom-call(f32[2048,1024]{1,0:T(8,128)} %panel.1.p_ref, f32[2048,256]{1,0:T(8,128)} %get-tuple-element.19.refs_0_, f32[2048,256]{1,0:T(8,128)} %get-tuple-element.23.refs_1_, f32[1024,256]{1,0:T(8,128)} %pick.17.refs_0_.refs_1_.refs_2_.refs_3_, ...), custom_call_target="tpu_custom_call" | custom-call | tf_op jit(solution)/shard_map/solve/pallas_call | solution.py:361
  208.4 13.7 %solve.7 = (f32[2048,256]{1,0:T(8,128)}, s16[8,272,256]{2,1,0:T(8,128)(2,1)}) custom-call(f32[2048,1024]{1,0:T(8,128)} %panel.1.p_ref, f32[2048,256]{1,0:T(8,128)} %get-tuple-element.19.refs_0_, f32[2048,256]{1,0:T(8,128)} %get-tuple-element.23.refs_1_, f32[2048,256]{1,0:T(8,128)} %get-tuple-element.27.refs_2_, ...), custom_call_target="tpu_custom_call" | custom-call | tf_op jit(solution)/shard_map/solve/pallas_call | solution.py:361
  225.6 10.3 %collective-permute-done.18.refs_1_ = s16[8,272,256]{2,1,0:T(8,128)(2,1)S(1)} collective-permute-done((s16[8,272,256]{2,1,0:T(8,128)(2,1)}, s16[8,272,256]{2,1,0:T(8,128)(2,1)S(1)}, u32[]{:S(2)}, u32[]{:S(2)}) %collective-permute-start.18) | collective-permute-done | bytes 1114144 | tf_op jit(solution)/shard_map/ppermute | solution.py:548
  236.6 23.1 %collective-permute-done.32.refs_1_ = s16[8,272,256]{2,1,0:T(8,128)(2,1)S(1)} collective-permute-done((s16[8,272,256]{2,1,0:T(8,128)(2,1)}, s16[8,272,256]{2,1,0:T(8,128)(2,1)S(1)}, u32[]{:S(2)}, u32[]{:S(2)}) %collective-permute-start.32) | collective-permute-done | bytes 1114144 | tf_op jit(solution)/shard_map/ppermute | solution.py:548
  259.7 1.7 collective-permute-start.33
  261.4 21.6 %collective-permute-done.25.refs_1_ = s16[8,272,256]{2,1,0:T(8,128)(2,1)S(1)} collective-permute-done((s16[8,272,256]{2,1,0:T(8,128)(2,1)S(1)}, s16[8,272,256]{2,1,0:T(8,128)(2,1)S(1)}, u32[]{:S(2)}, u32[]{:S(2)}) %collective-permute-start.25) | collective-permute-done | bytes 1114144 | tf_op jit(solution)/shard_map/ppermute | solution.py:548
  284.5 1.7 collective-permute-start.20
  286.2 1.7 collective-permute-start.34
  287.9 1.7 collective-permute-start.27
  290.6 2.0 pick.18.refs_0_
  292.7 4.4 collective-permute-start.35
  297.1 2.1 pick.21.refs_0_.refs_1_
  300.5 2.1 pick.27.refs_0_.refs_3_
  304.0 2.1 pick.24.refs_0_.refs_2_
  307.4 2.9 collective-permute-done.35.refs_1_
  310.3 38.3 %collective-permute-start.36 = (s16[8,272,256]{2,1,0:T(8,128)(2,1)S(1)}, s16[8,272,256]{2,1,0:T(8,128)(2,1)}, u32[]{:S(2)}, u32[]{:S(2)}) collective-permute-start(s16[8,272,256]{2,1,0:T(8,128)(2,1)S(1)} %collective-permute-done.35.refs_1_), channel_id=1, source_target_pairs={{8,24},{20,28},{25,17},{5,21},{2,10},{30,14},{19,3},{15,7}} | collective-permute-start | bytes 3342344 | tf_op jit(solution)/shard_map/ppermute | solution.py:552
  348.6 7.4 %collective-permute-start.39 = (s16[8,272,256]{2,1,0:T(8,128)(2,1)S(1)}, s16[8,272,256]{2,1,0:T(8,128)(2,1)}, u32[]{:S(2)}, u32[]{:S(2)}) collective-permute-start(s16[8,272,256]{2,1,0:T(8,128)(2,1)S(1)} %collective-permute-done.38.refs_1_), channel_id=1, source_target_pairs={{8,24},{20,28},{25,17},{5,21},{2,10},{30,14},{19,3},{15,7}} | collective-permute-start | bytes 3342344 | tf_op jit(solution)/shard_map/ppermute | solution.py:552
  355.9 7.4 %collective-permute-start.45 = (s16[8,272,256]{2,1,0:T(8,128)(2,1)S(1)}, s16[8,272,256]{2,1,0:T(8,128)(2,1)}, u32[]{:S(2)}, u32[]{:S(2)}) collective-permute-start(s16[8,272,256]{2,1,0:T(8,128)(2,1)S(1)} %collective-permute-done.44.refs_1_), channel_id=1, source_target_pairs={{8,24},{20,28},{25,17},{5,21},{2,10},{30,14},{19,3},{15,7}} | collective-permute-start | bytes 3342344 | tf_op jit(solution)/shard_map/ppermute | solution.py:552
  363.3 10.9 %collective-permute-start.42 = (s16[8,272,256]{2,1,0:T(8,128)(2,1)S(1)}, s16[8,272,256]{2,1,0:T(8,128)(2,1)}, u32[]{:S(2)}, u32[]{:S(2)}) collective-permute-start(s16[8,272,256]{2,1,0:T(8,128)(2,1)S(1)} %collective-permute-done.41.refs_1_), channel_id=1, source_target_pairs={{8,24},{20,28},{25,17},{5,21},{2,10},{30,14},{19,3},{15,7}} | collective-permute-start | bytes 3342344 | tf_op jit(solution)/shard_map/ppermute | solution.py:552
  374.3 7.4 %collective-permute-start.37 = (s16[8,272,256]{2,1,0:T(8,128)(2,1)}, s16[8,272,256]{2,1,0:T(8,128)(2,1)}, u32[]{:S(2)}, u32[]{:S(2)}) collective-permute-start(s16[8,272,256]{2,1,0:T(8,128)(2,1)} %collective-permute-done.36.refs_2_), channel_id=1, source_target_pairs={{24,16},{28,12},{17,1},{21,29},{10,26},{14,6},{3,11},{7,23}} | collective-permute-start | bytes 3342344 | tf_op jit(solution)/shard_map/ppermute | solution.py:552
  381.6 7.4 %collective-permute-start.40 = (s16[8,272,256]{2,1,0:T(8,128)(2,1)}, s16[8,272,256]{2,1,0:T(8,128)(2,1)}, u32[]{:S(2)}, u32[]{:S(2)}) collective-permute-start(s16[8,272,256]{2,1,0:T(8,128)(2,1)} %collective-permute-done.39.refs_2_), channel_id=1, source_target_pairs={{24,16},{28,12},{17,1},{21,29},{10,26},{14,6},{3,11},{7,23}} | collective-permute-start | bytes 3342344 | tf_op jit(solution)/shard_map/ppermute | solution.py:552
  389.0 7.4 %collective-permute-start.46 = (s16[8,272,256]{2,1,0:T(8,128)(2,1)}, s16[8,272,256]{2,1,0:T(8,128)(2,1)}, u32[]{:S(2)}, u32[]{:S(2)}) collective-permute-start(s16[8,272,256]{2,1,0:T(8,128)(2,1)} %collective-permute-done.45.refs_2_), channel_id=1, source_target_pairs={{24,16},{28,12},{17,1},{21,29},{10,26},{14,6},{3,11},{7,23}} | collective-permute-start | bytes 3342344 | tf_op jit(solution)/shard_map/ppermute | solution.py:552
  396.4 8.1 %collective-permute-start.43 = (s16[8,272,256]{2,1,0:T(8,128)(2,1)}, s16[8,272,256]{2,1,0:T(8,128)(2,1)}, u32[]{:S(2)}, u32[]{:S(2)}) collective-permute-start(s16[8,272,256]{2,1,0:T(8,128)(2,1)} %collective-permute-done.42.refs_2_), channel_id=1, source_target_pairs={{24,16},{28,12},{17,1},{21,29},{10,26},{14,6},{3,11},{7,23}} | collective-permute-start | bytes 3342344 | tf_op jit(solution)/shard_map/ppermute | solution.py:552
  408.5 2.0 pick.28.refs_4_
  410.5 5.8 %collective-permute-start.47 = (s16[8,272,256]{2,1,0:T(8,128)(2,1)}, s16[8,272,256]{2,1,0:T(8,128)(2,1)S(1)}, u32[]{:S(2)}, u32[]{:S(2)}) collective-permute-start(s16[8,272,256]{2,1,0:T(8,128)(2,1)} %pick.28.refs_4_), channel_id=1, source_target_pairs={{0,4},{1,5},{2,6},{3,7},{4,0},{5,1},{6,2},{7,3},{8,12},{9,13},{10,... | collective-permute-start | bytes 3342344 | tf_op jit(solution)/shard_map/ppermute | solution.py:554
  416.3 2.1 pick.29.refs_5_
  418.4 5.8 %collective-permute-start.48 = (s16[8,272,256]{2,1,0:T(8,128)(2,1)}, s16[8,272,256]{2,1,0:T(8,128)(2,1)S(1)}, u32[]{:S(2)}, u32[]{:S(2)}) collective-permute-start(s16[8,272,256]{2,1,0:T(8,128)(2,1)} %pick.29.refs_5_), channel_id=1, source_target_pairs={{0,4},{1,5},{2,6},{3,7},{4,0},{5,1},{6,2},{7,3},{8,12},{9,13},{10,... | collective-permute-start | bytes 3342344 | tf_op jit(solution)/shard_map/ppermute | solution.py:554
  424.2 2.0 pick.31.refs_7_
  426.2 6.1 %collective-permute-start.50 = (s16[8,272,256]{2,1,0:T(8,128)(2,1)}, s16[8,272,256]{2,1,0:T(8,128)(2,1)S(1)}, u32[]{:S(2)}, u32[]{:S(2)}) collective-permute-start(s16[8,272,256]{2,1,0:T(8,128)(2,1)} %pick.31.refs_7_), channel_id=1, source_target_pairs={{0,4},{1,5},{2,6},{3,7},{4,0},{5,1},{6,2},{7,3},{8,12},{9,13},{10,... | collective-permute-start | bytes 3342344 | tf_op jit(solution)/shard_map/ppermute | solution.py:554
  432.3 2.0 pick.30.refs_6_
  434.4 5.8 %collective-permute-start.49 = (s16[8,272,256]{2,1,0:T(8,128)(2,1)}, s16[8,272,256]{2,1,0:T(8,128)(2,1)S(1)}, u32[]{:S(2)}, u32[]{:S(2)}) collective-permute-start(s16[8,272,256]{2,1,0:T(8,128)(2,1)} %pick.30.refs_6_), channel_id=1, source_target_pairs={{0,4},{1,5},{2,6},{3,7},{4,0},{5,1},{6,2},{7,3},{8,12},{9,13},{10,... | collective-permute-start | bytes 3342344 | tf_op jit(solution)/shard_map/ppermute | solution.py:554
  444.4 75.2 %schur.1 = (f32[2048,1024]{1,0:T(8,128)}, f32[2048,4096]{1,0:T(8,128)}) custom-call(s32[32]{0:T(128)} %get-tuple-element.36.rows_ref, s32[32]{0:T(128)} %get-tuple-element.35.cols_ref, s32[32]{0:T(128)} %select_reduce_fusion.2.order_ref, s32[17]{0:T(128)} %convert_reduce_fusion.3.starts_ref, s32[1]{0:T(128)} %bitcast.1.idx_ref.member_ref, ...), custom_call_target="tpu_custom_call" | custom-call | tf_op jit(solution)/shard_map/schur/pallas_call | solution.py:444
  (163 shorter events, 49.1 us)
Async XLA Ops:
  4.7 15.7 %collective-permute-start.6 = (bf16[4,256,256]{2,1,0:T(8,128)(2,1)}, bf16[4,256,256]{2,1,0:T(8,128)(2,1)S(1)}, u32[]{:S(2)}, u32[]{:S(2)}) collective-permute-start(bf16[4,256,256]{2,1,0:T(8,128)(2,1)} %pack.3.refs_0_), channel_id=1, source_target_pairs={{28,0}} | collective-permute-start | bytes 1572872 | tf_op jit(solution)/shard_map/ppermute | solution.py:523
  6.0 16.1 %collective-permute-start.5 = (bf16[4,256,256]{2,1,0:T(8,128)(2,1)}, bf16[4,256,256]{2,1,0:T(8,128)(2,1)S(1)}, u32[]{:S(2)}, u32[]{:S(2)}) collective-permute-start(bf16[4,256,256]{2,1,0:T(8,128)(2,1)} %pack.3.refs_0_), channel_id=1, source_target_pairs={{24,0}} | collective-permute-start | bytes 1572872 | tf_op jit(solution)/shard_map/ppermute | solution.py:523
  7.3 32.5 %collective-permute-start.4 = (bf16[4,256,256]{2,1,0:T(8,128)(2,1)}, bf16[4,256,256]{2,1,0:T(8,128)(2,1)S(1)}, u32[]{:S(2)}, u32[]{:S(2)}) collective-permute-start(bf16[4,256,256]{2,1,0:T(8,128)(2,1)} %pack.3.refs_0_), channel_id=1, source_target_pairs={{20,0}} | collective-permute-start | bytes 1572872 | tf_op jit(solution)/shard_map/ppermute | solution.py:523
  8.6 31.2 %collective-permute-start.3 = (bf16[4,256,256]{2,1,0:T(8,128)(2,1)}, bf16[4,256,256]{2,1,0:T(8,128)(2,1)S(1)}, u32[]{:S(2)}, u32[]{:S(2)}) collective-permute-start(bf16[4,256,256]{2,1,0:T(8,128)(2,1)} %pack.3.refs_0_), channel_id=1, source_target_pairs={{16,0}} | collective-permute-start | bytes 1572872 | tf_op jit(solution)/shard_map/ppermute | solution.py:523
  9.9 30.0 %collective-permute-start.2 = (bf16[4,256,256]{2,1,0:T(8,128)(2,1)}, bf16[4,256,256]{2,1,0:T(8,128)(2,1)S(1)}, u32[]{:S(2)}, u32[]{:S(2)}) collective-permute-start(bf16[4,256,256]{2,1,0:T(8,128)(2,1)} %pack.3.refs_0_), channel_id=1, source_target_pairs={{12,0}} | collective-permute-start | bytes 1572872 | tf_op jit(solution)/shard_map/ppermute | solution.py:523
  20.4 19.5 %collective-permute-start.1 = (bf16[4,256,256]{2,1,0:T(8,128)(2,1)}, bf16[4,256,256]{2,1,0:T(8,128)(2,1)S(1)}, u32[]{:S(2)}, u32[]{:S(2)}) collective-permute-start(bf16[4,256,256]{2,1,0:T(8,128)(2,1)} %pack.3.refs_0_), channel_id=1, source_target_pairs={{8,0}} | collective-permute-start | bytes 1572872 | tf_op jit(solution)/shard_map/ppermute | solution.py:523
  22.1 17.8 %collective-permute-start = (bf16[4,256,256]{2,1,0:T(8,128)(2,1)}, bf16[4,256,256]{2,1,0:T(8,128)(2,1)}, u32[]{:S(2)}, u32[]{:S(2)}) collective-permute-start(bf16[4,256,256]{2,1,0:T(8,128)(2,1)} %pack.3.refs_0_), channel_id=1, source_target_pairs={{4,0}} | collective-permute-start | bytes 1572872 | tf_op jit(solution)/shard_map/ppermute | solution.py:523
  24.1 9.3 %all-to-all-start = ((s32[8,4,1]{1,2,0:T(1,128)}), s32[8,4,1]{1,2,0:T(1,128)S(1)}, u32[]{:S(2)}, u32[]{:S(2)}) async-start(s32[8,4,1]{1,2,0:T(1,128)} %bitcast), calls=%async_computation | async-start | bytes 8192 | tf_op jit(solution)/shard_map/all_to_all | solution.py:507
  33.4 137.8 %all-to-all-start.1 = ((bf16[32,256,256]{2,1,0:T(8,128)(2,1)}), bf16[32,256,256]{2,1,0:T(8,128)(2,1)}, u32[]{:S(2)}, u32[]{:S(2)}) async-start(bf16[32,256,256]{2,1,0:T(8,128)(2,1)} %pack.2), calls=%async_computation.1 | async-start | bytes 8388608 | tf_op jit(solution)/shard_map/all_to_all | solution.py:525
  59.9 35.6 %collective-permute-start.7 = (f32[1024,256]{1,0:T(8,128)}, f32[1024,256]{1,0:T(8,128)S(1)}, u32[]{:S(2)}, u32[]{:S(2)}) collective-permute-start(f32[1024,256]{1,0:T(8,128)} %get-tuple-element.17.refs_0_), channel_id=1, source_target_pairs={{0,8}} | collective-permute-start | bytes 3145736 | tf_op jit(solution)/shard_map/ppermute | solution.py:540
  64.0 15.9 %copy-start.19 = (f32[1024,256]{1,0:T(8,128)S(1)}, f32[1024,256]{1,0:T(8,128)}, u32[]{:S(2)}) copy-start(f32[1024,256]{1,0:T(8,128)} %get-tuple-element.17.refs_0_) | copy-start | bytes 3145732
  77.7 38.7 %collective-permute-start.14 = (f32[768,256]{1,0:T(8,128)}, f32[768,256]{1,0:T(8,128)}, u32[]{:S(2)}, u32[]{:S(2)}) collective-permute-start(f32[768,256]{1,0:T(8,128)} %get-tuple-element.21.refs_0_), channel_id=1, source_target_pairs={{0,8}} | collective-permute-start | bytes 2359304 | tf_op jit(solution)/shard_map/ppermute | solution.py:540
  79.9 44.7 %collective-permute-start.8 = (f32[1024,256]{1,0:T(8,128)S(1)}, f32[1024,256]{1,0:T(8,128)S(1)}, u32[]{:S(2)}, u32[]{:S(2)}) collective-permute-start(f32[1024,256]{1,0:T(8,128)S(1)} %copy-done.19), channel_id=1, source_target_pairs={{0,16}} | collective-permute-start | bytes 3145736 | tf_op jit(solution)/shard_map/ppermute | solution.py:540
  95.5 30.6 %copy-start.20 = (f32[1024,256]{1,0:T(8,128)}, f32[1024,256]{1,0:T(8,128)S(1)}, u32[]{:S(2)}) copy-start(f32[1024,256]{1,0:T(8,128)S(1)} %collective-permute-done.7.refs_1_) | copy-start | bytes 3145732
  95.6 30.6 %collective-permute-start.9 = (f32[1024,256]{1,0:T(8,128)S(1)}, f32[1024,256]{1,0:T(8,128)}, u32[]{:S(2)}, u32[]{:S(2)}) collective-permute-start(f32[1024,256]{1,0:T(8,128)S(1)} %collective-permute-done.7.refs_1_), channel_id=1, source_target_pairs={{8,24}} | collective-permute-start | bytes 3145736 | tf_op jit(solution)/shard_map/ppermute | solution.py:540
  97.2 43.3 %collective-permute-start.15 = (f32[768,256]{1,0:T(8,128)}, f32[768,256]{1,0:T(8,128)}, u32[]{:S(2)}, u32[]{:S(2)}) collective-permute-start(f32[768,256]{1,0:T(8,128)} %get-tuple-element.21.refs_0_), channel_id=1, source_target_pairs={{0,16}} | collective-permute-start | bytes 2359304 | tf_op jit(solution)/shard_map/ppermute | solution.py:540
  111.3 11.3 %collective-permute-start.21 = (f32[512,256]{1,0:T(8,128)}, f32[512,256]{1,0:T(8,128)}, u32[]{:S(2)}, u32[]{:S(2)}) collective-permute-start(f32[512,256]{1,0:T(8,128)} %get-tuple-element.25.refs_0_), channel_id=1, source_target_pairs={{0,8}} | collective-permute-start | bytes 1572872 | tf_op jit(solution)/shard_map/ppermute | solution.py:540
  116.4 28.7 %collective-permute-start.16 = (f32[768,256]{1,0:T(8,128)}, f32[768,256]{1,0:T(8,128)}, u32[]{:S(2)}, u32[]{:S(2)}) collective-permute-start(f32[768,256]{1,0:T(8,128)} %collective-permute-done.14.refs_1_), channel_id=1, source_target_pairs={{8,24}} | collective-permute-start | bytes 2359304 | tf_op jit(solution)/shard_map/ppermute | solution.py:540
  122.6 28.0 %collective-permute-start.22 = (f32[512,256]{1,0:T(8,128)}, f32[512,256]{1,0:T(8,128)}, u32[]{:S(2)}, u32[]{:S(2)}) collective-permute-start(f32[512,256]{1,0:T(8,128)} %get-tuple-element.25.refs_0_), channel_id=1, source_target_pairs={{0,16}} | collective-permute-start | bytes 1572872 | tf_op jit(solution)/shard_map/ppermute | solution.py:540
  124.7 26.6 %collective-permute-start.23 = (f32[512,256]{1,0:T(8,128)}, f32[512,256]{1,0:T(8,128)}, u32[]{:S(2)}, u32[]{:S(2)}) collective-permute-start(f32[512,256]{1,0:T(8,128)} %collective-permute-done.21.refs_1_), channel_id=1, source_target_pairs={{8,24}} | collective-permute-start | bytes 1572872 | tf_op jit(solution)/shard_map/ppermute | solution.py:540
  128.2 40.0 %collective-permute-start.10 = (f32[1024,256]{1,0:T(8,128)}, f32[1024,256]{1,0:T(8,128)S(1)}, u32[]{:S(2)}, u32[]{:S(2)}) collective-permute-start(f32[1024,256]{1,0:T(8,128)} %pick.16.refs_0_), channel_id=1, source_target_pairs={{0,4},{8,12},{16,20},{24,28}} | collective-permute-start | bytes 3145736 | tf_op jit(solution)/shard_map/ppermute | solution.py:542
  140.6 8.7 %collective-permute-start.28 = (f32[256,256]{1,0:T(8,128)}, f32[256,256]{1,0:T(8,128)S(1)}, u32[]{:S(2)}, u32[]{:S(2)}) collective-permute-start(f32[256,256]{1,0:T(8,128)} %chol.7.refs_0_), channel_id=1, source_target_pairs={{0,8}} | collective-permute-start | bytes 786440 | tf_op jit(solution)/shard_map/ppermute | solution.py:540
  147.1 18.2 %collective-permute-start.17 = (f32[768,256]{1,0:T(8,128)}, f32[768,256]{1,0:T(8,128)S(1)}, u32[]{:S(2)}, u32[]{:S(2)}) collective-permute-start(f32[768,256]{1,0:T(8,128)} %pick.19.refs_0_), channel_id=1, source_target_pairs={{0,4},{8,12},{16,20},{24,28}} | collective-permute-start | bytes 2359304 | tf_op jit(solution)/shard_map/ppermute | solution.py:542
  149.3 5.2 collective-permute-start.29
  150.6 3.9 collective-permute-start.30
  153.1 9.6 %collective-permute-start.24 = (f32[512,256]{1,0:T(8,128)}, f32[512,256]{1,0:T(8,128)S(1)}, u32[]{:S(2)}, u32[]{:S(2)}) collective-permute-start(f32[512,256]{1,0:T(8,128)} %pick.22.refs_0_), channel_id=1, source_target_pairs={{0,4},{8,12},{16,20},{24,28}} | collective-permute-start | bytes 1572872 | tf_op jit(solution)/shard_map/ppermute | solution.py:542
  157.5 2.9 collective-permute-start.31
  185.4 39.4 %collective-permute-start.11 = (s16[8,272,256]{2,1,0:T(8,128)(2,1)}, s16[8,272,256]{2,1,0:T(8,128)(2,1)S(1)}, u32[]{:S(2)}, u32[]{:S(2)}) collective-permute-start(s16[8,272,256]{2,1,0:T(8,128)(2,1)} %get-tuple-element.18.refs_0_), channel_id=1, source_target_pairs={{0,1},{4,5},{8,9},{12,13},{16,17},{20,21},{24,25},{28,29}} | collective-permute-start | bytes 3342344 | tf_op jit(solution)/shard_map/ppermute | solution.py:548
  195.0 40.8 %collective-permute-start.18 = (s16[8,272,256]{2,1,0:T(8,128)(2,1)}, s16[8,272,256]{2,1,0:T(8,128)(2,1)S(1)}, u32[]{:S(2)}, u32[]{:S(2)}) collective-permute-start(s16[8,272,256]{2,1,0:T(8,128)(2,1)} %get-tuple-element.22.refs_0_), channel_id=1, source_target_pairs={{0,1},{4,5},{8,9},{12,13},{16,17},{20,21},{24,25},{28,29}} | collective-permute-start | bytes 3342344 | tf_op jit(solution)/shard_map/ppermute | solution.py:548
  208.4 15.0 %copy-start.4 = (s16[8,272,256]{2,1,0:T(8,128)(2,1)S(1)}, s16[8,272,256]{2,1,0:T(8,128)(2,1)}, u32[]{:S(2)}) copy-start(s16[8,272,256]{2,1,0:T(8,128)(2,1)} %get-tuple-element.26.refs_0_) | copy-start | bytes 3342340
  222.1 37.7 %collective-permute-start.32 = (s16[8,272,256]{2,1,0:T(8,128)(2,1)}, s16[8,272,256]{2,1,0:T(8,128)(2,1)S(1)}, u32[]{:S(2)}, u32[]{:S(2)}) collective-permute-start(s16[8,272,256]{2,1,0:T(8,128)(2,1)} %get-tuple-element.29.refs_0_), channel_id=1, source_target_pairs={{0,1},{4,5},{8,9},{12,13},{16,17},{20,21},{24,25},{28,29}} | collective-permute-start | bytes 3342344 | tf_op jit(solution)/shard_map/ppermute | solution.py:548
  223.4 59.6 %collective-permute-start.25 = (s16[8,272,256]{2,1,0:T(8,128)(2,1)S(1)}, s16[8,272,256]{2,1,0:T(8,128)(2,1)S(1)}, u32[]{:S(2)}, u32[]{:S(2)}) collective-permute-start(s16[8,272,256]{2,1,0:T(8,128)(2,1)S(1)} %copy-done.4), channel_id=1, source_target_pairs={{0,1},{4,5},{8,9},{12,13},{16,17},{20,21},{24,25},{28,29}} | collective-permute-start | bytes 3342344 | tf_op jit(solution)/shard_map/ppermute | solution.py:548
  224.8 65.8 %copy-start.7 = (s16[8,272,256]{2,1,0:T(8,128)(2,1)}, s16[8,272,256]{2,1,0:T(8,128)(2,1)S(1)}, u32[]{:S(2)}) copy-start(s16[8,272,256]{2,1,0:T(8,128)(2,1)S(1)} %collective-permute-done.11.refs_1_) | copy-start | bytes 3342340
  224.8 58.9 %collective-permute-start.12 = (s16[8,272,256]{2,1,0:T(8,128)(2,1)S(1)}, s16[8,272,256]{2,1,0:T(8,128)(2,1)S(1)}, u32[]{:S(2)}, u32[]{:S(2)}) collective-permute-start(s16[8,272,256]{2,1,0:T(8,128)(2,1)S(1)} %collective-permute-done.11.refs_1_), channel_id=1, source_target_pairs={{1,2},{5,6},{9,10},{13,14},{17,18},{21,22},{25,26},{29,30}} | collective-permute-start | bytes 3342344 | tf_op jit(solution)/shard_map/ppermute | solution.py:548
  235.9 56.8 %copy-start.5 = (s16[8,272,256]{2,1,0:T(8,128)(2,1)}, s16[8,272,256]{2,1,0:T(8,128)(2,1)S(1)}, u32[]{:S(2)}) copy-start(s16[8,272,256]{2,1,0:T(8,128)(2,1)S(1)} %collective-permute-done.18.refs_1_) | copy-start | bytes 3342340
  235.9 48.6 %collective-permute-start.19 = (s16[8,272,256]{2,1,0:T(8,128)(2,1)S(1)}, s16[8,272,256]{2,1,0:T(8,128)(2,1)S(1)}, u32[]{:S(2)}, u32[]{:S(2)}) collective-permute-start(s16[8,272,256]{2,1,0:T(8,128)(2,1)S(1)} %collective-permute-done.18.refs_1_), channel_id=1, source_target_pairs={{1,2},{5,6},{9,10},{13,14},{17,18},{21,22},{25,26},{29,30}} | collective-permute-start | bytes 3342344 | tf_op jit(solution)/shard_map/ppermute | solution.py:548
  259.7 39.4 %copy-start.8 = (s16[8,272,256]{2,1,0:T(8,128)(2,1)}, s16[8,272,256]{2,1,0:T(8,128)(2,1)S(1)}, u32[]{:S(2)}) copy-start(s16[8,272,256]{2,1,0:T(8,128)(2,1)S(1)} %collective-permute-done.32.refs_1_) | copy-start | bytes 3342340
  259.7 26.5 %collective-permute-start.33 = (s16[8,272,256]{2,1,0:T(8,128)(2,1)S(1)}, s16[8,272,256]{2,1,0:T(8,128)(2,1)}, u32[]{:S(2)}, u32[]{:S(2)}) collective-permute-start(s16[8,272,256]{2,1,0:T(8,128)(2,1)S(1)} %collective-permute-done.32.refs_1_), channel_id=1, source_target_pairs={{1,2},{5,6},{9,10},{13,14},{17,18},{21,22},{25,26},{29,30}} | collective-permute-start | bytes 3342344 | tf_op jit(solution)/shard_map/ppermute | solution.py:548
  283.0 4.9 collective-permute-start.26
  283.8 5.8 %collective-permute-start.13 = (s16[8,272,256]{2,1,0:T(8,128)(2,1)S(1)}, s16[8,272,256]{2,1,0:T(8,128)(2,1)S(1)}, u32[]{:S(2)}, u32[]{:S(2)}) collective-permute-start(s16[8,272,256]{2,1,0:T(8,128)(2,1)S(1)} %collective-permute-done.12.refs_2_), channel_id=1, source_target_pairs={{2,3},{6,7},{10,11},{14,15},{18,19},{22,23},{26,27},{30,31}} | collective-permute-start | bytes 3342344 | tf_op jit(solution)/shard_map/ppermute | solution.py:548
  284.5 12.5 %collective-permute-start.20 = (s16[8,272,256]{2,1,0:T(8,128)(2,1)S(1)}, s16[8,272,256]{2,1,0:T(8,128)(2,1)}, u32[]{:S(2)}, u32[]{:S(2)}) collective-permute-start(s16[8,272,256]{2,1,0:T(8,128)(2,1)S(1)} %collective-permute-done.19.refs_2_), channel_id=1, source_target_pairs={{2,3},{6,7},{10,11},{14,15},{18,19},{22,23},{26,27},{30,31}} | collective-permute-start | bytes 3342344 | tf_op jit(solution)/shard_map/ppermute | solution.py:548
  286.2 14.3 %collective-permute-start.34 = (s16[8,272,256]{2,1,0:T(8,128)(2,1)}, s16[8,272,256]{2,1,0:T(8,128)(2,1)}, u32[]{:S(2)}, u32[]{:S(2)}) collective-permute-start(s16[8,272,256]{2,1,0:T(8,128)(2,1)} %collective-permute-done.33.refs_2_), channel_id=1, source_target_pairs={{2,3},{6,7},{10,11},{14,15},{18,19},{22,23},{26,27},{30,31}} | collective-permute-start | bytes 3342344 | tf_op jit(solution)/shard_map/ppermute | solution.py:548
  287.9 16.1 %collective-permute-start.27 = (s16[8,272,256]{2,1,0:T(8,128)(2,1)S(1)}, s16[8,272,256]{2,1,0:T(8,128)(2,1)}, u32[]{:S(2)}, u32[]{:S(2)}) collective-permute-start(s16[8,272,256]{2,1,0:T(8,128)(2,1)S(1)} %collective-permute-done.26.refs_2_), channel_id=1, source_target_pairs={{2,3},{6,7},{10,11},{14,15},{18,19},{22,23},{26,27},{30,31}} | collective-permute-start | bytes 3342344 | tf_op jit(solution)/shard_map/ppermute | solution.py:548
  292.7 17.6 %collective-permute-start.35 = (s16[8,272,256]{2,1,0:T(8,128)(2,1)}, s16[8,272,256]{2,1,0:T(8,128)(2,1)S(1)}, u32[]{:S(2)}, u32[]{:S(2)}) collective-permute-start(s16[8,272,256]{2,1,0:T(8,128)(2,1)} %pick.18.refs_0_), channel_id=1, source_target_pairs={{0,8},{4,20},{9,25},{13,5},{18,2},{22,30},{27,19},{31,15}} | collective-permute-start | bytes 3342344 | tf_op jit(solution)/shard_map/ppermute | solution.py:552
  299.1 49.4 %collective-permute-start.38 = (s16[8,272,256]{2,1,0:T(8,128)(2,1)}, s16[8,272,256]{2,1,0:T(8,128)(2,1)S(1)}, u32[]{:S(2)}, u32[]{:S(2)}) collective-permute-start(s16[8,272,256]{2,1,0:T(8,128)(2,1)} %pick.21.refs_0_.refs_1_), channel_id=1, source_target_pairs={{0,8},{4,20},{9,25},{13,5},{18,2},{22,30},{27,19},{31,15}} | collective-permute-start | bytes 3342344 | tf_op jit(solution)/shard_map/ppermute | solution.py:552
  302.6 102.0 %copy-start.36 = (s32[4]{0:T(128)S(1)}, s32[4]{0:T(128)}, u32[]{:S(2)}) copy-start(s32[4]{0:T(128)} %constant.157.clone) | copy-start | bytes 52
  302.6 53.4 %collective-permute-start.44 = (s16[8,272,256]{2,1,0:T(8,128)(2,1)}, s16[8,272,256]{2,1,0:T(8,128)(2,1)S(1)}, u32[]{:S(2)}, u32[]{:S(2)}) collective-permute-start(s16[8,272,256]{2,1,0:T(8,128)(2,1)} %pick.27.refs_0_.refs_3_), channel_id=1, source_target_pairs={{0,8},{4,20},{9,25},{13,5},{18,2},{22,30},{27,19},{31,15}} | collective-permute-start | bytes 3342344 | tf_op jit(solution)/shard_map/ppermute | solution.py:552
  306.1 57.3 %collective-permute-start.41 = (s16[8,272,256]{2,1,0:T(8,128)(2,1)}, s16[8,272,256]{2,1,0:T(8,128)(2,1)S(1)}, u32[]{:S(2)}, u32[]{:S(2)}) collective-permute-start(s16[8,272,256]{2,1,0:T(8,128)(2,1)} %pick.24.refs_0_.refs_2_), channel_id=1, source_target_pairs={{0,8},{4,20},{9,25},{13,5},{18,2},{22,30},{27,19},{31,15}} | collective-permute-start | bytes 3342344 | tf_op jit(solution)/shard_map/ppermute | solution.py:552
  310.3 98.2 %copy-start = (s16[8,272,256]{2,1,0:T(8,128)(2,1)}, s16[8,272,256]{2,1,0:T(8,128)(2,1)S(1)}, u32[]{:S(2)}) copy-start(s16[8,272,256]{2,1,0:T(8,128)(2,1)S(1)} %collective-permute-done.35.refs_1_) | copy-start | bytes 3342340
  310.3 64.0 %collective-permute-start.36 = (s16[8,272,256]{2,1,0:T(8,128)(2,1)S(1)}, s16[8,272,256]{2,1,0:T(8,128)(2,1)}, u32[]{:S(2)}, u32[]{:S(2)}) collective-permute-start(s16[8,272,256]{2,1,0:T(8,128)(2,1)S(1)} %collective-permute-done.35.refs_1_), channel_id=1, source_target_pairs={{8,24},{20,28},{25,17},{5,21},{2,10},{30,14},{19,3},{15,7}} | collective-permute-start | bytes 3342344 | tf_op jit(solution)/shard_map/ppermute | solution.py:552
  348.6 61.9 %copy-start.1 = (s16[8,272,256]{2,1,0:T(8,128)(2,1)}, s16[8,272,256]{2,1,0:T(8,128)(2,1)S(1)}, u32[]{:S(2)}) copy-start(s16[8,272,256]{2,1,0:T(8,128)(2,1)S(1)} %collective-permute-done.38.refs_1_) | copy-start | bytes 3342340
  348.6 33.1 %collective-permute-start.39 = (s16[8,272,256]{2,1,0:T(8,128)(2,1)S(1)}, s16[8,272,256]{2,1,0:T(8,128)(2,1)}, u32[]{:S(2)}, u32[]{:S(2)}) collective-permute-start(s16[8,272,256]{2,1,0:T(8,128)(2,1)S(1)} %collective-permute-done.38.refs_1_), channel_id=1, source_target_pairs={{8,24},{20,28},{25,17},{5,21},{2,10},{30,14},{19,3},{15,7}} | collective-permute-start | bytes 3342344 | tf_op jit(solution)/shard_map/ppermute | solution.py:552
  355.9 54.5 %copy-start.2 = (s16[8,272,256]{2,1,0:T(8,128)(2,1)}, s16[8,272,256]{2,1,0:T(8,128)(2,1)S(1)}, u32[]{:S(2)}) copy-start(s16[8,272,256]{2,1,0:T(8,128)(2,1)S(1)} %collective-permute-done.44.refs_1_) | copy-start | bytes 3342340
  355.9 33.1 %collective-permute-start.45 = (s16[8,272,256]{2,1,0:T(8,128)(2,1)S(1)}, s16[8,272,256]{2,1,0:T(8,128)(2,1)}, u32[]{:S(2)}, u32[]{:S(2)}) collective-permute-start(s16[8,272,256]{2,1,0:T(8,128)(2,1)S(1)} %collective-permute-done.44.refs_1_), channel_id=1, source_target_pairs={{8,24},{20,28},{25,17},{5,21},{2,10},{30,14},{19,3},{15,7}} | collective-permute-start | bytes 3342344 | tf_op jit(solution)/shard_map/ppermute | solution.py:552
  363.3 25.7 %copy-start.3 = (s16[8,272,256]{2,1,0:T(8,128)(2,1)}, s16[8,272,256]{2,1,0:T(8,128)(2,1)S(1)}, u32[]{:S(2)}) copy-start(s16[8,272,256]{2,1,0:T(8,128)(2,1)S(1)} %collective-permute-done.41.refs_1_) | copy-start | bytes 3342340
  363.3 33.0 %collective-permute-start.42 = (s16[8,272,256]{2,1,0:T(8,128)(2,1)S(1)}, s16[8,272,256]{2,1,0:T(8,128)(2,1)}, u32[]{:S(2)}, u32[]{:S(2)}) collective-permute-start(s16[8,272,256]{2,1,0:T(8,128)(2,1)S(1)} %collective-permute-done.41.refs_1_), channel_id=1, source_target_pairs={{8,24},{20,28},{25,17},{5,21},{2,10},{30,14},{19,3},{15,7}} | collective-permute-start | bytes 3342344 | tf_op jit(solution)/shard_map/ppermute | solution.py:552
  374.3 34.2 %collective-permute-start.37 = (s16[8,272,256]{2,1,0:T(8,128)(2,1)}, s16[8,272,256]{2,1,0:T(8,128)(2,1)}, u32[]{:S(2)}, u32[]{:S(2)}) collective-permute-start(s16[8,272,256]{2,1,0:T(8,128)(2,1)} %collective-permute-done.36.refs_2_), channel_id=1, source_target_pairs={{24,16},{28,12},{17,1},{21,29},{10,26},{14,6},{3,11},{7,23}} | collective-permute-start | bytes 3342344 | tf_op jit(solution)/shard_map/ppermute | solution.py:552
  381.6 34.7 %collective-permute-start.40 = (s16[8,272,256]{2,1,0:T(8,128)(2,1)}, s16[8,272,256]{2,1,0:T(8,128)(2,1)}, u32[]{:S(2)}, u32[]{:S(2)}) collective-permute-start(s16[8,272,256]{2,1,0:T(8,128)(2,1)} %collective-permute-done.39.refs_2_), channel_id=1, source_target_pairs={{24,16},{28,12},{17,1},{21,29},{10,26},{14,6},{3,11},{7,23}} | collective-permute-start | bytes 3342344 | tf_op jit(solution)/shard_map/ppermute | solution.py:552
  389.0 35.2 %collective-permute-start.46 = (s16[8,272,256]{2,1,0:T(8,128)(2,1)}, s16[8,272,256]{2,1,0:T(8,128)(2,1)}, u32[]{:S(2)}, u32[]{:S(2)}) collective-permute-start(s16[8,272,256]{2,1,0:T(8,128)(2,1)} %collective-permute-done.45.refs_2_), channel_id=1, source_target_pairs={{24,16},{28,12},{17,1},{21,29},{10,26},{14,6},{3,11},{7,23}} | collective-permute-start | bytes 3342344 | tf_op jit(solution)/shard_map/ppermute | solution.py:552
  396.4 35.9 %collective-permute-start.43 = (s16[8,272,256]{2,1,0:T(8,128)(2,1)}, s16[8,272,256]{2,1,0:T(8,128)(2,1)}, u32[]{:S(2)}, u32[]{:S(2)}) collective-permute-start(s16[8,272,256]{2,1,0:T(8,128)(2,1)} %collective-permute-done.42.refs_2_), channel_id=1, source_target_pairs={{24,16},{28,12},{17,1},{21,29},{10,26},{14,6},{3,11},{7,23}} | collective-permute-start | bytes 3342344 | tf_op jit(solution)/shard_map/ppermute | solution.py:552
  410.5 31.1 %collective-permute-start.47 = (s16[8,272,256]{2,1,0:T(8,128)(2,1)}, s16[8,272,256]{2,1,0:T(8,128)(2,1)S(1)}, u32[]{:S(2)}, u32[]{:S(2)}) collective-permute-start(s16[8,272,256]{2,1,0:T(8,128)(2,1)} %pick.28.refs_4_), channel_id=1, source_target_pairs={{0,4},{1,5},{2,6},{3,7},{4,0},{5,1},{6,2},{7,3},{8,12},{9,13},{10,... | collective-permute-start | bytes 3342344 | tf_op jit(solution)/shard_map/ppermute | solution.py:554
  418.4 23.2 %collective-permute-start.48 = (s16[8,272,256]{2,1,0:T(8,128)(2,1)}, s16[8,272,256]{2,1,0:T(8,128)(2,1)S(1)}, u32[]{:S(2)}, u32[]{:S(2)}) collective-permute-start(s16[8,272,256]{2,1,0:T(8,128)(2,1)} %pick.29.refs_5_), channel_id=1, source_target_pairs={{0,4},{1,5},{2,6},{3,7},{4,0},{5,1},{6,2},{7,3},{8,12},{9,13},{10,... | collective-permute-start | bytes 3342344 | tf_op jit(solution)/shard_map/ppermute | solution.py:554
  426.2 15.4 %collective-permute-start.50 = (s16[8,272,256]{2,1,0:T(8,128)(2,1)}, s16[8,272,256]{2,1,0:T(8,128)(2,1)S(1)}, u32[]{:S(2)}, u32[]{:S(2)}) collective-permute-start(s16[8,272,256]{2,1,0:T(8,128)(2,1)} %pick.31.refs_7_), channel_id=1, source_target_pairs={{0,4},{1,5},{2,6},{3,7},{4,0},{5,1},{6,2},{7,3},{8,12},{9,13},{10,... | collective-permute-start | bytes 3342344 | tf_op jit(solution)/shard_map/ppermute | solution.py:554
  434.4 8.6 %collective-permute-start.49 = (s16[8,272,256]{2,1,0:T(8,128)(2,1)}, s16[8,272,256]{2,1,0:T(8,128)(2,1)S(1)}, u32[]{:S(2)}, u32[]{:S(2)}) collective-permute-start(s16[8,272,256]{2,1,0:T(8,128)(2,1)} %pick.30.refs_6_), channel_id=1, source_target_pairs={{0,4},{1,5},{2,6},{3,7},{4,0},{5,1},{6,2},{7,3},{8,12},{9,13},{10,... | collective-permute-start | bytes 3342344 | tf_op jit(solution)/shard_map/ppermute | solution.py:554
  (26 other events, 99.5 us)
where the time goes:
time: 529 us; the launch traced here: 520 us
  Pallas kernels  217 us (41%)
  starting transfers between devices  192 us (36%)
  waiting for transfers between devices  89.1 us (17%)
  local copies, waits for them, and re-layouts  9.83 us (2%)
  other arithmetic  7.26 us (1%)
    ppermute x12, starting transfers between devices, body(): lax.ppermute(steps[-1], both, ring_pairs(row_count, col_count, hop))  103 us
    pallas_call x1, Pallas kernels, schur(): pl.pallas_call(functools.partial(schur_kernel, count=count), out_shape=[j...  75.2 us
    ppermute x12, waiting for transfers between devices, body(): steps.append(lax.ppermute(steps[-1], 'col', [(hop, hop + 1)]))  55 us
    pallas_call x4, Pallas kernels, solve(): pl.pallas_call(functools.partial(solve_kernel, k=k), out_shape=[jax.Shape...  38.7 us
    pallas_call x3, Pallas kernels, chol_next(): pl.pallas_call(next_kernel, out_shape=shapes, grid=(1,), in_specs=[whole(...  36.4 us
    pallas_call x16, Pallas kernels, pick(): pl.pallas_call(pick_kernel, out_shape=jax.ShapeDtypeStruct(shape, dtype),...  31.2 us
    ppermute x12, starting transfers between devices, body(): held.append(lax.ppermute(held[parent], both, [pair]))  28.2 us
    ppermute x4, starting transfers between devices, body(): other.append(lax.ppermute(mine[-1], both, swap))  23.4 us
  transfers between devices with their start and end apart: 53, of which 11 were waited for; matrix products, arithmetic and copies ran while one was open for 1% of the time, Pallas kernels for 24%

commit v1 on v0

--- a/solution.py
+++ b/solution.py
@@ -226,21 +226,23 @@
     return unit * lax.rsqrt(diag)
 
 
-def first_kernel(rows_ref, cols_ref, front_ref, *refs, sources):
-    tiles, (l_ref, trail_ref, pivot, work) = refs[:sources], refs[sources:]
+def first_kernel(rows_ref, cols_ref, front_ref, tiles_ref, l_ref, trail_ref, pivot, work):
     pivot[...] = front_ref[...]
-    tile = tiles[0].shape[1]
+    slots, tile = tiles_ref.shape[:2]
     side = PW // tile
-    for r, tile_ref in enumerate(tiles):
-        for s in range(CAP):
-            row, col = rows_ref[r * CAP + s], cols_ref[r * CAP + s]
-
-            @pl.when((row >= 0) & (row < side) & (col < side))
-            def _(row=row, col=col, tile_ref=tile_ref, s=s):
-                at = pl.ds(pl.multiple_of(row * tile, tile), tile)
-                to = pl.ds(pl.multiple_of(col * tile, tile), tile)
-                pivot[at, to] += tile_ref[s].astype(F32)
-
+
+    def add(t, carry):
+        row, col = rows_ref[t], cols_ref[t]
+
+        @pl.when((row >= 0) & (row < side) & (col < side))
+        def _():
+            at = pl.ds(pl.multiple_of(row * tile, tile), tile)
+            to = pl.ds(pl.multiple_of(col * tile, tile), tile)
+            pivot[at, to] += tiles_ref[t].astype(F32)
+
+        return carry
+
+    lax.fori_loop(0, slots, add, 0)
     for i in range(PW // KP):
         for j in range(i + 1):
             si, sj = pl.ds(i * KP, KP), pl.ds(j * KP, KP)
@@ -296,21 +298,21 @@
     return pl.BlockSpec(shape, lambda i, *_: (0,) * len(shape))
 
 
-def chol_first(place_rows, place_cols, front, gathered):
+def chol_first(place_rows, place_cols, front, tiles):
     shapes = [jax.ShapeDtypeStruct((PW, KP), F32), jax.ShapeDtypeStruct((PW - KP, PW - KP), F32)]
     return pl.pallas_call(
-        functools.partial(first_kernel, sources=len(gathered)),
+        first_kernel,
         out_shape=shapes,
         grid_spec=pltpu.PrefetchScalarGridSpec(
             num_scalar_prefetch=2,
             grid=(1,),
-            in_specs=[whole((PW, PW))] + [whole(g.shape) for g in gathered],
+            in_specs=[whole((PW, PW)), whole(tiles.shape)],
             out_specs=[whole(s.shape) for s in shapes],
             scratch_shapes=[pltpu.VMEM((PW, PW), F32)] * 2,
         ),
         compiler_params=params(),
         name="chol",
-    )(place_rows, place_cols, front, *gathered)
+    )(place_rows, place_cols, front, tiles)
 
 
 def chol_next(a):
@@ -334,15 +336,37 @@
     return lax.broadcasted_iota(jnp.int32, (n, n), 0) == lax.broadcasted_iota(jnp.int32, (n, n), 1)
 
 
-def solve_kernel(p_ref, *refs, k):
-    factors, lowers = refs[:k], refs[k : 2 * k + 1]
-    f_ref, q_ref = refs[2 * k + 1 :]
+def halves(x):
+    high = x.astype(jnp.bfloat16)
+    return high, (x - high.astype(F32)).astype(jnp.bfloat16)
+
+
+def dot_halves(a, b):
+    return dot_t(a[0], b[0], None) + (dot_t(a[0], b[1], None) + dot_t(a[1], b[0], None))
+
+
+def solve_kernel(row_ref, p_ref, *refs, k, sources):
+    factors, lowers, held = refs[:k], refs[k : 2 * k], refs[2 * k : 2 * k + sources]
+    f_ref, q_ref, low_ref, sem = refs[2 * k + sources :]
+
+    @pl.when(pl.program_id(0) == 0)
+    def _():
+        for r, source in enumerate(held):
+
+            @pl.when(row_ref[0] == r)
+            def _(source=source):
+                copy = pltpu.make_async_copy(source, low_ref, sem)
+                copy.start()
+                copy.wait()
+
+    sides = [halves(lowers[j][(k - j) * KP : (k - j + 1) * KP, :]) for j in range(k)]
+    top = halves(low_ref[0:KP, :])
     for g in range(q_ref.shape[0]):
         at = slice(g * GRP, (g + 1) * GRP)
         acc = p_ref[at, :]
         for j in range(k):
-            acc = acc - dot_t(factors[j][at, :], lowers[j][(k - j) * KP : (k - j + 1) * KP, :])
-        f = dot_t(acc, lowers[k][0:KP, :])
+            acc = acc - dot_halves(halves(factors[j][at, :]), sides[j])
+        f = dot_halves(halves(acc), top)
         f_ref[at, :] = f
         peak = jnp.maximum(jnp.max(jnp.abs(f), axis=1, keepdims=True), 1e-30)
         code = jnp.ceil(jnp.log2(peak) * CODE)
@@ -353,25 +377,35 @@
         q_ref[g, GRP : GRP + EXT, :] = codes.astype(jnp.int32).astype(jnp.int16)
 
 
-def solve(panel_sum, factors, lowers):
+def solve(row, panel_sum, factors, lowers, held):
     k = len(factors)
     rows = panel_sum.shape[0]
     high = min(rows, 4 * GRP)
-    block = pl.BlockSpec((high, KP), lambda i: (i, 0))
-    return pl.pallas_call(
-        functools.partial(solve_kernel, k=k),
+    block = pl.BlockSpec((high, KP), lambda i, *_: (i, 0))
+    return pl.pallas_call(
+        functools.partial(solve_kernel, k=k, sources=len(held)),
         out_shape=[
             jax.ShapeDtypeStruct((rows, KP), F32),
             jax.ShapeDtypeStruct((rows // GRP, GRP + EXT, KP), jnp.int16),
+            jax.ShapeDtypeStruct(held[0].shape, F32),
         ],
-        grid=(rows // high,),
-        in_specs=[pl.BlockSpec((high, KP), lambda i: (i, k))]
-        + [block] * k
-        + [pl.BlockSpec(low.shape, lambda i: (0, 0)) for low in lowers],
-        out_specs=[block, pl.BlockSpec((high // GRP, GRP + EXT, KP), lambda i: (i, 0, 0))],
+        grid_spec=pltpu.PrefetchScalarGridSpec(
+            num_scalar_prefetch=1,
+            grid=(rows // high,),
+            in_specs=[pl.BlockSpec((high, KP), lambda i, *_: (i, k))]
+            + [block] * k
+            + [whole(low.shape) for low in lowers]
+            + [ANY] * len(held),
+            out_specs=[
+                block,
+                pl.BlockSpec((high // GRP, GRP + EXT, KP), lambda i, *_: (i, 0, 0)),
+                whole(held[0].shape),
+            ],
+            scratch_shapes=[pltpu.SemaphoreType.DMA],
+        ),
         compiler_params=params(),
         name="solve",
-    )(panel_sum, *factors, *lowers)
+    )(row, panel_sum, *factors, *lowers, *held)
 
 
 def decode(q_ref, g):
@@ -381,17 +415,94 @@
     return q_ref[g, 0:GRP, :].astype(jnp.int32).astype(F32) * scale
 
 
-def halves(x):
-    high = x.astype(jnp.bfloat16)
-    return high, (x - high.astype(F32)).astype(jnp.bfloat16)
-
-
-def schur_kernel(rows_ref, cols_ref, order_ref, starts_ref, member_ref, front_ref, tiles_ref, *refs, count):
+PIECES = 4
+
+
+def stash(f, k, at, high_ref, low_ref):
+    high, low = halves(f)
+    high_ref[at, k * KP : (k + 1) * KP] = high
+    low_ref[at, k * KP : (k + 1) * KP] = low
+
+
+def piece_kernel(
+    rows_ref, cols_ref, order_ref, starts_ref, member_ref, front_ref, tiles_ref, *refs, piece, count
+):
     own, mine, other = refs[:count], refs[count : 2 * count], refs[2 * count : 3 * count]
-    f_ref, out_ref, fh_ref, fl_ref, sh_ref, sl_ref = refs[3 * count :]
+    sh_ref, sl_ref = refs[-2:]
+    outs = refs[3 * count + (piece > 0) : -2]
+    out_ref = outs[0]
+    i = pl.program_id(0)
+    groups = mine[0].shape[0]
+    tile = tiles_ref.shape[1]
+
+    @pl.when(i == 0)
+    def _():
+        for e, strip in enumerate((mine, other)):
+
+            @pl.when(member_ref[0] == (e + (2 * piece) // PIECES) % 2)
+            def _(strip=strip):
+                def step(g, carry):
+                    at = pl.ds(pl.multiple_of(g * GRP, GRP), GRP)
+                    for k in range(count):
+                        stash(decode(strip[k], g), k, at, sh_ref, sl_ref)
+                    return carry
+
+                lax.fori_loop(0, groups, step, 0)
+
+    high, wide = out_ref.shape
+    for g in range(high // GRP):
+        at = slice(g * GRP, (g + 1) * GRP)
+        f = jnp.concatenate([decode(own[k], g) for k in range(count)], axis=1)
+        if piece == 0:
+            outs[1][at, :] = f
+        prod = dot_halves(halves(f), (sh_ref[...], sl_ref[...]))
+        out_ref[at, :] = front_ref[at, :] - prod
+    scalars = (rows_ref, cols_ref, order_ref, starts_ref)
+    block = i * PIECES + piece
+    add_tiles(scalars, tiles_ref, out_ref, block, i * (high // tile), piece * (wide // tile))
+
+
+def schur_piece(piece, scalars, member, front, tiles, own, mine, other, previous):
+    rows, cols = front.shape
+    count = len(own)
+    high, wide = min(rows, 512), cols // PIECES
+    depth = count * KP
+    block = pl.BlockSpec((high, wide), lambda i, *_: (i, piece))
+    coded = pl.BlockSpec((high // GRP, GRP + EXT, KP), lambda i, *_: (i, 0, 0))
+    strip = pl.BlockSpec(
+        (wide // GRP, GRP + EXT, KP), lambda i, *_: (piece % (PIECES // 2), 0, 0), pipeline_mode=pl.Buffered(1)
+    )
+    shapes, specs = [jax.ShapeDtypeStruct((rows, cols), F32)], [block]
+    if piece == 0:
+        shapes.append(jax.ShapeDtypeStruct((rows, PW), F32))
+        specs.append(pl.BlockSpec((high, depth), lambda i, *_: (i, 0)))
+    return pl.pallas_call(
+        functools.partial(piece_kernel, piece=piece, count=count),
+        out_shape=shapes,
+        grid_spec=pltpu.PrefetchScalarGridSpec(
+            num_scalar_prefetch=5,
+            grid=(rows // high,),
+            in_specs=[
+                block,
+                pl.BlockSpec(tiles.shape, lambda i, *_: (0, 0, 0), pipeline_mode=pl.Buffered(1)),
+            ]
+            + [coded] * count
+            + [strip] * (2 * count)
+            + [ANY] * len(previous),
+            out_specs=specs,
+            scratch_shapes=[pltpu.VMEM((wide, depth), jnp.bfloat16)] * 2,
+        ),
+        input_output_aliases={7 + 3 * count: 0} if previous else {},
+        compiler_params=params(),
+        name="piece",
+    )(*scalars, member, front, tiles, *own, *mine, *other, *previous)
+
+
+def schur_kernel(member_ref, front_ref, *refs, count):
+    own, mine, other = refs[:count], refs[count : 2 * count], refs[2 * count : 3 * count]
+    out_ref, f_ref, fh_ref, fl_ref, sh_ref, sl_ref = refs[3 * count + 1 :]
     i, j = pl.program_id(0), pl.program_id(1)
     groups = mine[0].shape[0]
-    tile = tiles_ref.shape[1]
 
     @pl.when((i == 0) & (j == 0))
     def _():
@@ -400,9 +511,7 @@
                 member = member_ref[0] if e == 0 else 1 - member_ref[0]
                 at = pl.ds(pl.multiple_of((member * groups + g) * GRP, GRP), GRP)
                 for k in range(count):
-                    high, low = halves(decode(strip[k], g))
-                    sh_ref[at, k * KP : (k + 1) * KP] = high
-                    sl_ref[at, k * KP : (k + 1) * KP] = low
+                    stash(decode(strip[k], g), k, at, sh_ref, sl_ref)
             return carry
 
         lax.fori_loop(0, groups, step, 0)
@@ -414,49 +523,40 @@
             for k in range(count):
                 f = decode(own[k], g)
                 f_ref[at, k * KP : (k + 1) * KP] = f
-                high, low = halves(f)
-                fh_ref[at, k * KP : (k + 1) * KP] = high
-                fl_ref[at, k * KP : (k + 1) * KP] = low
+                stash(f, k, at, fh_ref, fl_ref)
             return carry
 
         lax.fori_loop(0, own[0].shape[0], step, 0)
 
-    high, wide = out_ref.shape
+    wide = out_ref.shape[1]
     at = pl.ds(pl.multiple_of(j * wide, wide), wide)
-    fh, fl, sh, sl = fh_ref[...], fl_ref[...], sh_ref[at, :], sl_ref[at, :]
-    out_ref[...] = front_ref[...] - (dot_t(fh, sh, None) + (dot_t(fh, sl, None) + dot_t(fl, sh, None)))
-    block = i * pl.num_programs(1) + j
-    scalars = (rows_ref, cols_ref, order_ref, starts_ref)
-    add_tiles(scalars, tiles_ref, out_ref, block, i * (high // tile), j * (wide // tile))
-
-
-def schur(place_rows, place_cols, member, front, tiles, own, mine, other):
+    prod = dot_halves((fh_ref[...], fl_ref[...]), (sh_ref[at, :], sl_ref[at, :]))
+    out_ref[...] = front_ref[...] - prod
+
+
+def schur_rest(member, front, factor, own, mine, other):
     rows, cols = front.shape
     count = len(own)
-    once = pl.Buffered(1)
-    high, wide = min(rows, 1024), min(cols, 512)
+    high, wide = min(rows, 1024), min(cols, 1024)
     depth = count * KP
-    tile = tiles.shape[1]
-    order, starts = bucket(place_rows, place_cols, high // tile, wide // tile, rows // high, cols // wide)
     block = pl.BlockSpec((high, wide), lambda i, j, *_: (i, j))
     coded = pl.BlockSpec((high // GRP, GRP + EXT, KP), lambda i, j, *_: (i, 0, 0))
-    strip = pl.BlockSpec(mine[0].shape, lambda i, j, *_: (0, 0, 0), pipeline_mode=once)
+    strip = pl.BlockSpec(mine[0].shape, lambda i, j, *_: (0, 0, 0), pipeline_mode=pl.Buffered(1))
     return pl.pallas_call(
         functools.partial(schur_kernel, count=count),
-        out_shape=[jax.ShapeDtypeStruct((rows, PW), F32), jax.ShapeDtypeStruct((rows, cols), F32)],
+        out_shape=[jax.ShapeDtypeStruct((rows, cols), F32), jax.ShapeDtypeStruct((rows, PW), F32)],
         grid_spec=pltpu.PrefetchScalarGridSpec(
-            num_scalar_prefetch=5,
+            num_scalar_prefetch=1,
             grid=(rows // high, cols // wide),
-            in_specs=[block, pl.BlockSpec(tiles.shape, lambda i, j, *_: (0, 0, 0), pipeline_mode=once)]
-            + [coded] * count
-            + [strip] * (2 * count),
-            out_specs=[pl.BlockSpec((high, depth), lambda i, j, *_: (i, 0)), block],
+            in_specs=[block] + [coded] * count + [strip] * (2 * count) + [ANY],
+            out_specs=[block, pl.BlockSpec((high, depth), lambda i, j, *_: (i, PW // depth - 1))],
             scratch_shapes=[pltpu.VMEM((high, depth), jnp.bfloat16)] * 2
             + [pltpu.VMEM((cols, depth), jnp.bfloat16)] * 2,
         ),
+        input_output_aliases={1: 0, 2 + 3 * count: 1},
         compiler_params=params(),
         name="schur",
-    )(place_rows, place_cols, order, starts, member, front, tiles, *own, *mine, *other)
+    )(member, front, *own, *mine, *other, factor)
 
 
 def gray(n):
@@ -517,32 +617,29 @@
     distance = jnp.where(member == 0, here - there, there - here) % chips
     swap = [(r * col_count + c, (r ^ 1) * col_count + c) for r in range(row_count) for c in range(col_count)]
 
-    first = pack(index[:CAP], child_tiles)
-    gathered = [first]
-    for r in range(1, row_count):
-        gathered.append(lax.ppermute(first, both, [(r * col_count, 0)]))
     outgoing = pack(index, child_tiles)
     arrived = lax.all_to_all(outgoing, "row", split_axis=0, concat_axis=0, tiled=True)
+
+    count = PW // KP
+    row = row_index.reshape(1).astype(jnp.int32)
+    own, mine, other, factors, lowers = [], [], [], [], []
+    result = chol_first(place_rows, place_cols, front_init, arrived)
     panel_sum = panel(place_rows, place_cols, front_init, arrived)
-
-    own, mine, other, factors, lowers = [], [], [], [], []
-    pivot = None
-    for k in range(PW // KP):
-        if k == 0:
-            result = chol_first(place_rows, place_cols, front_init, gathered)
-        else:
-            result = chol_next(pivot)
-        pivot = result[-1]
-        held = [result[0]]
+    for k in range(count):
+        if k > 0:
+            result = chol_next(result[-1])
+        even = [result[0]]
         for chip in range(1, chips):
             parent = above(chip)
             pair = (2 * parent * col_count, 2 * chip * col_count)
-            held.append(lax.ppermute(held[parent], both, [pair]))
-        even = pick(row_index // 2, held)
-        odd = lax.ppermute(even, both, [(2 * c * col_count, (2 * c + 1) * col_count) for c in range(chips)])
-        lowers.append(pick(member, [even, odd]))
-        factor, coded = solve(panel_sum, factors, lowers)
+            even.append(lax.ppermute(even[parent], both, [pair]))
+        held = []
+        for chip in range(chips):
+            pair = (2 * chip * col_count, (2 * chip + 1) * col_count)
+            held += [even[chip], lax.ppermute(even[chip], both, [pair])]
+        factor, coded, lower = solve(row, panel_sum, factors, lowers, held)
         factors.append(factor)
+        lowers.append(lower)
         steps = [coded]
         for hop in range(col_count - 1):
             steps.append(lax.ppermute(steps[-1], "col", [(hop, hop + 1)]))
@@ -553,8 +650,35 @@
         mine.append(pick(distance, steps))
         other.append(lax.ppermute(mine[-1], both, swap))
 
-    panel_factor, schur_update = schur(
-        place_rows, place_cols, member.reshape(1).astype(jnp.int32), front_init, arrived, own, mine, other
+    member = member.reshape(1).astype(jnp.int32)
+    part = count // 2
+    high = min(row_extent, 512)
+    scalars = (place_rows, place_cols) + bucket(
+        place_rows,
+        place_cols,
+        high // tile_width,
+        col_tiles // PIECES,
+        row_extent // high,
+        PIECES,
+    )
+    previous, factor = [], None
+    for piece in range(PIECES):
+        result = schur_piece(
+            piece,
+            scalars,
+            member,
+            front_init,
+            arrived,
+            own[:part],
+            mine[:part],
+            other[:part],
+            previous,
+        )
+        previous = [result[0]]
+        if piece == 0:
+            factor = result[1]
+    schur_update, panel_factor = schur_rest(
+        member, previous[0], factor, own[part:], mine[part:], other[part:]
     )
     return (panel_factor, schur_update)
 

time: 529 us -> 571 us (1.079)
  waiting for transfers between devices: 89.1 us -> 146 us
  starting transfers between devices: 192 us -> 174 us
    all_to_all x1, waiting for transfers between devices: 0.01 us -> 47.3 us  [body(): lax.all_to_all(outgoing, 'row', split_axis=0, concat_axis=0, tiled=True)]
    pallas_call x6 -> x10, Pallas kernels: 133 us -> 153 us  [the longest x4 60.6 us: schur_piece(): pl.pallas_call(functools.partial(piece_kernel, piece=piece, count=count),...]
    ppermute x12, waiting for transfers between devices: 2.89 us -> 22.4 us  [body(): lax.ppermute(steps[-1], both, ring_pairs(row_count, col_count, hop))]
    pallas_call x16 -> x8, Pallas kernels: 31.2 us -> 16.5 us  [pick(): pl.pallas_call(pick_kernel, out_shape=jax.ShapeDtypeStruct(shape, dtype),...]
    ppermute x12, starting transfers between devices: 103 us -> 88.1 us  [body(): lax.ppermute(steps[-1], both, ring_pairs(row_count, col_count, hop))]
    ppermute x23 -> x28, waiting for transfers between devices: 29.4 us -> 19.6 us  [the longest x12 19.6 us: body(): even.append(lax.ppermute(even[parent], both, [pair]))]
    ppermute x23 -> x28, starting transfers between devices: 42.7 us -> 37.9 us  [the longest x12 19.6 us: body(): even.append(lax.ppermute(even[parent], both, [pair]))]
  transfers between devices with their start and end apart: 53 -> 58, of which waited for: 11 -> 11; matrix products, arithmetic and copies ran while one was open for 1% -> 1% of each run, Pallas kernels for 24% -> 24%
where the time goes in v1:
time: 571 us; the launch traced here: 560 us
  Pallas kernels  220 us (39%)
  starting transfers between devices  174 us (30%)
  waiting for transfers between devices  146 us (26%)
  local copies, waits for them, and re-layouts  8.08 us (1%)
  other arithmetic  7.13 us (1%)
    ppermute x12, starting transfers between devices, body(): lax.ppermute(steps[-1], both, ring_pairs(row_count, col_count, hop))  88.1 us
    pallas_call x4, Pallas kernels, schur_piece(): pl.pallas_call(functools.partial(piece_kernel, piece=piece, count=count),...  60.6 us
    ppermute x12, waiting for transfers between devices, body(): steps.append(lax.ppermute(steps[-1], 'col', [(hop, hop + 1)]))  56.8 us
    all_to_all x1, waiting for transfers between devices, body(): lax.all_to_all(outgoing, 'row', split_axis=0, concat_axis=0, tiled=True)  47.3 us
    pallas_call x1, Pallas kernels, schur_rest(): pl.pallas_call(functools.partial(schur_kernel, count=count), out_shape=[j...  40.2 us
    pallas_call x3, Pallas kernels, chol_next(): pl.pallas_call(next_kernel, out_shape=shapes, grid=(1,), in_specs=[whole(...  36.8 us
    pallas_call x4, Pallas kernels, solve(): pl.pallas_call(functools.partial(solve_kernel, k=k, sources=len(held)), o...  32.8 us
    ppermute x4, starting transfers between devices, body(): other.append(lax.ppermute(mine[-1], both, swap))  23.3 us
  transfers between devices with their start and end apart: 58, of which 11 were waited for; matrix products, arithmetic and copies ran while one was open for 1% of the time, Pallas kernels for 24%

profile of v1, /device:TPU:0, one launch (start us, length us, event | category | flops | bytes accessed | tf_op | source)
XLA Modules:
  0.0 560.1 jit_solution(9807647176030041313)
XLA Ops:
  2.9 5.2 all-to-all-start
  8.1 5.2 pack.1
  13.3 4.6 all-to-all-start.1
  19.7 47.3 %all-to-all-done.1.tiles_ref = bf16[32,256,256]{2,1,0:T(8,128)(2,1)} async-done(((bf16[32,256,256]{2,1,0:T(8,128)(2,1)}), bf16[32,256,256]{2,1,0:T(8,128)(2,1)}, u32[]{:S(2)}, u32[]{:S(2)}) %all-to-all-start.1) | async-done | bytes 4194336 | tf_op jit(solution)/shard_map/all_to_all | solution.py:621
  67.0 19.0 %chol.4 = (f32[1024,256]{1,0:T(8,128)}, f32[768,768]{1,0:T(8,128)}) custom-call(s32[32]{0:T(128)} %get-tuple-element.52.rows_ref, s32[32]{0:T(128)} %get-tuple-element.51.cols_ref, f32[2048,4096]{1,0:T(8,128)} %front_ref.11, bf16[32,256,256]{2,1,0:T(8,128)(2,1)} %all-to-all-done.1.tiles_ref), custom_call_target="tpu_custom_call" | custom-call | tf_op jit(solution)/shard_map/chol/pallas_call | solution.py:303
  86.0 14.0 %chol.5 = (f32[768,256]{1,0:T(8,128)}, f32[512,512]{1,0:T(8,128)}) custom-call(f32[768,768]{1,0:T(8,128)} %get-tuple-element.28.a_ref), custom_call_target="tpu_custom_call" | custom-call | tf_op jit(solution)/shard_map/chol/pallas_call | solution.py:323
  100.0 12.0 %chol.6 = (f32[512,256]{1,0:T(8,128)}, f32[256,256]{1,0:T(8,128)}) custom-call(f32[512,512]{1,0:T(8,128)} %get-tuple-element.36.a_ref), custom_call_target="tpu_custom_call" | custom-call | tf_op jit(solution)/shard_map/chol/pallas_call | solution.py:323
  112.0 2.5 collective-permute-start.31
  117.2 10.8 %chol.7.refs_6_ = f32[256,256]{1,0:T(8,128)} custom-call(f32[256,256]{1,0:T(8,128)} %get-tuple-element.41.a_ref), custom_call_target="tpu_custom_call" | custom-call | tf_op jit(solution)/shard_map/chol/pallas_call | solution.py:323
  130.7 2.9 collective-permute-done.41.refs_10_
  134.9 3.7 collective-permute-start.13
  140.0 2.2 collective-permute-start.10
  143.6 4.8 collective-permute-done.13.refs_6_
  148.4 1.5 collective-permute-start.33
  149.8 5.8 %collective-permute-done.11.refs_4_ = f32[768,256]{1,0:T(8,128)S(1)} collective-permute-done((f32[768,256]{1,0:T(8,128)}, f32[768,256]{1,0:T(8,128)S(1)}, u32[]{:S(2)}, u32[]{:S(2)}) %collective-permute-start.11) | collective-permute-done | bytes 786464 | tf_op jit(solution)/shard_map/ppermute | solution.py:635
  159.1 1.7 collective-permute-start.5
  161.5 1.6 collective-permute-start.15
  163.1 6.1 %collective-permute-done.3.refs_4_ = f32[1024,256]{1,0:T(8,128)S(1)} collective-permute-done((f32[1024,256]{1,0:T(8,128)S(1)}, f32[1024,256]{1,0:T(8,128)S(1)}, u32[]{:S(2)}, u32[]{:S(2)}) %collective-permute-start.3) | collective-permute-done | bytes 1048608 | tf_op jit(solution)/shard_map/ppermute | solution.py:635
  169.2 1.6 collective-permute-start.4
  171.9 1.7 collective-permute-start.6
  174.3 1.6 collective-permute-start.16
  176.8 1.5 collective-permute-start.34
  183.3 9.2 %panel.1.p_ref = f32[2048,1024]{1,0:T(8,128)} custom-call(s32[32]{0:T(128)} %get-tuple-element.52.rows_ref, s32[32]{0:T(128)} %get-tuple-element.51.cols_ref, s32[32]{0:T(128)} %select_reduce_fusion.order_ref, s32[5]{0:T(128)} %convert_reduce_fusion.4.starts_ref, f32[2048,4096]{1,0:T(8,128)} %front_ref.11, bf16[32,256,256]{2,1,0:T(8,128)(2,1)} %all-to-all-done.1.tiles_ref), custom_call_target="tpu_custom_call" | custom-call | tf_op jit(solution)/shard_map/panel/pallas_call | solution.py:161
  192.5 5.3 solve.4
  197.8 7.4 %solve.5 = (f32[2048,256]{1,0:T(8,128)}, s16[8,272,256]{2,1,0:T(8,128)(2,1)}, f32[768,256]{1,0:T(8,128)}) custom-call(s32[1]{0:T(128)} %bitcast.3.row_ref, f32[2048,1024]{1,0:T(8,128)} %panel.1.p_ref, f32[2048,256]{1,0:T(8,128)} %get-tuple-element.26.refs_0_, f32[1024,256]{1,0:T(8,128)} %get-tuple-element.27.refs_1_.refs_2_.refs_3_, ...), custom_call_target="tpu_custom_call" | custom-call | tf_op jit(solution)/shard_map/solve/pallas_call | solution.py:385
  206.6 9.7 %solve.6 = (f32[2048,256]{1,0:T(8,128)}, s16[8,272,256]{2,1,0:T(8,128)(2,1)}, f32[512,256]{1,0:T(8,128)}) custom-call(s32[1]{0:T(128)} %bitcast.3.row_ref, f32[2048,1024]{1,0:T(8,128)} %panel.1.p_ref, f32[2048,256]{1,0:T(8,128)} %get-tuple-element.26.refs_0_, f32[2048,256]{1,0:T(8,128)} %get-tuple-element.34.refs_1_, ...), custom_call_target="tpu_custom_call" | custom-call | tf_op jit(solution)/shard_map/solve/pallas_call | solution.py:385
  216.3 1.4 collective-permute-start.7
  218.6 10.4 %solve.7 = (f32[2048,256]{1,0:T(8,128)}, s16[8,272,256]{2,1,0:T(8,128)(2,1)}, f32[256,256]{1,0:T(8,128)}) custom-call(s32[1]{0:T(128)} %bitcast.3.row_ref, f32[2048,1024]{1,0:T(8,128)} %panel.1.p_ref, f32[2048,256]{1,0:T(8,128)} %get-tuple-element.26.refs_0_, f32[2048,256]{1,0:T(8,128)} %get-tuple-element.34.refs_1_, f32[2048,256]{1,0:T(8,128)} %get-tuple-element.39.refs_2_, ...), custom_call_target="tpu_custom_call" | custom-call | tf_op jit(solution)/shard_map/solve/pallas_call | solution.py:385
  232.6 23.0 %collective-permute-done.7.refs_1_ = s16[8,272,256]{2,1,0:T(8,128)(2,1)S(1)} collective-permute-done((s16[8,272,256]{2,1,0:T(8,128)(2,1)S(1)}, s16[8,272,256]{2,1,0:T(8,128)(2,1)S(1)}, u32[]{:S(2)}, u32[]{:S(2)}) %collective-permute-start.7) | collective-permute-done | bytes 1114144 | tf_op jit(solution)/shard_map/ppermute | solution.py:645
  255.6 1.7 collective-permute-start.8
  257.2 22.3 %collective-permute-done.45.refs_1_ = s16[8,272,256]{2,1,0:T(8,128)(2,1)S(1)} collective-permute-done((s16[8,272,256]{2,1,0:T(8,128)(2,1)}, s16[8,272,256]{2,1,0:T(8,128)(2,1)S(1)}, u32[]{:S(2)}, u32[]{:S(2)}) %collective-permute-start.45) | collective-permute-done | bytes 1114144 | tf_op jit(solution)/shard_map/ppermute | solution.py:645
  279.5 1.7 collective-permute-start.46
  281.2 11.5 %collective-permute-done.35.refs_1_ = s16[8,272,256]{2,1,0:T(8,128)(2,1)S(1)} collective-permute-done((s16[8,272,256]{2,1,0:T(8,128)(2,1)S(1)}, s16[8,272,256]{2,1,0:T(8,128)(2,1)S(1)}, u32[]{:S(2)}, u32[]{:S(2)}) %collective-permute-start.35) | collective-permute-done | bytes 1114144 | tf_op jit(solution)/shard_map/ppermute | solution.py:645
  294.2 1.7 collective-permute-start.9
  295.9 1.6 collective-permute-start.47
  299.3 2.0 pick.9.refs_0_.refs_1_
  301.4 15.8 %collective-permute-start.23 = (s16[8,272,256]{2,1,0:T(8,128)(2,1)}, s16[8,272,256]{2,1,0:T(8,128)(2,1)S(1)}, u32[]{:S(2)}, u32[]{:S(2)}) collective-permute-start(s16[8,272,256]{2,1,0:T(8,128)(2,1)} %pick.9.refs_0_.refs_1_), channel_id=1, source_target_pairs={{0,8},{4,20},{9,25},{13,5},{18,2},{22,30},{27,19},{31,15}} | collective-permute-start | bytes 3342344 | tf_op jit(solution)/shard_map/ppermute | solution.py:649
  317.2 2.1 pick.8.refs_0_
  320.7 2.1 pick.13.refs_0_.refs_1_
  325.1 2.1 pick.12.refs_0_
  328.6 1.8 collective-permute-done.23.refs_1_
  330.4 1.7 collective-permute-start.24
  332.1 10.2 %collective-permute-done.20.refs_1_ = s16[8,272,256]{2,1,0:T(8,128)(2,1)S(1)} collective-permute-done((s16[8,272,256]{2,1,0:T(8,128)(2,1)}, s16[8,272,256]{2,1,0:T(8,128)(2,1)S(1)}, u32[]{:S(2)}, u32[]{:S(2)}) %collective-permute-start.20) | collective-permute-done | bytes 1114144 | tf_op jit(solution)/shard_map/ppermute | solution.py:649
  342.3 1.7 collective-permute-start.21
  344.0 10.2 %collective-permute-done.51.refs_1_ = s16[8,272,256]{2,1,0:T(8,128)(2,1)S(1)} collective-permute-done((s16[8,272,256]{2,1,0:T(8,128)(2,1)}, s16[8,272,256]{2,1,0:T(8,128)(2,1)S(1)}, u32[]{:S(2)}, u32[]{:S(2)}) %collective-permute-start.51) | collective-permute-done | bytes 1114144 | tf_op jit(solution)/shard_map/ppermute | solution.py:649
  354.3 28.6 %collective-permute-start.52 = (s16[8,272,256]{2,1,0:T(8,128)(2,1)S(1)}, s16[8,272,256]{2,1,0:T(8,128)(2,1)}, u32[]{:S(2)}, u32[]{:S(2)}) collective-permute-start(s16[8,272,256]{2,1,0:T(8,128)(2,1)S(1)} %collective-permute-done.51.refs_1_), channel_id=1, source_target_pairs={{8,24},{20,28},{25,17},{5,21},{2,10},{30,14},{19,3},{15,7}} | collective-permute-start | bytes 3342344 | tf_op jit(solution)/shard_map/ppermute | solution.py:649
  382.9 1.7 collective-permute-start.49
  384.6 12.6 %collective-permute-start.25 = (s16[8,272,256]{2,1,0:T(8,128)(2,1)}, s16[8,272,256]{2,1,0:T(8,128)(2,1)}, u32[]{:S(2)}, u32[]{:S(2)}) collective-permute-start(s16[8,272,256]{2,1,0:T(8,128)(2,1)} %collective-permute-done.24.refs_2_), channel_id=1, source_target_pairs={{24,16},{28,12},{17,1},{21,29},{10,26},{14,6},{3,11},{7,23}} | collective-permute-start | bytes 3342344 | tf_op jit(solution)/shard_map/ppermute | solution.py:649
  397.1 7.3 %collective-permute-start.22 = (s16[8,272,256]{2,1,0:T(8,128)(2,1)}, s16[8,272,256]{2,1,0:T(8,128)(2,1)}, u32[]{:S(2)}, u32[]{:S(2)}) collective-permute-start(s16[8,272,256]{2,1,0:T(8,128)(2,1)} %collective-permute-done.21.refs_2_), channel_id=1, source_target_pairs={{24,16},{28,12},{17,1},{21,29},{10,26},{14,6},{3,11},{7,23}} | collective-permute-start | bytes 3342344 | tf_op jit(solution)/shard_map/ppermute | solution.py:649
  404.5 7.4 %collective-permute-start.53 = (s16[8,272,256]{2,1,0:T(8,128)(2,1)}, s16[8,272,256]{2,1,0:T(8,128)(2,1)}, u32[]{:S(2)}, u32[]{:S(2)}) collective-permute-start(s16[8,272,256]{2,1,0:T(8,128)(2,1)} %collective-permute-done.52.refs_2_), channel_id=1, source_target_pairs={{24,16},{28,12},{17,1},{21,29},{10,26},{14,6},{3,11},{7,23}} | collective-permute-start | bytes 3342344 | tf_op jit(solution)/shard_map/ppermute | solution.py:649
  411.9 7.4 %collective-permute-start.50 = (s16[8,272,256]{2,1,0:T(8,128)(2,1)}, s16[8,272,256]{2,1,0:T(8,128)(2,1)}, u32[]{:S(2)}, u32[]{:S(2)}) collective-permute-start(s16[8,272,256]{2,1,0:T(8,128)(2,1)} %collective-permute-done.49.refs_2_), channel_id=1, source_target_pairs={{24,16},{28,12},{17,1},{21,29},{10,26},{14,6},{3,11},{7,23}} | collective-permute-start | bytes 3342344 | tf_op jit(solution)/shard_map/ppermute | solution.py:649
  423.2 2.0 pick.11.refs_3_
  425.2 5.8 %collective-permute-start.27 = (s16[8,272,256]{2,1,0:T(8,128)(2,1)}, s16[8,272,256]{2,1,0:T(8,128)(2,1)S(1)}, u32[]{:S(2)}, u32[]{:S(2)}) collective-permute-start(s16[8,272,256]{2,1,0:T(8,128)(2,1)} %pick.11.refs_3_), channel_id=1, source_target_pairs={{0,4},{1,5},{2,6},{3,7},{4,0},{5,1},{6,2},{7,3},{8,12},{9,13},{10,... | collective-permute-start | bytes 3342344 | tf_op jit(solution)/shard_map/ppermute | solution.py:651
  431.0 2.1 pick.10.refs_2_
  433.1 5.8 %collective-permute-start.26 = (s16[8,272,256]{2,1,0:T(8,128)(2,1)}, s16[8,272,256]{2,1,0:T(8,128)(2,1)S(1)}, u32[]{:S(2)}, u32[]{:S(2)}) collective-permute-start(s16[8,272,256]{2,1,0:T(8,128)(2,1)} %pick.10.refs_2_), channel_id=1, source_target_pairs={{0,4},{1,5},{2,6},{3,7},{4,0},{5,1},{6,2},{7,3},{8,12},{9,13},{10,... | collective-permute-start | bytes 3342344 | tf_op jit(solution)/shard_map/ppermute | solution.py:651
  438.9 2.1 pick.15.refs_3_
  441.0 5.8 %collective-permute-start.55 = (s16[8,272,256]{2,1,0:T(8,128)(2,1)}, s16[8,272,256]{2,1,0:T(8,128)(2,1)S(1)}, u32[]{:S(2)}, u32[]{:S(2)}) collective-permute-start(s16[8,272,256]{2,1,0:T(8,128)(2,1)} %pick.15.refs_3_), channel_id=1, source_target_pairs={{0,4},{1,5},{2,6},{3,7},{4,0},{5,1},{6,2},{7,3},{8,12},{9,13},{10,... | collective-permute-start | bytes 3342344 | tf_op jit(solution)/shard_map/ppermute | solution.py:651
  446.8 2.1 pick.14.refs_2_
  448.8 6.0 %collective-permute-start.54 = (s16[8,272,256]{2,1,0:T(8,128)(2,1)}, s16[8,272,256]{2,1,0:T(8,128)(2,1)S(1)}, u32[]{:S(2)}, u32[]{:S(2)}) collective-permute-start(s16[8,272,256]{2,1,0:T(8,128)(2,1)} %pick.14.refs_2_), channel_id=1, source_target_pairs={{0,4},{1,5},{2,6},{3,7},{4,0},{5,1},{6,2},{7,3},{8,12},{9,13},{10,... | collective-permute-start | bytes 3342344 | tf_op jit(solution)/shard_map/ppermute | solution.py:651
  457.7 15.7 %piece.4 = (f32[2048,4096]{1,0:T(8,128)}, f32[2048,1024]{1,0:T(8,128)}) custom-call(s32[32]{0:T(128)} %get-tuple-element.52.rows_ref, s32[32]{0:T(128)} %get-tuple-element.51.cols_ref, s32[32]{0:T(128)} %select_reduce_fusion.2.order_ref, s32[17]{0:T(128)} %convert_reduce_fusion.3.starts_ref, s32[1]{0:T(128)} %bitcast.member_ref, f32[2048,4096]{1,0:T(8,128)} %front_ref.11, ...), custom_call_target="tpu_custom_call" | custom-call | tf_op jit(solution)/shard_map/piece/pallas_call | solution.py:479
  473.4 15.0 %piece.5.refs_6_ = f32[2048,4096]{1,0:T(8,128)} custom-call(s32[32]{0:T(128)} %get-tuple-element.52.rows_ref, s32[32]{0:T(128)} %get-tuple-element.51.cols_ref, s32[32]{0:T(128)} %select_reduce_fusion.2.order_ref, s32[17]{0:T(128)} %convert_reduce_fusion.3.starts_ref, s32[1]{0:T(128)} %bitcast.member_ref, ...), custom_call_target="tpu_custom_call", output_to_operand_aliasing={{}: (13, {})} | custom-call | tf_op jit(solution)/shard_map/piece/pallas_call | solution.py:479
  488.4 14.9 %piece.6.refs_6_ = f32[2048,4096]{1,0:T(8,128)} custom-call(s32[32]{0:T(128)} %get-tuple-element.52.rows_ref, s32[32]{0:T(128)} %get-tuple-element.51.cols_ref, s32[32]{0:T(128)} %select_reduce_fusion.2.order_ref, s32[17]{0:T(128)} %convert_reduce_fusion.3.starts_ref, s32[1]{0:T(128)} %bitcast.member_ref, ...), custom_call_target="tpu_custom_call", output_to_operand_aliasing={{}: (13, {})} | custom-call | tf_op jit(solution)/shard_map/piece/pallas_call | solution.py:479
  503.2 15.0 %piece.7.front_ref = f32[2048,4096]{1,0:T(8,128)} custom-call(s32[32]{0:T(128)} %get-tuple-element.52.rows_ref, s32[32]{0:T(128)} %get-tuple-element.51.cols_ref, s32[32]{0:T(128)} %select_reduce_fusion.2.order_ref, s32[17]{0:T(128)} %convert_reduce_fusion.3.starts_ref, s32[1]{0:T(128)} %bitcast.member_ref, ...), custom_call_target="tpu_custom_call", output_to_operand_aliasing={{}: (13, {})} | custom-call | tf_op jit(solution)/shard_map/piece/pallas_call | solution.py:479
  519.6 40.2 %schur.1 = (f32[2048,4096]{1,0:T(8,128)}, f32[2048,1024]{1,0:T(8,128)}) custom-call(s32[1]{0:T(128)} %bitcast.member_ref, f32[2048,4096]{1,0:T(8,128)} %piece.7.front_ref, s16[8,272,256]{2,1,0:T(8,128)(2,1)} %pick.12.refs_0_, s16[8,272,256]{2,1,0:T(8,128)(2,1)} %pick.13.refs_0_.refs_1_, ...), custom_call_target="tpu_custom_call", output_to_operand_aliasing={{0}: (1, {}), {1}: (8, {})} | custom-call | tf_op jit(solution)/shard_map/schur/pallas_call | solution.py:545
  (178 shorter events, 44.7 us)
Async XLA Ops:
  2.9 10.4 %all-to-all-start = ((s32[8,4,1]{1,2,0:T(1,128)}), s32[8,4,1]{1,2,0:T(1,128)S(1)}, u32[]{:S(2)}, u32[]{:S(2)}) async-start(s32[8,4,1]{1,2,0:T(1,128)} %bitcast.1), calls=%async_computation | async-start | bytes 8192 | tf_op jit(solution)/shard_map/all_to_all | solution.py:607
  13.3 53.7 %all-to-all-start.1 = ((bf16[32,256,256]{2,1,0:T(8,128)(2,1)}), bf16[32,256,256]{2,1,0:T(8,128)(2,1)}, u32[]{:S(2)}, u32[]{:S(2)}) async-start(bf16[32,256,256]{2,1,0:T(8,128)(2,1)} %pack.1), calls=%async_computation.1 | async-start | bytes 8388608 | tf_op jit(solution)/shard_map/all_to_all | solution.py:621
  112.0 26.6 %collective-permute-start.31 = (f32[512,256]{1,0:T(8,128)}, f32[512,256]{1,0:T(8,128)S(1)}, u32[]{:S(2)}, u32[]{:S(2)}) collective-permute-start(f32[512,256]{1,0:T(8,128)} %get-tuple-element.37.refs_4_), channel_id=1, source_target_pairs={{0,16}} | collective-permute-start | bytes 1572872 | tf_op jit(solution)/shard_map/ppermute | solution.py:635
  114.6 25.4 %collective-permute-start.29 = (f32[512,256]{1,0:T(8,128)}, f32[512,256]{1,0:T(8,128)S(1)}, u32[]{:S(2)}, u32[]{:S(2)}) collective-permute-start(f32[512,256]{1,0:T(8,128)} %get-tuple-element.37.refs_4_), channel_id=1, source_target_pairs={{0,8}} | collective-permute-start | bytes 1572872 | tf_op jit(solution)/shard_map/ppermute | solution.py:635
  115.9 26.3 %collective-permute-start.28 = (f32[512,256]{1,0:T(8,128)}, f32[512,256]{1,0:T(8,128)S(1)}, u32[]{:S(2)}, u32[]{:S(2)}) collective-permute-start(f32[512,256]{1,0:T(8,128)} %get-tuple-element.37.refs_4_), channel_id=1, source_target_pairs={{0,4}} | collective-permute-start | bytes 1572872 | tf_op jit(solution)/shard_map/ppermute | solution.py:639
  128.0 5.5 collective-permute-start.41
  129.3 5.5 collective-permute-start.39
  133.5 58.9 %copy-start.32 = (f32[256,256]{1,0:T(8,128)}, f32[256,256]{1,0:T(8,128)S(1)}, u32[]{:S(2)}) copy-start(f32[256,256]{1,0:T(8,128)S(1)} %collective-permute-done.41.refs_10_) | copy-start | bytes 786436
  133.5 25.6 %collective-permute-start.1 = (f32[1024,256]{1,0:T(8,128)S(1)}, f32[1024,256]{1,0:T(8,128)S(1)}, u32[]{:S(2)}, u32[]{:S(2)}) collective-permute-start(f32[1024,256]{1,0:T(8,128)S(1)} %copy-done.18), channel_id=1, source_target_pairs={{0,8}} | collective-permute-start | bytes 3145736 | tf_op jit(solution)/shard_map/ppermute | solution.py:635
  134.9 13.5 %collective-permute-start.13 = (f32[768,256]{1,0:T(8,128)}, f32[768,256]{1,0:T(8,128)S(1)}, u32[]{:S(2)}, u32[]{:S(2)}) collective-permute-start(f32[768,256]{1,0:T(8,128)} %get-tuple-element.29.refs_2_), channel_id=1, source_target_pairs={{0,16}} | collective-permute-start | bytes 2359304 | tf_op jit(solution)/shard_map/ppermute | solution.py:635
  138.6 17.0 %collective-permute-start.11 = (f32[768,256]{1,0:T(8,128)}, f32[768,256]{1,0:T(8,128)S(1)}, u32[]{:S(2)}, u32[]{:S(2)}) collective-permute-start(f32[768,256]{1,0:T(8,128)} %get-tuple-element.29.refs_2_), channel_id=1, source_target_pairs={{0,8}} | collective-permute-start | bytes 2359304 | tf_op jit(solution)/shard_map/ppermute | solution.py:635
  140.0 17.0 %collective-permute-start.10 = (f32[768,256]{1,0:T(8,128)}, f32[768,256]{1,0:T(8,128)}, u32[]{:S(2)}, u32[]{:S(2)}) collective-permute-start(f32[768,256]{1,0:T(8,128)} %get-tuple-element.29.refs_2_), channel_id=1, source_target_pairs={{0,4}} | collective-permute-start | bytes 2359304 | tf_op jit(solution)/shard_map/ppermute | solution.py:639
  142.2 0.7 collective-permute-start.43
  142.9 15.5 %collective-permute-start.32 = (f32[512,256]{1,0:T(8,128)S(1)}, f32[512,256]{1,0:T(8,128)S(1)}, u32[]{:S(2)}, u32[]{:S(2)}) collective-permute-start(f32[512,256]{1,0:T(8,128)S(1)} %collective-permute-done.31.refs_8_), channel_id=1, source_target_pairs={{16,20}} | collective-permute-start | bytes 1572872 | tf_op jit(solution)/shard_map/ppermute | solution.py:639
  148.4 12.4 %collective-permute-start.33 = (f32[512,256]{1,0:T(8,128)S(1)}, f32[512,256]{1,0:T(8,128)}, u32[]{:S(2)}, u32[]{:S(2)}) collective-permute-start(f32[512,256]{1,0:T(8,128)S(1)} %collective-permute-done.29.refs_6_), channel_id=1, source_target_pairs={{8,24}} | collective-permute-start | bytes 1572872 | tf_op jit(solution)/shard_map/ppermute | solution.py:635
  155.6 13.6 %collective-permute-start.3 = (f32[1024,256]{1,0:T(8,128)S(1)}, f32[1024,256]{1,0:T(8,128)S(1)}, u32[]{:S(2)}, u32[]{:S(2)}) collective-permute-start(f32[1024,256]{1,0:T(8,128)S(1)} %copy-done.18), channel_id=1, source_target_pairs={{0,16}} | collective-permute-start | bytes 3145736 | tf_op jit(solution)/shard_map/ppermute | solution.py:635
  157.0 13.8 %collective-permute-start = (f32[1024,256]{1,0:T(8,128)S(1)}, f32[1024,256]{1,0:T(8,128)S(1)}, u32[]{:S(2)}, u32[]{:S(2)}) collective-permute-start(f32[1024,256]{1,0:T(8,128)S(1)} %copy-done.18), channel_id=1, source_target_pairs={{0,4}} | collective-permute-start | bytes 3145736 | tf_op jit(solution)/shard_map/ppermute | solution.py:639
  158.4 3.1 collective-permute-start.30
  159.1 12.5 %collective-permute-start.5 = (f32[1024,256]{1,0:T(8,128)S(1)}, f32[1024,256]{1,0:T(8,128)}, u32[]{:S(2)}, u32[]{:S(2)}) collective-permute-start(f32[1024,256]{1,0:T(8,128)S(1)} %collective-permute-done.1.refs_2_), channel_id=1, source_target_pairs={{8,24}} | collective-permute-start | bytes 3145736 | tf_op jit(solution)/shard_map/ppermute | solution.py:635
  160.8 12.8 %collective-permute-start.14 = (f32[768,256]{1,0:T(8,128)S(1)}, f32[768,256]{1,0:T(8,128)S(1)}, u32[]{:S(2)}, u32[]{:S(2)}) collective-permute-start(f32[768,256]{1,0:T(8,128)S(1)} %collective-permute-done.13.refs_6_), channel_id=1, source_target_pairs={{16,20}} | collective-permute-start | bytes 2359304 | tf_op jit(solution)/shard_map/ppermute | solution.py:639
  161.5 12.8 %collective-permute-start.15 = (f32[768,256]{1,0:T(8,128)S(1)}, f32[768,256]{1,0:T(8,128)}, u32[]{:S(2)}, u32[]{:S(2)}) collective-permute-start(f32[768,256]{1,0:T(8,128)S(1)} %collective-permute-done.11.refs_4_), channel_id=1, source_target_pairs={{8,24}} | collective-permute-start | bytes 2359304 | tf_op jit(solution)/shard_map/ppermute | solution.py:635
  169.2 9.1 %collective-permute-start.4 = (f32[1024,256]{1,0:T(8,128)S(1)}, f32[1024,256]{1,0:T(8,128)}, u32[]{:S(2)}, u32[]{:S(2)}) collective-permute-start(f32[1024,256]{1,0:T(8,128)S(1)} %collective-permute-done.3.refs_4_), channel_id=1, source_target_pairs={{16,20}} | collective-permute-start | bytes 3145736 | tf_op jit(solution)/shard_map/ppermute | solution.py:639
  170.9 8.7 %collective-permute-start.2 = (f32[1024,256]{1,0:T(8,128)S(1)}, f32[1024,256]{1,0:T(8,128)S(1)}, u32[]{:S(2)}, u32[]{:S(2)}) collective-permute-start(f32[1024,256]{1,0:T(8,128)S(1)} %collective-permute-done.1.refs_2_), channel_id=1, source_target_pairs={{8,12}} | collective-permute-start | bytes 3145736 | tf_op jit(solution)/shard_map/ppermute | solution.py:639
  171.9 9.1 %collective-permute-start.6 = (f32[1024,256]{1,0:T(8,128)}, f32[1024,256]{1,0:T(8,128)}, u32[]{:S(2)}, u32[]{:S(2)}) collective-permute-start(f32[1024,256]{1,0:T(8,128)} %collective-permute-done.5.refs_6_), channel_id=1, source_target_pairs={{24,28}} | collective-permute-start | bytes 3145736 | tf_op jit(solution)/shard_map/ppermute | solution.py:639
  173.6 2.3 collective-permute-start.12
  174.3 6.0 %collective-permute-start.16 = (f32[768,256]{1,0:T(8,128)}, f32[768,256]{1,0:T(8,128)}, u32[]{:S(2)}, u32[]{:S(2)}) collective-permute-start(f32[768,256]{1,0:T(8,128)} %collective-permute-done.15.refs_8_), channel_id=1, source_target_pairs={{24,28}} | collective-permute-start | bytes 2359304 | tf_op jit(solution)/shard_map/ppermute | solution.py:639
  176.8 28.4 %collective-permute-start.34 = (f32[512,256]{1,0:T(8,128)}, f32[512,256]{1,0:T(8,128)}, u32[]{:S(2)}, u32[]{:S(2)}) collective-permute-start(f32[512,256]{1,0:T(8,128)} %collective-permute-done.33.refs_10_), channel_id=1, source_target_pairs={{24,28}} | collective-permute-start | bytes 1572872 | tf_op jit(solution)/shard_map/ppermute | solution.py:639
  178.3 38.0 %collective-permute-start.38 = (f32[256,256]{1,0:T(8,128)}, f32[256,256]{1,0:T(8,128)S(1)}, u32[]{:S(2)}, u32[]{:S(2)}) collective-permute-start(f32[256,256]{1,0:T(8,128)} %chol.7.refs_6_), channel_id=1, source_target_pairs={{0,4}} | collective-permute-start | bytes 786440 | tf_op jit(solution)/shard_map/ppermute | solution.py:639
  179.6 38.1 %collective-permute-start.40 = (f32[256,256]{1,0:T(8,128)}, f32[256,256]{1,0:T(8,128)S(1)}, u32[]{:S(2)}, u32[]{:S(2)}) collective-permute-start(f32[256,256]{1,0:T(8,128)} %copy-done.33), channel_id=1, source_target_pairs={{8,12}} | collective-permute-start | bytes 786440 | tf_op jit(solution)/shard_map/ppermute | solution.py:639
  180.3 37.4 %collective-permute-start.42 = (f32[256,256]{1,0:T(8,128)S(1)}, f32[256,256]{1,0:T(8,128)S(1)}, u32[]{:S(2)}, u32[]{:S(2)}) collective-permute-start(f32[256,256]{1,0:T(8,128)S(1)} %collective-permute-done.41.refs_10_), channel_id=1, source_target_pairs={{16,20}} | collective-permute-start | bytes 786440 | tf_op jit(solution)/shard_map/ppermute | solution.py:639
  181.0 36.7 %collective-permute-start.44 = (f32[256,256]{1,0:T(8,128)}, f32[256,256]{1,0:T(8,128)S(1)}, u32[]{:S(2)}, u32[]{:S(2)}) collective-permute-start(f32[256,256]{1,0:T(8,128)} %copy-done.34), channel_id=1, source_target_pairs={{24,28}} | collective-permute-start | bytes 786440 | tf_op jit(solution)/shard_map/ppermute | solution.py:639
  205.2 26.6 %collective-permute-start.17 = (s16[8,272,256]{2,1,0:T(8,128)(2,1)}, s16[8,272,256]{2,1,0:T(8,128)(2,1)S(1)}, u32[]{:S(2)}, u32[]{:S(2)}) collective-permute-start(s16[8,272,256]{2,1,0:T(8,128)(2,1)} %get-tuple-element.30.refs_0_), channel_id=1, source_target_pairs={{0,1},{4,5},{8,9},{12,13},{16,17},{20,21},{24,25},{28,29}} | collective-permute-start | bytes 3342344 | tf_op jit(solution)/shard_map/ppermute | solution.py:645
  216.3 39.2 %collective-permute-start.7 = (s16[8,272,256]{2,1,0:T(8,128)(2,1)S(1)}, s16[8,272,256]{2,1,0:T(8,128)(2,1)S(1)}, u32[]{:S(2)}, u32[]{:S(2)}) collective-permute-start(s16[8,272,256]{2,1,0:T(8,128)(2,1)S(1)} %copy-done.8), channel_id=1, source_target_pairs={{0,1},{4,5},{8,9},{12,13},{16,17},{20,21},{24,25},{28,29}} | collective-permute-start | bytes 3342344 | tf_op jit(solution)/shard_map/ppermute | solution.py:645
  229.0 50.5 %collective-permute-start.45 = (s16[8,272,256]{2,1,0:T(8,128)(2,1)}, s16[8,272,256]{2,1,0:T(8,128)(2,1)S(1)}, u32[]{:S(2)}, u32[]{:S(2)}) collective-permute-start(s16[8,272,256]{2,1,0:T(8,128)(2,1)} %get-tuple-element.42.refs_0_), channel_id=1, source_target_pairs={{0,1},{4,5},{8,9},{12,13},{16,17},{20,21},{24,25},{28,29}} | collective-permute-start | bytes 3342344 | tf_op jit(solution)/shard_map/ppermute | solution.py:645
  230.4 62.3 %collective-permute-start.35 = (s16[8,272,256]{2,1,0:T(8,128)(2,1)S(1)}, s16[8,272,256]{2,1,0:T(8,128)(2,1)S(1)}, u32[]{:S(2)}, u32[]{:S(2)}) collective-permute-start(s16[8,272,256]{2,1,0:T(8,128)(2,1)S(1)} %copy-done.9), channel_id=1, source_target_pairs={{0,1},{4,5},{8,9},{12,13},{16,17},{20,21},{24,25},{28,29}} | collective-permute-start | bytes 3342344 | tf_op jit(solution)/shard_map/ppermute | solution.py:645
  231.8 67.5 %copy-start.10 = (s16[8,272,256]{2,1,0:T(8,128)(2,1)}, s16[8,272,256]{2,1,0:T(8,128)(2,1)S(1)}, u32[]{:S(2)}) copy-start(s16[8,272,256]{2,1,0:T(8,128)(2,1)S(1)} %collective-permute-done.17.refs_1_) | copy-start | bytes 3342340
  231.8 61.6 %collective-permute-start.18 = (s16[8,272,256]{2,1,0:T(8,128)(2,1)S(1)}, s16[8,272,256]{2,1,0:T(8,128)(2,1)S(1)}, u32[]{:S(2)}, u32[]{:S(2)}) collective-permute-start(s16[8,272,256]{2,1,0:T(8,128)(2,1)S(1)} %collective-permute-done.17.refs_1_), channel_id=1, source_target_pairs={{1,2},{5,6},{9,10},{13,14},{17,18},{21,22},{25,26},{29,30}} | collective-permute-start | bytes 3342344 | tf_op jit(solution)/shard_map/ppermute | solution.py:645
  255.6 38.7 %collective-permute-start.8 = (s16[8,272,256]{2,1,0:T(8,128)(2,1)S(1)}, s16[8,272,256]{2,1,0:T(8,128)(2,1)}, u32[]{:S(2)}, u32[]{:S(2)}) collective-permute-start(s16[8,272,256]{2,1,0:T(8,128)(2,1)S(1)} %collective-permute-done.7.refs_1_), channel_id=1, source_target_pairs={{1,2},{5,6},{9,10},{13,14},{17,18},{21,22},{25,26},{29,30}} | collective-permute-start | bytes 3342344 | tf_op jit(solution)/shard_map/ppermute | solution.py:645
  279.5 16.4 %collective-permute-start.46 = (s16[8,272,256]{2,1,0:T(8,128)(2,1)S(1)}, s16[8,272,256]{2,1,0:T(8,128)(2,1)}, u32[]{:S(2)}, u32[]{:S(2)}) collective-permute-start(s16[8,272,256]{2,1,0:T(8,128)(2,1)S(1)} %collective-permute-done.45.refs_1_), channel_id=1, source_target_pairs={{1,2},{5,6},{9,10},{13,14},{17,18},{21,22},{25,26},{29,30}} | collective-permute-start | bytes 3342344 | tf_op jit(solution)/shard_map/ppermute | solution.py:645
  292.7 4.8 collective-permute-start.36
  293.5 4.8 collective-permute-start.19
  294.2 22.9 %collective-permute-start.9 = (s16[8,272,256]{2,1,0:T(8,128)(2,1)}, s16[8,272,256]{2,1,0:T(8,128)(2,1)}, u32[]{:S(2)}, u32[]{:S(2)}) collective-permute-start(s16[8,272,256]{2,1,0:T(8,128)(2,1)} %collective-permute-done.8.refs_2_), channel_id=1, source_target_pairs={{2,3},{6,7},{10,11},{14,15},{18,19},{22,23},{26,27},{30,31}} | collective-permute-start | bytes 3342344 | tf_op jit(solution)/shard_map/ppermute | solution.py:645
  295.9 24.8 %collective-permute-start.47 = (s16[8,272,256]{2,1,0:T(8,128)(2,1)}, s16[8,272,256]{2,1,0:T(8,128)(2,1)}, u32[]{:S(2)}, u32[]{:S(2)}) collective-permute-start(s16[8,272,256]{2,1,0:T(8,128)(2,1)} %collective-permute-done.46.refs_2_), channel_id=1, source_target_pairs={{2,3},{6,7},{10,11},{14,15},{18,19},{22,23},{26,27},{30,31}} | collective-permute-start | bytes 3342344 | tf_op jit(solution)/shard_map/ppermute | solution.py:645
  297.6 26.5 %collective-permute-start.37 = (s16[8,272,256]{2,1,0:T(8,128)(2,1)S(1)}, s16[8,272,256]{2,1,0:T(8,128)(2,1)S(1)}, u32[]{:S(2)}, u32[]{:S(2)}) collective-permute-start(s16[8,272,256]{2,1,0:T(8,128)(2,1)S(1)} %collective-permute-done.36.refs_2_), channel_id=1, source_target_pairs={{2,3},{6,7},{10,11},{14,15},{18,19},{22,23},{26,27},{30,31}} | collective-permute-start | bytes 3342344 | tf_op jit(solution)/shard_map/ppermute | solution.py:645
  301.4 29.0 %collective-permute-start.23 = (s16[8,272,256]{2,1,0:T(8,128)(2,1)}, s16[8,272,256]{2,1,0:T(8,128)(2,1)S(1)}, u32[]{:S(2)}, u32[]{:S(2)}) collective-permute-start(s16[8,272,256]{2,1,0:T(8,128)(2,1)} %pick.9.refs_0_.refs_1_), channel_id=1, source_target_pairs={{0,8},{4,20},{9,25},{13,5},{18,2},{22,30},{27,19},{31,15}} | collective-permute-start | bytes 3342344 | tf_op jit(solution)/shard_map/ppermute | solution.py:649
  319.3 23.0 %collective-permute-start.20 = (s16[8,272,256]{2,1,0:T(8,128)(2,1)}, s16[8,272,256]{2,1,0:T(8,128)(2,1)S(1)}, u32[]{:S(2)}, u32[]{:S(2)}) collective-permute-start(s16[8,272,256]{2,1,0:T(8,128)(2,1)} %pick.8.refs_0_), channel_id=1, source_target_pairs={{0,8},{4,20},{9,25},{13,5},{18,2},{22,30},{27,19},{31,15}} | collective-permute-start | bytes 3342344 | tf_op jit(solution)/shard_map/ppermute | solution.py:649
  322.7 96.5 %copy-start.41 = (s32[4]{0:T(128)S(1)}, s32[4]{0:T(128)}, u32[]{:S(2)}) copy-start(s32[4]{0:T(128)} %constant.139.clone) | copy-start | bytes 52
  322.8 31.5 %collective-permute-start.51 = (s16[8,272,256]{2,1,0:T(8,128)(2,1)}, s16[8,272,256]{2,1,0:T(8,128)(2,1)S(1)}, u32[]{:S(2)}, u32[]{:S(2)}) collective-permute-start(s16[8,272,256]{2,1,0:T(8,128)(2,1)} %pick.13.refs_0_.refs_1_), channel_id=1, source_target_pairs={{0,8},{4,20},{9,25},{13,5},{18,2},{22,30},{27,19},{31,15}} | collective-permute-start | bytes 3342344 | tf_op jit(solution)/shard_map/ppermute | solution.py:649
  327.2 55.7 %collective-permute-start.48 = (s16[8,272,256]{2,1,0:T(8,128)(2,1)}, s16[8,272,256]{2,1,0:T(8,128)(2,1)S(1)}, u32[]{:S(2)}, u32[]{:S(2)}) collective-permute-start(s16[8,272,256]{2,1,0:T(8,128)(2,1)} %pick.12.refs_0_), channel_id=1, source_target_pairs={{0,8},{4,20},{9,25},{13,5},{18,2},{22,30},{27,19},{31,15}} | collective-permute-start | bytes 3342344 | tf_op jit(solution)/shard_map/ppermute | solution.py:649
  330.4 92.8 %copy-start.4 = (s16[8,272,256]{2,1,0:T(8,128)(2,1)}, s16[8,272,256]{2,1,0:T(8,128)(2,1)S(1)}, u32[]{:S(2)}) copy-start(s16[8,272,256]{2,1,0:T(8,128)(2,1)S(1)} %collective-permute-done.23.refs_1_) | copy-start | bytes 3342340
  330.4 54.1 %collective-permute-start.24 = (s16[8,272,256]{2,1,0:T(8,128)(2,1)S(1)}, s16[8,272,256]{2,1,0:T(8,128)(2,1)}, u32[]{:S(2)}, u32[]{:S(2)}) collective-permute-start(s16[8,272,256]{2,1,0:T(8,128)(2,1)S(1)} %collective-permute-done.23.refs_1_), channel_id=1, source_target_pairs={{8,24},{20,28},{25,17},{5,21},{2,10},{30,14},{19,3},{15,7}} | collective-permute-start | bytes 3342344 | tf_op jit(solution)/shard_map/ppermute | solution.py:649
  342.3 82.9 %copy-start.5 = (s16[8,272,256]{2,1,0:T(8,128)(2,1)}, s16[8,272,256]{2,1,0:T(8,128)(2,1)S(1)}, u32[]{:S(2)}) copy-start(s16[8,272,256]{2,1,0:T(8,128)(2,1)S(1)} %collective-permute-done.20.refs_1_) | copy-start | bytes 3342340
  342.3 54.8 %collective-permute-start.21 = (s16[8,272,256]{2,1,0:T(8,128)(2,1)S(1)}, s16[8,272,256]{2,1,0:T(8,128)(2,1)}, u32[]{:S(2)}, u32[]{:S(2)}) collective-permute-start(s16[8,272,256]{2,1,0:T(8,128)(2,1)S(1)} %collective-permute-done.20.refs_1_), channel_id=1, source_target_pairs={{8,24},{20,28},{25,17},{5,21},{2,10},{30,14},{19,3},{15,7}} | collective-permute-start | bytes 3342344 | tf_op jit(solution)/shard_map/ppermute | solution.py:649
  354.3 71.0 %copy-start.6 = (s16[8,272,256]{2,1,0:T(8,128)(2,1)}, s16[8,272,256]{2,1,0:T(8,128)(2,1)S(1)}, u32[]{:S(2)}) copy-start(s16[8,272,256]{2,1,0:T(8,128)(2,1)S(1)} %collective-permute-done.51.refs_1_) | copy-start | bytes 3342340
  354.3 50.2 %collective-permute-start.52 = (s16[8,272,256]{2,1,0:T(8,128)(2,1)S(1)}, s16[8,272,256]{2,1,0:T(8,128)(2,1)}, u32[]{:S(2)}, u32[]{:S(2)}) collective-permute-start(s16[8,272,256]{2,1,0:T(8,128)(2,1)S(1)} %collective-permute-done.51.refs_1_), channel_id=1, source_target_pairs={{8,24},{20,28},{25,17},{5,21},{2,10},{30,14},{19,3},{15,7}} | collective-permute-start | bytes 3342344 | tf_op jit(solution)/shard_map/ppermute | solution.py:649
  382.9 29.0 %collective-permute-start.49 = (s16[8,272,256]{2,1,0:T(8,128)(2,1)S(1)}, s16[8,272,256]{2,1,0:T(8,128)(2,1)}, u32[]{:S(2)}, u32[]{:S(2)}) collective-permute-start(s16[8,272,256]{2,1,0:T(8,128)(2,1)S(1)} %collective-permute-done.48.refs_1_), channel_id=1, source_target_pairs={{8,24},{20,28},{25,17},{5,21},{2,10},{30,14},{19,3},{15,7}} | collective-permute-start | bytes 3342344 | tf_op jit(solution)/shard_map/ppermute | solution.py:649
  384.6 38.6 %collective-permute-start.25 = (s16[8,272,256]{2,1,0:T(8,128)(2,1)}, s16[8,272,256]{2,1,0:T(8,128)(2,1)}, u32[]{:S(2)}, u32[]{:S(2)}) collective-permute-start(s16[8,272,256]{2,1,0:T(8,128)(2,1)} %collective-permute-done.24.refs_2_), channel_id=1, source_target_pairs={{24,16},{28,12},{17,1},{21,29},{10,26},{14,6},{3,11},{7,23}} | collective-permute-start | bytes 3342344 | tf_op jit(solution)/shard_map/ppermute | solution.py:649
  397.1 33.9 %collective-permute-start.22 = (s16[8,272,256]{2,1,0:T(8,128)(2,1)}, s16[8,272,256]{2,1,0:T(8,128)(2,1)}, u32[]{:S(2)}, u32[]{:S(2)}) collective-permute-start(s16[8,272,256]{2,1,0:T(8,128)(2,1)} %collective-permute-done.21.refs_2_), channel_id=1, source_target_pairs={{24,16},{28,12},{17,1},{21,29},{10,26},{14,6},{3,11},{7,23}} | collective-permute-start | bytes 3342344 | tf_op jit(solution)/shard_map/ppermute | solution.py:649
  404.5 34.4 %collective-permute-start.53 = (s16[8,272,256]{2,1,0:T(8,128)(2,1)}, s16[8,272,256]{2,1,0:T(8,128)(2,1)}, u32[]{:S(2)}, u32[]{:S(2)}) collective-permute-start(s16[8,272,256]{2,1,0:T(8,128)(2,1)} %collective-permute-done.52.refs_2_), channel_id=1, source_target_pairs={{24,16},{28,12},{17,1},{21,29},{10,26},{14,6},{3,11},{7,23}} | collective-permute-start | bytes 3342344 | tf_op jit(solution)/shard_map/ppermute | solution.py:649
  411.9 34.9 %collective-permute-start.50 = (s16[8,272,256]{2,1,0:T(8,128)(2,1)}, s16[8,272,256]{2,1,0:T(8,128)(2,1)}, u32[]{:S(2)}, u32[]{:S(2)}) collective-permute-start(s16[8,272,256]{2,1,0:T(8,128)(2,1)} %collective-permute-done.49.refs_2_), channel_id=1, source_target_pairs={{24,16},{28,12},{17,1},{21,29},{10,26},{14,6},{3,11},{7,23}} | collective-permute-start | bytes 3342344 | tf_op jit(solution)/shard_map/ppermute | solution.py:649
  425.2 31.1 %collective-permute-start.27 = (s16[8,272,256]{2,1,0:T(8,128)(2,1)}, s16[8,272,256]{2,1,0:T(8,128)(2,1)S(1)}, u32[]{:S(2)}, u32[]{:S(2)}) collective-permute-start(s16[8,272,256]{2,1,0:T(8,128)(2,1)} %pick.11.refs_3_), channel_id=1, source_target_pairs={{0,4},{1,5},{2,6},{3,7},{4,0},{5,1},{6,2},{7,3},{8,12},{9,13},{10,... | collective-permute-start | bytes 3342344 | tf_op jit(solution)/shard_map/ppermute | solution.py:651
  433.1 23.2 %collective-permute-start.26 = (s16[8,272,256]{2,1,0:T(8,128)(2,1)}, s16[8,272,256]{2,1,0:T(8,128)(2,1)S(1)}, u32[]{:S(2)}, u32[]{:S(2)}) collective-permute-start(s16[8,272,256]{2,1,0:T(8,128)(2,1)} %pick.10.refs_2_), channel_id=1, source_target_pairs={{0,4},{1,5},{2,6},{3,7},{4,0},{5,1},{6,2},{7,3},{8,12},{9,13},{10,... | collective-permute-start | bytes 3342344 | tf_op jit(solution)/shard_map/ppermute | solution.py:651
  441.0 77.3 %collective-permute-start.55 = (s16[8,272,256]{2,1,0:T(8,128)(2,1)}, s16[8,272,256]{2,1,0:T(8,128)(2,1)S(1)}, u32[]{:S(2)}, u32[]{:S(2)}) collective-permute-start(s16[8,272,256]{2,1,0:T(8,128)(2,1)} %pick.15.refs_3_), channel_id=1, source_target_pairs={{0,4},{1,5},{2,6},{3,7},{4,0},{5,1},{6,2},{7,3},{8,12},{9,13},{10,... | collective-permute-start | bytes 3342344 | tf_op jit(solution)/shard_map/ppermute | solution.py:651
  448.8 69.4 %collective-permute-start.54 = (s16[8,272,256]{2,1,0:T(8,128)(2,1)}, s16[8,272,256]{2,1,0:T(8,128)(2,1)S(1)}, u32[]{:S(2)}, u32[]{:S(2)}) collective-permute-start(s16[8,272,256]{2,1,0:T(8,128)(2,1)} %pick.14.refs_2_), channel_id=1, source_target_pairs={{0,4},{1,5},{2,6},{3,7},{4,0},{5,1},{6,2},{7,3},{8,12},{9,13},{10,... | collective-permute-start | bytes 3342344 | tf_op jit(solution)/shard_map/ppermute | solution.py:651
  (36 other events, 501.9 us)

commit v2 on v1

--- a/solution.py
+++ b/solution.py
@@ -145,14 +145,16 @@
     lax.fori_loop(starts_ref[block], starts_ref[block + 1], step, 0)
 
 
-def panel_kernel(rows_ref, cols_ref, order_ref, starts_ref, front_ref, tiles_ref, out_ref):
-    out_ref[...] = front_ref[...]
-    i = pl.program_id(0)
-    high = out_ref.shape[0] // tiles_ref.shape[1]
-    add_tiles((rows_ref, cols_ref, order_ref, starts_ref), tiles_ref, out_ref, i, i * high, 0)
-
-
-def panel(place_rows, place_cols, front, tiles):
+def panel_kernel(active_ref, rows_ref, cols_ref, order_ref, starts_ref, front_ref, tiles_ref, out_ref):
+    @pl.when(active_ref[0] == 1)
+    def _():
+        out_ref[...] = front_ref[...]
+        i = pl.program_id(0)
+        high = out_ref.shape[0] // tiles_ref.shape[1]
+        add_tiles((rows_ref, cols_ref, order_ref, starts_ref), tiles_ref, out_ref, i, i * high, 0)
+
+
+def panel(active, place_rows, place_cols, front, tiles):
     rows = front.shape[0]
     tile = tiles.shape[1]
     high = min(rows, 512)
@@ -162,17 +164,17 @@
         panel_kernel,
         out_shape=jax.ShapeDtypeStruct((rows, PW), F32),
         grid_spec=pltpu.PrefetchScalarGridSpec(
-            num_scalar_prefetch=4,
+            num_scalar_prefetch=5,
             grid=(steps,),
             in_specs=[
-                pl.BlockSpec((high, PW), lambda i, *_: (i, 0)),
+                pl.BlockSpec((high, PW), lambda i, active, *_: (i * active[0], 0)),
                 pl.BlockSpec(tiles.shape, lambda i, *_: (0, 0, 0), pipeline_mode=pl.Buffered(1)),
             ],
-            out_specs=pl.BlockSpec((high, PW), lambda i, *_: (i, 0)),
+            out_specs=pl.BlockSpec((high, PW), lambda i, active, *_: (i * active[0], 0)),
         ),
         compiler_params=params(),
         name="panel",
-    )(place_rows, place_cols, order, starts, front, tiles)
+    )(active, place_rows, place_cols, order, starts, front, tiles)
 
 
 def spread(x, s):
@@ -226,7 +228,13 @@
     return unit * lax.rsqrt(diag)
 
 
-def first_kernel(rows_ref, cols_ref, front_ref, tiles_ref, l_ref, trail_ref, pivot, work):
+def first_kernel(active_ref, rows_ref, cols_ref, front_ref, tiles_ref, l_ref, trail_ref, pivot, work):
+    @pl.when(active_ref[0] == 1)
+    def _():
+        first_step(rows_ref, cols_ref, front_ref, tiles_ref, l_ref, trail_ref, pivot, work)
+
+
+def first_step(rows_ref, cols_ref, front_ref, tiles_ref, l_ref, trail_ref, pivot, work):
     pivot[...] = front_ref[...]
     slots, tile = tiles_ref.shape[:2]
     side = PW // tile
@@ -250,10 +258,12 @@
     eliminate(l_ref, trail_ref, work)
 
 
-def next_kernel(a_ref, l_ref, *rest):
-    work = rest[-1]
-    work[...] = a_ref[...]
-    eliminate(l_ref, rest[0] if len(rest) == 2 else None, work)
+def next_kernel(active_ref, a_ref, l_ref, *rest):
+    @pl.when(active_ref[0] == 1)
+    def _():
+        work = rest[-1]
+        work[...] = a_ref[...]
+        eliminate(l_ref, rest[0] if len(rest) == 2 else None, work)
 
 
 def eliminate(l_ref, trail_ref, work):
@@ -298,13 +308,13 @@
     return pl.BlockSpec(shape, lambda i, *_: (0,) * len(shape))
 
 
-def chol_first(place_rows, place_cols, front, tiles):
+def chol_first(active, place_rows, place_cols, front, tiles):
     shapes = [jax.ShapeDtypeStruct((PW, KP), F32), jax.ShapeDtypeStruct((PW - KP, PW - KP), F32)]
     return pl.pallas_call(
         first_kernel,
         out_shape=shapes,
         grid_spec=pltpu.PrefetchScalarGridSpec(
-            num_scalar_prefetch=2,
+            num_scalar_prefetch=3,
             grid=(1,),
             in_specs=[whole((PW, PW)), whole(tiles.shape)],
             out_specs=[whole(s.shape) for s in shapes],
@@ -312,10 +322,10 @@
         ),
         compiler_params=params(),
         name="chol",
-    )(place_rows, place_cols, front, tiles)
-
-
-def chol_next(a):
+    )(active, place_rows, place_cols, front, tiles)
+
+
+def chol_next(active, a):
     n = a.shape[0]
     shapes = [jax.ShapeDtypeStruct((n, KP), F32)]
     if n > KP:
@@ -323,13 +333,16 @@
     return pl.pallas_call(
         next_kernel,
         out_shape=shapes,
-        grid=(1,),
-        in_specs=[whole((n, n))],
-        out_specs=[whole(s.shape) for s in shapes],
-        scratch_shapes=[pltpu.VMEM((n, n), F32)],
+        grid_spec=pltpu.PrefetchScalarGridSpec(
+            num_scalar_prefetch=1,
+            grid=(1,),
+            in_specs=[whole((n, n))],
+            out_specs=[whole(s.shape) for s in shapes],
+            scratch_shapes=[pltpu.VMEM((n, n), F32)],
+        ),
         compiler_params=params(),
         name="chol",
-    )(a)
+    )(active, a)
 
 
 def eye(n):
@@ -346,6 +359,12 @@
 
 
 def solve_kernel(row_ref, p_ref, *refs, k, sources):
+    @pl.when(row_ref[1] == 1)
+    def _():
+        solve_step(row_ref, p_ref, *refs, k=k, sources=sources)
+
+
+def solve_step(row_ref, p_ref, *refs, k, sources):
     factors, lowers, held = refs[:k], refs[k : 2 * k], refs[2 * k : 2 * k + sources]
     f_ref, q_ref, low_ref, sem = refs[2 * k + sources :]
 
@@ -381,7 +400,7 @@
     k = len(factors)
     rows = panel_sum.shape[0]
     high = min(rows, 4 * GRP)
-    block = pl.BlockSpec((high, KP), lambda i, *_: (i, 0))
+    block = pl.BlockSpec((high, KP), lambda i, row: (i * row[1], 0))
     return pl.pallas_call(
         functools.partial(solve_kernel, k=k, sources=len(held)),
         out_shape=[
@@ -392,13 +411,13 @@
         grid_spec=pltpu.PrefetchScalarGridSpec(
             num_scalar_prefetch=1,
             grid=(rows // high,),
-            in_specs=[pl.BlockSpec((high, KP), lambda i, *_: (i, k))]
+            in_specs=[pl.BlockSpec((high, KP), lambda i, row: (i * row[1], k))]
             + [block] * k
             + [whole(low.shape) for low in lowers]
             + [ANY] * len(held),
             out_specs=[
                 block,
-                pl.BlockSpec((high // GRP, GRP + EXT, KP), lambda i, *_: (i, 0, 0)),
+                pl.BlockSpec((high // GRP, GRP + EXT, KP), lambda i, row: (i * row[1], 0, 0)),
                 whole(held[0].shape),
             ],
             scratch_shapes=[pltpu.SemaphoreType.DMA],
@@ -563,14 +582,14 @@
     return [i ^ (i >> 1) for i in range(n)]
 
 
-def ring_pairs(row_count, col_count, hop):
+def ring_pairs(row_count, col_count, hop, turn):
     chips = row_count // 2
     order = gray(chips)
     pairs = []
     for col in range(col_count):
         at = order.index(col)
         for member in range(2):
-            way = 1 if member == 0 else -1
+            way = turn if member == 0 else -turn
             src = order[(at + way * (hop - 1)) % chips] * 2 + member
             dst = order[(at + way * hop) % chips] * 2 + member
             pairs.append((src * col_count + col, dst * col_count + col))
@@ -621,13 +640,16 @@
     arrived = lax.all_to_all(outgoing, "row", split_axis=0, concat_axis=0, tiled=True)
 
     count = PW // KP
-    row = row_index.reshape(1).astype(jnp.int32)
+    at_first = (col_index == 0).astype(jnp.int32)
+    row = jnp.stack([row_index.astype(jnp.int32), at_first])
+    active = at_first.reshape(1)
+    root = active * (row_index == 0).astype(jnp.int32)
     own, mine, other, factors, lowers = [], [], [], [], []
-    result = chol_first(place_rows, place_cols, front_init, arrived)
-    panel_sum = panel(place_rows, place_cols, front_init, arrived)
+    result = chol_first(root, place_rows, place_cols, front_init, arrived)
+    panel_sum = panel(active, place_rows, place_cols, front_init, arrived)
     for k in range(count):
         if k > 0:
-            result = chol_next(result[-1])
+            result = chol_next(root, result[-1])
         even = [result[0]]
         for chip in range(1, chips):
             parent = above(chip)
@@ -644,10 +666,12 @@
         for hop in range(col_count - 1):
             steps.append(lax.ppermute(steps[-1], "col", [(hop, hop + 1)]))
         own.append(pick(col_index, steps))
-        steps = [own[-1]]
-        for hop in range(1, chips):
-            steps.append(lax.ppermute(steps[-1], both, ring_pairs(row_count, col_count, hop)))
-        mine.append(pick(distance, steps))
+        ahead, back = [own[-1]], [own[-1]]
+        for hop in range(1, chips // 2 + 1):
+            ahead.append(lax.ppermute(ahead[-1], both, ring_pairs(row_count, col_count, hop, 1)))
+        for hop in range(1, chips - chips // 2):
+            back.append(lax.ppermute(back[-1], both, ring_pairs(row_count, col_count, hop, -1)))
+        mine.append(pick(distance, ahead + back[:0:-1]))
         other.append(lax.ppermute(mine[-1], both, swap))
 
     member = member.reshape(1).astype(jnp.int32)

time: 571 us -> 636 us (1.11)
  waiting for transfers between devices: 146 us -> 190 us
  starting transfers between devices: 174 us -> 194 us
    ppermute x12, waiting for transfers between devices: 56.8 us -> 80 us  [body(): steps.append(lax.ppermute(steps[-1], 'col', [(hop, hop + 1)]))]
    ppermute x12, waiting for transfers between devices: 22.4 us -> 44 us  [the longest x8 44 us: body(): lax.ppermute(ahead[-1], both, ring_pairs(row_count, col_count, hop, 1))]
    ppermute x12, starting transfers between devices: 15 us -> 36.2 us  [body(): steps.append(lax.ppermute(steps[-1], 'col', [(hop, hop + 1)]))]
  transfers between devices with their start and end apart: 58 -> 58, of which waited for: 11 -> 12; matrix products, arithmetic and copies ran while one was open for 1% -> 1% of each run, Pallas kernels for 24% -> 20%
where the time goes in v2:
time: 636 us; the launch traced here: 628 us
  Pallas kernels  225 us (35%)
  starting transfers between devices  194 us (31%)
  waiting for transfers between devices  190 us (30%)
  other arithmetic  7.75 us (1%)
    ppermute x12, waiting for transfers between devices, body(): steps.append(lax.ppermute(steps[-1], 'col', [(hop, hop + 1)]))  80 us
    ppermute x8, starting transfers between devices, body(): lax.ppermute(ahead[-1], both, ring_pairs(row_count, col_count, hop, 1))  73 us
    pallas_call x4, Pallas kernels, schur_piece(): pl.pallas_call(functools.partial(piece_kernel, piece=piece, count=count),...  60.6 us
    all_to_all x1, waiting for transfers between devices, body(): lax.all_to_all(outgoing, 'row', split_axis=0, concat_axis=0, tiled=True)  47.2 us
    ppermute x8, waiting for transfers between devices, body(): lax.ppermute(ahead[-1], both, ring_pairs(row_count, col_count, hop, 1))  44 us
    pallas_call x1, Pallas kernels, schur_rest(): pl.pallas_call(functools.partial(schur_kernel, count=count), out_shape=[j...  40.2 us
    pallas_call x3, Pallas kernels, chol_next(): pl.pallas_call(next_kernel, out_shape=shapes, grid_spec=pltpu.PrefetchSca...  37.1 us
    pallas_call x4, Pallas kernels, solve(): pl.pallas_call(functools.partial(solve_kernel, k=k, sources=len(held)), o...  36.9 us
  transfers between devices with their start and end apart: 58, of which 12 were waited for; matrix products, arithmetic and copies ran while one was open for 1% of the time, Pallas kernels for 20%

profile of v2, /device:TPU:0, one launch (start us, length us, event | category | flops | bytes accessed | tf_op | source)
XLA Modules:
  0.0 627.8 jit_solution(6528139071812776679)
XLA Ops:
  2.8 5.2 all-to-all-start
  8.0 5.2 pack.1
  13.2 4.6 all-to-all-start.1
  19.7 47.2 %all-to-all-done.1.tiles_ref = bf16[32,256,256]{2,1,0:T(8,128)(2,1)} async-done(((bf16[32,256,256]{2,1,0:T(8,128)(2,1)}), bf16[32,256,256]{2,1,0:T(8,128)(2,1)}, u32[]{:S(2)}, u32[]{:S(2)}) %all-to-all-start.1) | async-done | bytes 4194336 | tf_op jit(solution)/shard_map/all_to_all | solution.py:640
  66.9 19.4 %chol.4 = (f32[1024,256]{1,0:T(8,128)}, f32[768,768]{1,0:T(8,128)}) custom-call(s32[1]{0:T(128)S(6)} %mul.37.active_ref, s32[32]{0:T(128)} %get-tuple-element.52.rows_ref, s32[32]{0:T(128)} %get-tuple-element.51.cols_ref, f32[2048,4096]{1,0:T(8,128)} %front_ref.11, bf16[32,256,256]{2,1,0:T(8,128)(2,1)} %all-to-all-done.1.tiles_ref), custom_call_target="tpu_custom_call" | custom-call | tf_op jit(solution)/shard_map/chol/pallas_call | solution.py:313
  86.3 14.0 %chol.5 = (f32[768,256]{1,0:T(8,128)}, f32[512,512]{1,0:T(8,128)}) custom-call(s32[1]{0:T(128)S(6)} %mul.37.active_ref, f32[768,768]{1,0:T(8,128)} %get-tuple-element.28.a_ref), custom_call_target="tpu_custom_call" | custom-call | tf_op jit(solution)/shard_map/chol/pallas_call | solution.py:333
  100.2 12.2 %chol.6 = (f32[512,256]{1,0:T(8,128)}, f32[256,256]{1,0:T(8,128)}) custom-call(s32[1]{0:T(128)S(6)} %mul.37.active_ref, f32[512,512]{1,0:T(8,128)} %get-tuple-element.36.a_ref), custom_call_target="tpu_custom_call" | custom-call | tf_op jit(solution)/shard_map/chol/pallas_call | solution.py:333
  113.7 2.1 collective-permute-start.29
  117.1 11.0 %chol.7.refs_6_ = f32[256,256]{1,0:T(8,128)} custom-call(s32[1]{0:T(128)S(6)} %mul.37.active_ref, f32[256,256]{1,0:T(8,128)} %get-tuple-element.41.a_ref), custom_call_target="tpu_custom_call" | custom-call | tf_op jit(solution)/shard_map/chol/pallas_call | solution.py:333
  128.1 2.0 collective-permute-start.41
  130.1 2.0 collective-permute-start.39
  132.1 1.5 collective-permute-done.41.refs_10_
  135.6 3.2 collective-permute-start.13
  138.8 1.9 collective-permute-start.11
  140.8 2.2 collective-permute-start.10
  145.0 3.5 collective-permute-done.13.refs_6_
  148.6 1.5 collective-permute-start.33
  150.1 5.7 collective-permute-done.11.refs_4_
  161.4 7.9 %collective-permute-done.3.refs_4_ = f32[1024,256]{1,0:T(8,128)S(1)} collective-permute-done((f32[1024,256]{1,0:T(8,128)S(1)}, f32[1024,256]{1,0:T(8,128)S(1)}, u32[]{:S(2)}, u32[]{:S(2)}) %collective-permute-start.3) | collective-permute-done | bytes 1048608 | tf_op jit(solution)/shard_map/ppermute | solution.py:657
  173.1 1.5 collective-permute-start.34
  175.2 2.0 collective-permute-start.38
  178.6 1.4 collective-permute-start.42
  179.9 1.8 collective-permute-start.44
  183.1 9.2 %panel.1.p_ref = f32[2048,1024]{1,0:T(8,128)} custom-call(s32[1]{0:T(128)} %bitcast.4.active_ref, s32[32]{0:T(128)} %get-tuple-element.52.rows_ref, s32[32]{0:T(128)} %get-tuple-element.51.cols_ref, s32[32]{0:T(128)} %select_reduce_fusion.order_ref, s32[5]{0:T(128)} %convert_reduce_fusion.4.starts_ref, f32[2048,4096]{1,0:T(8,128)} %front_ref.11, ...), custom_call_target="tpu_custom_call" | custom-call | tf_op jit(solution)/shard_map/panel/pallas_call | solution.py:163
  192.3 6.5 %solve.4 = (f32[2048,256]{1,0:T(8,128)}, s16[8,272,256]{2,1,0:T(8,128)(2,1)}, f32[1024,256]{1,0:T(8,128)}) custom-call(s32[2]{0:T(128)} %pad_add_fusion.row_ref, f32[2048,1024]{1,0:T(8,128)} %panel.1.p_ref, f32[1024,256]{1,0:T(8,128)} %get-tuple-element.24.refs_0_, f32[1024,256]{1,0:T(8,128)} %copy-done.27, f32[1024,256]{1,0:T(8,128)} %copy-done.25, ...), custom_call_target="tpu_custom_call" | custom-call | tf_op jit(solution)/shard_map/solve/pallas_call | solution.py:404
  198.8 8.2 %solve.5 = (f32[2048,256]{1,0:T(8,128)}, s16[8,272,256]{2,1,0:T(8,128)(2,1)}, f32[768,256]{1,0:T(8,128)}) custom-call(s32[2]{0:T(128)} %pad_add_fusion.row_ref, f32[2048,1024]{1,0:T(8,128)} %panel.1.p_ref, f32[2048,256]{1,0:T(8,128)} %get-tuple-element.26.refs_0_, f32[1024,256]{1,0:T(8,128)} %get-tuple-element.27.refs_1_.refs_2_.refs_3_, ...), custom_call_target="tpu_custom_call" | custom-call | tf_op jit(solution)/shard_map/solve/pallas_call | solution.py:404
  207.1 10.6 %solve.6 = (f32[2048,256]{1,0:T(8,128)}, s16[8,272,256]{2,1,0:T(8,128)(2,1)}, f32[512,256]{1,0:T(8,128)}) custom-call(s32[2]{0:T(128)} %pad_add_fusion.row_ref, f32[2048,1024]{1,0:T(8,128)} %panel.1.p_ref, f32[2048,256]{1,0:T(8,128)} %get-tuple-element.26.refs_0_, f32[2048,256]{1,0:T(8,128)} %get-tuple-element.34.refs_1_, ...), custom_call_target="tpu_custom_call" | custom-call | tf_op jit(solution)/shard_map/solve/pallas_call | solution.py:404
  217.8 11.5 %solve.7 = (f32[2048,256]{1,0:T(8,128)}, s16[8,272,256]{2,1,0:T(8,128)(2,1)}, f32[256,256]{1,0:T(8,128)}) custom-call(s32[2]{0:T(128)} %pad_add_fusion.row_ref, f32[2048,1024]{1,0:T(8,128)} %panel.1.p_ref, f32[2048,256]{1,0:T(8,128)} %get-tuple-element.26.refs_0_, f32[2048,256]{1,0:T(8,128)} %get-tuple-element.34.refs_1_, ...), custom_call_target="tpu_custom_call" | custom-call | tf_op jit(solution)/shard_map/solve/pallas_call | solution.py:404
  230.7 1.4 collective-permute-start.17
  234.8 21.0 %collective-permute-done.45.refs_1_ = s16[8,272,256]{2,1,0:T(8,128)(2,1)S(1)} collective-permute-done((s16[8,272,256]{2,1,0:T(8,128)(2,1)}, s16[8,272,256]{2,1,0:T(8,128)(2,1)S(1)}, u32[]{:S(2)}, u32[]{:S(2)}) %collective-permute-start.45) | collective-permute-done | bytes 1114144 | tf_op jit(solution)/shard_map/ppermute | solution.py:667
  256.6 23.0 %collective-permute-done.17.refs_1_ = s16[8,272,256]{2,1,0:T(8,128)(2,1)S(1)} collective-permute-done((s16[8,272,256]{2,1,0:T(8,128)(2,1)S(1)}, s16[8,272,256]{2,1,0:T(8,128)(2,1)S(1)}, u32[]{:S(2)}, u32[]{:S(2)}) %collective-permute-start.17) | collective-permute-done | bytes 1114144 | tf_op jit(solution)/shard_map/ppermute | solution.py:667
  280.4 23.1 %collective-permute-done.7.refs_1_ = s16[8,272,256]{2,1,0:T(8,128)(2,1)S(1)} collective-permute-done((s16[8,272,256]{2,1,0:T(8,128)(2,1)S(1)}, s16[8,272,256]{2,1,0:T(8,128)(2,1)S(1)}, u32[]{:S(2)}, u32[]{:S(2)}) %collective-permute-start.7) | collective-permute-done | bytes 1114144 | tf_op jit(solution)/shard_map/ppermute | solution.py:667
  304.2 12.8 %collective-permute-done.35.refs_1_ = s16[8,272,256]{2,1,0:T(8,128)(2,1)S(1)} collective-permute-done((s16[8,272,256]{2,1,0:T(8,128)(2,1)S(1)}, s16[8,272,256]{2,1,0:T(8,128)(2,1)S(1)}, u32[]{:S(2)}, u32[]{:S(2)}) %collective-permute-start.35) | collective-permute-done | bytes 1114144 | tf_op jit(solution)/shard_map/ppermute | solution.py:667
  317.8 22.9 %collective-permute-start.47 = (s16[8,272,256]{2,1,0:T(8,128)(2,1)S(1)}, s16[8,272,256]{2,1,0:T(8,128)(2,1)S(1)}, u32[]{:S(2)}, u32[]{:S(2)}) collective-permute-start(s16[8,272,256]{2,1,0:T(8,128)(2,1)S(1)} %collective-permute-done.46.refs_2_), channel_id=1, source_target_pairs={{2,3},{6,7},{10,11},{14,15},{18,19},{22,23},{26,27},{30,31}} | collective-permute-start | bytes 3342344 | tf_op jit(solution)/shard_map/ppermute | solution.py:667
  340.7 1.7 collective-permute-start.19
  342.4 1.7 collective-permute-start.9
  344.1 1.7 collective-permute-start.37
  346.8 2.1 pick.13.refs_0_.refs_1_
  348.9 3.9 collective-permute-start.51
  352.8 2.1 pick.9.refs_0_.refs_1_
  354.8 2.4 collective-permute-start.23
  357.2 2.1 pick.8.refs_0_
  359.3 2.6 collective-permute-start.20
  361.9 2.0 pick.12.refs_0_
  368.1 20.8 %collective-permute-done.23.refs_1_ = s16[8,272,256]{2,1,0:T(8,128)(2,1)} collective-permute-done((s16[8,272,256]{2,1,0:T(8,128)(2,1)}, s16[8,272,256]{2,1,0:T(8,128)(2,1)}, u32[]{:S(2)}, u32[]{:S(2)}) %collective-permute-start.23) | collective-permute-done | bytes 1114144 | tf_op jit(solution)/shard_map/ppermute | solution.py:671
  389.6 23.1 %collective-permute-done.20.refs_1_ = s16[8,272,256]{2,1,0:T(8,128)(2,1)} collective-permute-done((s16[8,272,256]{2,1,0:T(8,128)(2,1)}, s16[8,272,256]{2,1,0:T(8,128)(2,1)}, u32[]{:S(2)}, u32[]{:S(2)}) %collective-permute-start.20) | collective-permute-done | bytes 1114144 | tf_op jit(solution)/shard_map/ppermute | solution.py:671
  412.8 41.0 %collective-permute-start.21 = (s16[8,272,256]{2,1,0:T(8,128)(2,1)}, s16[8,272,256]{2,1,0:T(8,128)(2,1)}, u32[]{:S(2)}, u32[]{:S(2)}) collective-permute-start(s16[8,272,256]{2,1,0:T(8,128)(2,1)} %collective-permute-done.20.refs_1_), channel_id=1, source_target_pairs={{8,24},{20,28},{25,17},{5,21},{2,10},{30,14},{19,3},{15,7}} | collective-permute-start | bytes 3342344 | tf_op jit(solution)/shard_map/ppermute | solution.py:671
  453.8 4.8 collective-permute-start.53
  458.6 19.4 %collective-permute-start.52 = (s16[8,272,256]{2,1,0:T(8,128)(2,1)S(1)}, s16[8,272,256]{2,1,0:T(8,128)(2,1)}, u32[]{:S(2)}, u32[]{:S(2)}) collective-permute-start(s16[8,272,256]{2,1,0:T(8,128)(2,1)S(1)} %collective-permute-done.51.refs_1_), channel_id=1, source_target_pairs={{8,24},{20,28},{25,17},{5,21},{2,10},{30,14},{19,3},{15,7}} | collective-permute-start | bytes 3342344 | tf_op jit(solution)/shard_map/ppermute | solution.py:671
  478.0 4.8 collective-permute-start.50
  483.8 1.7 collective-permute-start.49
  489.5 2.0 pick.11.refs_3_
  491.6 7.1 %collective-permute-start.27 = (s16[8,272,256]{2,1,0:T(8,128)(2,1)}, s16[8,272,256]{2,1,0:T(8,128)(2,1)S(1)}, u32[]{:S(2)}, u32[]{:S(2)}) collective-permute-start(s16[8,272,256]{2,1,0:T(8,128)(2,1)} %pick.11.refs_3_), channel_id=1, source_target_pairs={{0,4},{1,5},{2,6},{3,7},{4,0},{5,1},{6,2},{7,3},{8,12},{9,13},{10,... | collective-permute-start | bytes 3342344 | tf_op jit(solution)/shard_map/ppermute | solution.py:675
  498.7 2.1 pick.10.refs_2_
  500.8 5.8 collective-permute-start.26
  506.6 2.1 pick.15.refs_3_
  508.7 5.8 collective-permute-start.55
  514.5 2.0 pick.14.refs_2_
  516.6 5.9 collective-permute-start.54
  525.4 15.7 %piece.4 = (f32[2048,4096]{1,0:T(8,128)}, f32[2048,1024]{1,0:T(8,128)}) custom-call(s32[32]{0:T(128)} %get-tuple-element.52.rows_ref, s32[32]{0:T(128)} %get-tuple-element.51.cols_ref, s32[32]{0:T(128)} %select_reduce_fusion.2.order_ref, s32[17]{0:T(128)} %convert_reduce_fusion.3.starts_ref, s32[1]{0:T(128)} %bitcast.member_ref, f32[2048,4096]{1,0:T(8,128)} %front_ref.11, ...), custom_call_target="tpu_custom_call" | custom-call | tf_op jit(solution)/shard_map/piece/pallas_call | solution.py:498
  541.1 15.0 %piece.5.refs_6_ = f32[2048,4096]{1,0:T(8,128)} custom-call(s32[32]{0:T(128)} %get-tuple-element.52.rows_ref, s32[32]{0:T(128)} %get-tuple-element.51.cols_ref, s32[32]{0:T(128)} %select_reduce_fusion.2.order_ref, s32[17]{0:T(128)} %convert_reduce_fusion.3.starts_ref, s32[1]{0:T(128)} %bitcast.member_ref, ...), custom_call_target="tpu_custom_call", output_to_operand_aliasing={{}: (13, {})} | custom-call | tf_op jit(solution)/shard_map/piece/pallas_call | solution.py:498
  556.1 14.9 %piece.6.refs_6_ = f32[2048,4096]{1,0:T(8,128)} custom-call(s32[32]{0:T(128)} %get-tuple-element.52.rows_ref, s32[32]{0:T(128)} %get-tuple-element.51.cols_ref, s32[32]{0:T(128)} %select_reduce_fusion.2.order_ref, s32[17]{0:T(128)} %convert_reduce_fusion.3.starts_ref, s32[1]{0:T(128)} %bitcast.member_ref, ...), custom_call_target="tpu_custom_call", output_to_operand_aliasing={{}: (13, {})} | custom-call | tf_op jit(solution)/shard_map/piece/pallas_call | solution.py:498
  570.9 15.0 %piece.7.front_ref = f32[2048,4096]{1,0:T(8,128)} custom-call(s32[32]{0:T(128)} %get-tuple-element.52.rows_ref, s32[32]{0:T(128)} %get-tuple-element.51.cols_ref, s32[32]{0:T(128)} %select_reduce_fusion.2.order_ref, s32[17]{0:T(128)} %convert_reduce_fusion.3.starts_ref, s32[1]{0:T(128)} %bitcast.member_ref, ...), custom_call_target="tpu_custom_call", output_to_operand_aliasing={{}: (13, {})} | custom-call | tf_op jit(solution)/shard_map/piece/pallas_call | solution.py:498
  587.4 40.2 %schur.1 = (f32[2048,4096]{1,0:T(8,128)}, f32[2048,1024]{1,0:T(8,128)}) custom-call(s32[1]{0:T(128)} %bitcast.member_ref, f32[2048,4096]{1,0:T(8,128)} %piece.7.front_ref, s16[8,272,256]{2,1,0:T(8,128)(2,1)} %pick.12.refs_0_, s16[8,272,256]{2,1,0:T(8,128)(2,1)} %pick.13.refs_0_.refs_1_, ...), custom_call_target="tpu_custom_call", output_to_operand_aliasing={{0}: (1, {}), {1}: (8, {})} | custom-call | tf_op jit(solution)/shard_map/schur/pallas_call | solution.py:564
  (185 shorter events, 42.9 us)
Async XLA Ops:
  2.8 10.4 %all-to-all-start = ((s32[8,4,1]{1,2,0:T(1,128)}), s32[8,4,1]{1,2,0:T(1,128)S(1)}, u32[]{:S(2)}, u32[]{:S(2)}) async-start(s32[8,4,1]{1,2,0:T(1,128)} %bitcast.1), calls=%async_computation | async-start | bytes 8192 | tf_op jit(solution)/shard_map/all_to_all | solution.py:626
  13.2 53.7 %all-to-all-start.1 = ((bf16[32,256,256]{2,1,0:T(8,128)(2,1)}), bf16[32,256,256]{2,1,0:T(8,128)(2,1)}, u32[]{:S(2)}, u32[]{:S(2)}) async-start(bf16[32,256,256]{2,1,0:T(8,128)(2,1)} %pack.1), calls=%async_computation.1 | async-start | bytes 8388608 | tf_op jit(solution)/shard_map/all_to_all | solution.py:640
  112.4 26.4 %collective-permute-start.31 = (f32[512,256]{1,0:T(8,128)}, f32[512,256]{1,0:T(8,128)S(1)}, u32[]{:S(2)}, u32[]{:S(2)}) collective-permute-start(f32[512,256]{1,0:T(8,128)} %get-tuple-element.37.refs_4_), channel_id=1, source_target_pairs={{0,16}} | collective-permute-start | bytes 1572872 | tf_op jit(solution)/shard_map/ppermute | solution.py:657
  113.7 27.1 %collective-permute-start.29 = (f32[512,256]{1,0:T(8,128)}, f32[512,256]{1,0:T(8,128)}, u32[]{:S(2)}, u32[]{:S(2)}) collective-permute-start(f32[512,256]{1,0:T(8,128)} %get-tuple-element.37.refs_4_), channel_id=1, source_target_pairs={{0,8}} | collective-permute-start | bytes 1572872 | tf_op jit(solution)/shard_map/ppermute | solution.py:657
  115.8 27.2 %collective-permute-start.28 = (f32[512,256]{1,0:T(8,128)}, f32[512,256]{1,0:T(8,128)S(1)}, u32[]{:S(2)}, u32[]{:S(2)}) collective-permute-start(f32[512,256]{1,0:T(8,128)} %get-tuple-element.37.refs_4_), channel_id=1, source_target_pairs={{0,4}} | collective-permute-start | bytes 1572872 | tf_op jit(solution)/shard_map/ppermute | solution.py:661
  128.1 5.5 collective-permute-start.41
  130.1 5.5 collective-permute-start.39
  133.6 25.6 %collective-permute-start.1 = (f32[1024,256]{1,0:T(8,128)S(1)}, f32[1024,256]{1,0:T(8,128)S(1)}, u32[]{:S(2)}, u32[]{:S(2)}) collective-permute-start(f32[1024,256]{1,0:T(8,128)S(1)} %copy-done.24), channel_id=1, source_target_pairs={{0,8}} | collective-permute-start | bytes 3145736 | tf_op jit(solution)/shard_map/ppermute | solution.py:657
  135.6 13.0 %collective-permute-start.13 = (f32[768,256]{1,0:T(8,128)}, f32[768,256]{1,0:T(8,128)S(1)}, u32[]{:S(2)}, u32[]{:S(2)}) collective-permute-start(f32[768,256]{1,0:T(8,128)} %get-tuple-element.29.refs_2_), channel_id=1, source_target_pairs={{0,16}} | collective-permute-start | bytes 2359304 | tf_op jit(solution)/shard_map/ppermute | solution.py:657
  138.8 16.9 %collective-permute-start.11 = (f32[768,256]{1,0:T(8,128)}, f32[768,256]{1,0:T(8,128)S(1)}, u32[]{:S(2)}, u32[]{:S(2)}) collective-permute-start(f32[768,256]{1,0:T(8,128)} %get-tuple-element.29.refs_2_), channel_id=1, source_target_pairs={{0,8}} | collective-permute-start | bytes 2359304 | tf_op jit(solution)/shard_map/ppermute | solution.py:657
  140.8 16.3 %collective-permute-start.10 = (f32[768,256]{1,0:T(8,128)}, f32[768,256]{1,0:T(8,128)}, u32[]{:S(2)}, u32[]{:S(2)}) collective-permute-start(f32[768,256]{1,0:T(8,128)} %get-tuple-element.29.refs_2_), channel_id=1, source_target_pairs={{0,4}} | collective-permute-start | bytes 2359304 | tf_op jit(solution)/shard_map/ppermute | solution.py:661
  143.0 1.4 collective-permute-start.43
  144.3 14.1 %collective-permute-start.32 = (f32[512,256]{1,0:T(8,128)S(1)}, f32[512,256]{1,0:T(8,128)S(1)}, u32[]{:S(2)}, u32[]{:S(2)}) collective-permute-start(f32[512,256]{1,0:T(8,128)S(1)} %collective-permute-done.31.refs_8_), channel_id=1, source_target_pairs={{16,20}} | collective-permute-start | bytes 1572872 | tf_op jit(solution)/shard_map/ppermute | solution.py:661
  148.6 43.8 %copy-start.32 = (f32[768,256]{1,0:T(8,128)}, f32[768,256]{1,0:T(8,128)S(1)}, u32[]{:S(2)}) copy-start(f32[768,256]{1,0:T(8,128)S(1)} %collective-permute-done.13.refs_6_) | copy-start | bytes 2359300
  148.6 11.4 %collective-permute-start.33 = (f32[512,256]{1,0:T(8,128)}, f32[512,256]{1,0:T(8,128)}, u32[]{:S(2)}, u32[]{:S(2)}) collective-permute-start(f32[512,256]{1,0:T(8,128)} %collective-permute-done.29.refs_6_), channel_id=1, source_target_pairs={{8,24}} | collective-permute-start | bytes 1572872 | tf_op jit(solution)/shard_map/ppermute | solution.py:657
  155.7 13.6 %collective-permute-start.3 = (f32[1024,256]{1,0:T(8,128)S(1)}, f32[1024,256]{1,0:T(8,128)S(1)}, u32[]{:S(2)}, u32[]{:S(2)}) collective-permute-start(f32[1024,256]{1,0:T(8,128)S(1)} %copy-done.24), channel_id=1, source_target_pairs={{0,16}} | collective-permute-start | bytes 3145736 | tf_op jit(solution)/shard_map/ppermute | solution.py:657
  157.1 13.0 %collective-permute-start = (f32[1024,256]{1,0:T(8,128)S(1)}, f32[1024,256]{1,0:T(8,128)S(1)}, u32[]{:S(2)}, u32[]{:S(2)}) collective-permute-start(f32[1024,256]{1,0:T(8,128)S(1)} %copy-done.24), channel_id=1, source_target_pairs={{0,4}} | collective-permute-start | bytes 3145736 | tf_op jit(solution)/shard_map/ppermute | solution.py:661
  158.5 2.2 collective-permute-start.30
  159.2 11.6 %collective-permute-start.5 = (f32[1024,256]{1,0:T(8,128)S(1)}, f32[1024,256]{1,0:T(8,128)S(1)}, u32[]{:S(2)}, u32[]{:S(2)}) collective-permute-start(f32[1024,256]{1,0:T(8,128)S(1)} %collective-permute-done.1.refs_2_), channel_id=1, source_target_pairs={{8,24}} | collective-permute-start | bytes 3145736 | tf_op jit(solution)/shard_map/ppermute | solution.py:657
  160.0 11.6 %collective-permute-start.14 = (f32[768,256]{1,0:T(8,128)S(1)}, f32[768,256]{1,0:T(8,128)S(1)}, u32[]{:S(2)}, u32[]{:S(2)}) collective-permute-start(f32[768,256]{1,0:T(8,128)S(1)} %collective-permute-done.13.refs_6_), channel_id=1, source_target_pairs={{16,20}} | collective-permute-start | bytes 2359304 | tf_op jit(solution)/shard_map/ppermute | solution.py:661
  160.7 11.6 %collective-permute-start.15 = (f32[768,256]{1,0:T(8,128)S(1)}, f32[768,256]{1,0:T(8,128)S(1)}, u32[]{:S(2)}, u32[]{:S(2)}) collective-permute-start(f32[768,256]{1,0:T(8,128)S(1)} %collective-permute-done.11.refs_4_), channel_id=1, source_target_pairs={{8,24}} | collective-permute-start | bytes 2359304 | tf_op jit(solution)/shard_map/ppermute | solution.py:657
  169.3 5.9 collective-permute-start.4
  170.1 7.1 %collective-permute-start.2 = (f32[1024,256]{1,0:T(8,128)S(1)}, f32[1024,256]{1,0:T(8,128)S(1)}, u32[]{:S(2)}, u32[]{:S(2)}) collective-permute-start(f32[1024,256]{1,0:T(8,128)S(1)} %collective-permute-done.1.refs_2_), channel_id=1, source_target_pairs={{8,12}} | collective-permute-start | bytes 3145736 | tf_op jit(solution)/shard_map/ppermute | solution.py:661
  170.8 9.1 %collective-permute-start.6 = (f32[1024,256]{1,0:T(8,128)S(1)}, f32[1024,256]{1,0:T(8,128)S(1)}, u32[]{:S(2)}, u32[]{:S(2)}) collective-permute-start(f32[1024,256]{1,0:T(8,128)S(1)} %collective-permute-done.5.refs_6_), channel_id=1, source_target_pairs={{24,28}} | collective-permute-start | bytes 3145736 | tf_op jit(solution)/shard_map/ppermute | solution.py:661
  171.6 1.5 collective-permute-start.12
  172.3 6.2 collective-permute-start.16
  173.1 34.0 %collective-permute-start.34 = (f32[512,256]{1,0:T(8,128)}, f32[512,256]{1,0:T(8,128)}, u32[]{:S(2)}, u32[]{:S(2)}) collective-permute-start(f32[512,256]{1,0:T(8,128)} %collective-permute-done.33.refs_10_), channel_id=1, source_target_pairs={{24,28}} | collective-permute-start | bytes 1572872 | tf_op jit(solution)/shard_map/ppermute | solution.py:661
  175.2 42.5 %collective-permute-start.38 = (f32[256,256]{1,0:T(8,128)}, f32[256,256]{1,0:T(8,128)}, u32[]{:S(2)}, u32[]{:S(2)}) collective-permute-start(f32[256,256]{1,0:T(8,128)} %chol.7.refs_6_), channel_id=1, source_target_pairs={{0,4}} | collective-permute-start | bytes 786440 | tf_op jit(solution)/shard_map/ppermute | solution.py:661
  177.2 40.5 %collective-permute-start.40 = (f32[256,256]{1,0:T(8,128)}, f32[256,256]{1,0:T(8,128)}, u32[]{:S(2)}, u32[]{:S(2)}) collective-permute-start(f32[256,256]{1,0:T(8,128)} %collective-permute-done.39.refs_8_), channel_id=1, source_target_pairs={{8,12}} | collective-permute-start | bytes 786440 | tf_op jit(solution)/shard_map/ppermute | solution.py:661
  178.6 39.2 %collective-permute-start.42 = (f32[256,256]{1,0:T(8,128)}, f32[256,256]{1,0:T(8,128)}, u32[]{:S(2)}, u32[]{:S(2)}) collective-permute-start(f32[256,256]{1,0:T(8,128)} %collective-permute-done.41.refs_10_), channel_id=1, source_target_pairs={{16,20}} | collective-permute-start | bytes 786440 | tf_op jit(solution)/shard_map/ppermute | solution.py:661
  179.9 37.8 %collective-permute-start.44 = (f32[256,256]{1,0:T(8,128)}, f32[256,256]{1,0:T(8,128)}, u32[]{:S(2)}, u32[]{:S(2)}) collective-permute-start(f32[256,256]{1,0:T(8,128)} %collective-permute-done.43.refs_12_), channel_id=1, source_target_pairs={{24,28}} | collective-permute-start | bytes 786440 | tf_op jit(solution)/shard_map/ppermute | solution.py:661
  229.3 26.6 %collective-permute-start.45 = (s16[8,272,256]{2,1,0:T(8,128)(2,1)}, s16[8,272,256]{2,1,0:T(8,128)(2,1)S(1)}, u32[]{:S(2)}, u32[]{:S(2)}) collective-permute-start(s16[8,272,256]{2,1,0:T(8,128)(2,1)} %get-tuple-element.42.refs_0_), channel_id=1, source_target_pairs={{0,1},{4,5},{8,9},{12,13},{16,17},{20,21},{24,25},{28,29}} | collective-permute-start | bytes 3342344 | tf_op jit(solution)/shard_map/ppermute | solution.py:667
  230.7 48.9 %collective-permute-start.17 = (s16[8,272,256]{2,1,0:T(8,128)(2,1)S(1)}, s16[8,272,256]{2,1,0:T(8,128)(2,1)S(1)}, u32[]{:S(2)}, u32[]{:S(2)}) collective-permute-start(s16[8,272,256]{2,1,0:T(8,128)(2,1)S(1)} %copy-done.11), channel_id=1, source_target_pairs={{0,1},{4,5},{8,9},{12,13},{16,17},{20,21},{24,25},{28,29}} | collective-permute-start | bytes 3342344 | tf_op jit(solution)/shard_map/ppermute | solution.py:667
  232.1 71.4 %collective-permute-start.7 = (s16[8,272,256]{2,1,0:T(8,128)(2,1)S(1)}, s16[8,272,256]{2,1,0:T(8,128)(2,1)S(1)}, u32[]{:S(2)}, u32[]{:S(2)}) collective-permute-start(s16[8,272,256]{2,1,0:T(8,128)(2,1)S(1)} %copy-done.9), channel_id=1, source_target_pairs={{0,1},{4,5},{8,9},{12,13},{16,17},{20,21},{24,25},{28,29}} | collective-permute-start | bytes 3342344 | tf_op jit(solution)/shard_map/ppermute | solution.py:667
  233.5 83.6 %collective-permute-start.35 = (s16[8,272,256]{2,1,0:T(8,128)(2,1)S(1)}, s16[8,272,256]{2,1,0:T(8,128)(2,1)S(1)}, u32[]{:S(2)}, u32[]{:S(2)}) collective-permute-start(s16[8,272,256]{2,1,0:T(8,128)(2,1)S(1)} %copy-done.10), channel_id=1, source_target_pairs={{0,1},{4,5},{8,9},{12,13},{16,17},{20,21},{24,25},{28,29}} | collective-permute-start | bytes 3342344 | tf_op jit(solution)/shard_map/ppermute | solution.py:667
  255.9 89.9 %copy-start.18 = (s16[8,272,256]{2,1,0:T(8,128)(2,1)}, s16[8,272,256]{2,1,0:T(8,128)(2,1)S(1)}, u32[]{:S(2)}) copy-start(s16[8,272,256]{2,1,0:T(8,128)(2,1)S(1)} %collective-permute-done.45.refs_1_) | copy-start | bytes 3342340
  255.9 61.9 %collective-permute-start.46 = (s16[8,272,256]{2,1,0:T(8,128)(2,1)S(1)}, s16[8,272,256]{2,1,0:T(8,128)(2,1)S(1)}, u32[]{:S(2)}, u32[]{:S(2)}) collective-permute-start(s16[8,272,256]{2,1,0:T(8,128)(2,1)S(1)} %collective-permute-done.45.refs_1_), channel_id=1, source_target_pairs={{1,2},{5,6},{9,10},{13,14},{17,18},{21,22},{25,26},{29,30}} | collective-permute-start | bytes 3342344 | tf_op jit(solution)/shard_map/ppermute | solution.py:667
  279.6 64.4 %copy-start.17 = (s16[8,272,256]{2,1,0:T(8,128)(2,1)}, s16[8,272,256]{2,1,0:T(8,128)(2,1)S(1)}, u32[]{:S(2)}) copy-start(s16[8,272,256]{2,1,0:T(8,128)(2,1)S(1)} %collective-permute-done.17.refs_1_) | copy-start | bytes 3342340
  279.6 61.0 %collective-permute-start.18 = (s16[8,272,256]{2,1,0:T(8,128)(2,1)S(1)}, s16[8,272,256]{2,1,0:T(8,128)(2,1)S(1)}, u32[]{:S(2)}, u32[]{:S(2)}) collective-permute-start(s16[8,272,256]{2,1,0:T(8,128)(2,1)S(1)} %collective-permute-done.17.refs_1_), channel_id=1, source_target_pairs={{1,2},{5,6},{9,10},{13,14},{17,18},{21,22},{25,26},{29,30}} | collective-permute-start | bytes 3342344 | tf_op jit(solution)/shard_map/ppermute | solution.py:667
  303.5 38.9 %collective-permute-start.8 = (s16[8,272,256]{2,1,0:T(8,128)(2,1)S(1)}, s16[8,272,256]{2,1,0:T(8,128)(2,1)S(1)}, u32[]{:S(2)}, u32[]{:S(2)}) collective-permute-start(s16[8,272,256]{2,1,0:T(8,128)(2,1)S(1)} %collective-permute-done.7.refs_1_), channel_id=1, source_target_pairs={{1,2},{5,6},{9,10},{13,14},{17,18},{21,22},{25,26},{29,30}} | collective-permute-start | bytes 3342344 | tf_op jit(solution)/shard_map/ppermute | solution.py:667
  317.0 27.1 %collective-permute-start.36 = (s16[8,272,256]{2,1,0:T(8,128)(2,1)S(1)}, s16[8,272,256]{2,1,0:T(8,128)(2,1)S(1)}, u32[]{:S(2)}, u32[]{:S(2)}) collective-permute-start(s16[8,272,256]{2,1,0:T(8,128)(2,1)S(1)} %collective-permute-done.35.refs_1_), channel_id=1, source_target_pairs={{1,2},{5,6},{9,10},{13,14},{17,18},{21,22},{25,26},{29,30}} | collective-permute-start | bytes 3342344 | tf_op jit(solution)/shard_map/ppermute | solution.py:667
  317.8 28.0 %collective-permute-start.47 = (s16[8,272,256]{2,1,0:T(8,128)(2,1)S(1)}, s16[8,272,256]{2,1,0:T(8,128)(2,1)S(1)}, u32[]{:S(2)}, u32[]{:S(2)}) collective-permute-start(s16[8,272,256]{2,1,0:T(8,128)(2,1)S(1)} %collective-permute-done.46.refs_2_), channel_id=1, source_target_pairs={{2,3},{6,7},{10,11},{14,15},{18,19},{22,23},{26,27},{30,31}} | collective-permute-start | bytes 3342344 | tf_op jit(solution)/shard_map/ppermute | solution.py:667
  340.7 12.0 %collective-permute-start.19 = (s16[8,272,256]{2,1,0:T(8,128)(2,1)S(1)}, s16[8,272,256]{2,1,0:T(8,128)(2,1)}, u32[]{:S(2)}, u32[]{:S(2)}) collective-permute-start(s16[8,272,256]{2,1,0:T(8,128)(2,1)S(1)} %collective-permute-done.18.refs_2_), channel_id=1, source_target_pairs={{2,3},{6,7},{10,11},{14,15},{18,19},{22,23},{26,27},{30,31}} | collective-permute-start | bytes 3342344 | tf_op jit(solution)/shard_map/ppermute | solution.py:667
  342.4 14.8 %collective-permute-start.9 = (s16[8,272,256]{2,1,0:T(8,128)(2,1)S(1)}, s16[8,272,256]{2,1,0:T(8,128)(2,1)}, u32[]{:S(2)}, u32[]{:S(2)}) collective-permute-start(s16[8,272,256]{2,1,0:T(8,128)(2,1)S(1)} %collective-permute-done.8.refs_2_), channel_id=1, source_target_pairs={{2,3},{6,7},{10,11},{14,15},{18,19},{22,23},{26,27},{30,31}} | collective-permute-start | bytes 3342344 | tf_op jit(solution)/shard_map/ppermute | solution.py:667
  344.1 17.8 %collective-permute-start.37 = (s16[8,272,256]{2,1,0:T(8,128)(2,1)S(1)}, s16[8,272,256]{2,1,0:T(8,128)(2,1)}, u32[]{:S(2)}, u32[]{:S(2)}) collective-permute-start(s16[8,272,256]{2,1,0:T(8,128)(2,1)S(1)} %collective-permute-done.36.refs_2_), channel_id=1, source_target_pairs={{2,3},{6,7},{10,11},{14,15},{18,19},{22,23},{26,27},{30,31}} | collective-permute-start | bytes 3342344 | tf_op jit(solution)/shard_map/ppermute | solution.py:667
  348.9 17.8 %collective-permute-start.51 = (s16[8,272,256]{2,1,0:T(8,128)(2,1)}, s16[8,272,256]{2,1,0:T(8,128)(2,1)S(1)}, u32[]{:S(2)}, u32[]{:S(2)}) collective-permute-start(s16[8,272,256]{2,1,0:T(8,128)(2,1)} %pick.13.refs_0_.refs_1_), channel_id=1, source_target_pairs={{0,8},{4,20},{9,25},{13,5},{18,2},{22,30},{27,19},{31,15}} | collective-permute-start | bytes 3342344 | tf_op jit(solution)/shard_map/ppermute | solution.py:671
  354.8 34.1 %collective-permute-start.23 = (s16[8,272,256]{2,1,0:T(8,128)(2,1)}, s16[8,272,256]{2,1,0:T(8,128)(2,1)}, u32[]{:S(2)}, u32[]{:S(2)}) collective-permute-start(s16[8,272,256]{2,1,0:T(8,128)(2,1)} %pick.9.refs_0_.refs_1_), channel_id=1, source_target_pairs={{0,8},{4,20},{9,25},{13,5},{18,2},{22,30},{27,19},{31,15}} | collective-permute-start | bytes 3342344 | tf_op jit(solution)/shard_map/ppermute | solution.py:671
  359.3 94.5 %copy-start.4 = (s16[8,272,256]{2,1,0:T(8,128)(2,1)S(1)}, s16[8,272,256]{2,1,0:T(8,128)(2,1)}, u32[]{:S(2)}) copy-start(s16[8,272,256]{2,1,0:T(8,128)(2,1)} %pick.13.refs_0_.refs_1_) | copy-start | bytes 3342340
  359.3 126.2 %copy-start.44 = (s32[4]{0:T(128)S(1)}, s32[4]{0:T(128)}, u32[]{:S(2)}) copy-start(s32[4]{0:T(128)} %constant.142.clone) | copy-start | bytes 52
  359.3 53.5 %collective-permute-start.20 = (s16[8,272,256]{2,1,0:T(8,128)(2,1)}, s16[8,272,256]{2,1,0:T(8,128)(2,1)}, u32[]{:S(2)}, u32[]{:S(2)}) collective-permute-start(s16[8,272,256]{2,1,0:T(8,128)(2,1)} %pick.8.refs_0_), channel_id=1, source_target_pairs={{0,8},{4,20},{9,25},{13,5},{18,2},{22,30},{27,19},{31,15}} | collective-permute-start | bytes 3342344 | tf_op jit(solution)/shard_map/ppermute | solution.py:671
  364.0 89.8 %collective-permute-start.48 = (s16[8,272,256]{2,1,0:T(8,128)(2,1)}, s16[8,272,256]{2,1,0:T(8,128)(2,1)S(1)}, u32[]{:S(2)}, u32[]{:S(2)}) collective-permute-start(s16[8,272,256]{2,1,0:T(8,128)(2,1)} %pick.12.refs_0_), channel_id=1, source_target_pairs={{0,8},{4,20},{9,25},{13,5},{18,2},{22,30},{27,19},{31,15}} | collective-permute-start | bytes 3342344 | tf_op jit(solution)/shard_map/ppermute | solution.py:671
  365.3 93.3 %collective-permute-start.25 = (s16[8,272,256]{2,1,0:T(8,128)(2,1)S(1)}, s16[8,272,256]{2,1,0:T(8,128)(2,1)S(1)}, u32[]{:S(2)}, u32[]{:S(2)}) collective-permute-start(s16[8,272,256]{2,1,0:T(8,128)(2,1)S(1)} %copy-done), channel_id=1, source_target_pairs={{0,16},{4,12},{9,1},{13,29},{18,26},{22,6},{27,11},{31,23}} | collective-permute-start | bytes 3342344 | tf_op jit(solution)/shard_map/ppermute | solution.py:673
  366.7 124.9 %copy-start.7 = (s16[8,272,256]{2,1,0:T(8,128)(2,1)}, s16[8,272,256]{2,1,0:T(8,128)(2,1)S(1)}, u32[]{:S(2)}) copy-start(s16[8,272,256]{2,1,0:T(8,128)(2,1)S(1)} %collective-permute-done.51.refs_1_) | copy-start | bytes 3342340
  366.7 111.3 %collective-permute-start.22 = (s16[8,272,256]{2,1,0:T(8,128)(2,1)S(1)}, s16[8,272,256]{2,1,0:T(8,128)(2,1)S(1)}, u32[]{:S(2)}, u32[]{:S(2)}) collective-permute-start(s16[8,272,256]{2,1,0:T(8,128)(2,1)S(1)} %copy-done.1), channel_id=1, source_target_pairs={{0,16},{4,12},{9,1},{13,29},{18,26},{22,6},{27,11},{31,23}} | collective-permute-start | bytes 3342344 | tf_op jit(solution)/shard_map/ppermute | solution.py:673
  388.9 93.9 %collective-permute-start.24 = (s16[8,272,256]{2,1,0:T(8,128)(2,1)}, s16[8,272,256]{2,1,0:T(8,128)(2,1)S(1)}, u32[]{:S(2)}, u32[]{:S(2)}) collective-permute-start(s16[8,272,256]{2,1,0:T(8,128)(2,1)} %collective-permute-done.23.refs_1_), channel_id=1, source_target_pairs={{8,24},{20,28},{25,17},{5,21},{2,10},{30,14},{19,3},{15,7}} | collective-permute-start | bytes 3342344 | tf_op jit(solution)/shard_map/ppermute | solution.py:671
  412.8 78.8 %collective-permute-start.21 = (s16[8,272,256]{2,1,0:T(8,128)(2,1)}, s16[8,272,256]{2,1,0:T(8,128)(2,1)}, u32[]{:S(2)}, u32[]{:S(2)}) collective-permute-start(s16[8,272,256]{2,1,0:T(8,128)(2,1)} %collective-permute-done.20.refs_1_), channel_id=1, source_target_pairs={{8,24},{20,28},{25,17},{5,21},{2,10},{30,14},{19,3},{15,7}} | collective-permute-start | bytes 3342344 | tf_op jit(solution)/shard_map/ppermute | solution.py:671
  453.8 47.0 %collective-permute-start.53 = (s16[8,272,256]{2,1,0:T(8,128)(2,1)S(1)}, s16[8,272,256]{2,1,0:T(8,128)(2,1)}, u32[]{:S(2)}, u32[]{:S(2)}) collective-permute-start(s16[8,272,256]{2,1,0:T(8,128)(2,1)S(1)} %copy-done.4), channel_id=1, source_target_pairs={{0,16},{4,12},{9,1},{13,29},{18,26},{22,6},{27,11},{31,23}} | collective-permute-start | bytes 3342344 | tf_op jit(solution)/shard_map/ppermute | solution.py:673
  458.6 48.0 %collective-permute-start.52 = (s16[8,272,256]{2,1,0:T(8,128)(2,1)S(1)}, s16[8,272,256]{2,1,0:T(8,128)(2,1)}, u32[]{:S(2)}, u32[]{:S(2)}) collective-permute-start(s16[8,272,256]{2,1,0:T(8,128)(2,1)S(1)} %collective-permute-done.51.refs_1_), channel_id=1, source_target_pairs={{8,24},{20,28},{25,17},{5,21},{2,10},{30,14},{19,3},{15,7}} | collective-permute-start | bytes 3342344 | tf_op jit(solution)/shard_map/ppermute | solution.py:671
  478.0 36.5 %collective-permute-start.50 = (s16[8,272,256]{2,1,0:T(8,128)(2,1)}, s16[8,272,256]{2,1,0:T(8,128)(2,1)}, u32[]{:S(2)}, u32[]{:S(2)}) collective-permute-start(s16[8,272,256]{2,1,0:T(8,128)(2,1)} %pick.12.refs_0_), channel_id=1, source_target_pairs={{0,16},{4,12},{9,1},{13,29},{18,26},{22,6},{27,11},{31,23}} | collective-permute-start | bytes 3342344 | tf_op jit(solution)/shard_map/ppermute | solution.py:673
  483.8 30.7 %collective-permute-start.49 = (s16[8,272,256]{2,1,0:T(8,128)(2,1)S(1)}, s16[8,272,256]{2,1,0:T(8,128)(2,1)}, u32[]{:S(2)}, u32[]{:S(2)}) collective-permute-start(s16[8,272,256]{2,1,0:T(8,128)(2,1)S(1)} %collective-permute-done.48.refs_1_), channel_id=1, source_target_pairs={{8,24},{20,28},{25,17},{5,21},{2,10},{30,14},{19,3},{15,7}} | collective-permute-start | bytes 3342344 | tf_op jit(solution)/shard_map/ppermute | solution.py:671
  491.6 32.4 %collective-permute-start.27 = (s16[8,272,256]{2,1,0:T(8,128)(2,1)}, s16[8,272,256]{2,1,0:T(8,128)(2,1)S(1)}, u32[]{:S(2)}, u32[]{:S(2)}) collective-permute-start(s16[8,272,256]{2,1,0:T(8,128)(2,1)} %pick.11.refs_3_), channel_id=1, source_target_pairs={{0,4},{1,5},{2,6},{3,7},{4,0},{5,1},{6,2},{7,3},{8,12},{9,13},{10,... | collective-permute-start | bytes 3342344 | tf_op jit(solution)/shard_map/ppermute | solution.py:675
  500.8 23.2 %collective-permute-start.26 = (s16[8,272,256]{2,1,0:T(8,128)(2,1)}, s16[8,272,256]{2,1,0:T(8,128)(2,1)S(1)}, u32[]{:S(2)}, u32[]{:S(2)}) collective-permute-start(s16[8,272,256]{2,1,0:T(8,128)(2,1)} %pick.10.refs_2_), channel_id=1, source_target_pairs={{0,4},{1,5},{2,6},{3,7},{4,0},{5,1},{6,2},{7,3},{8,12},{9,13},{10,... | collective-permute-start | bytes 3342344 | tf_op jit(solution)/shard_map/ppermute | solution.py:675
  508.7 77.3 %collective-permute-start.55 = (s16[8,272,256]{2,1,0:T(8,128)(2,1)}, s16[8,272,256]{2,1,0:T(8,128)(2,1)S(1)}, u32[]{:S(2)}, u32[]{:S(2)}) collective-permute-start(s16[8,272,256]{2,1,0:T(8,128)(2,1)} %pick.15.refs_3_), channel_id=1, source_target_pairs={{0,4},{1,5},{2,6},{3,7},{4,0},{5,1},{6,2},{7,3},{8,12},{9,13},{10,... | collective-permute-start | bytes 3342344 | tf_op jit(solution)/shard_map/ppermute | solution.py:675
  516.6 69.4 %collective-permute-start.54 = (s16[8,272,256]{2,1,0:T(8,128)(2,1)}, s16[8,272,256]{2,1,0:T(8,128)(2,1)S(1)}, u32[]{:S(2)}, u32[]{:S(2)}) collective-permute-start(s16[8,272,256]{2,1,0:T(8,128)(2,1)} %pick.14.refs_2_), channel_id=1, source_target_pairs={{0,4},{1,5},{2,6},{3,7},{4,0},{5,1},{6,2},{7,3},{8,12},{9,13},{10,... | collective-permute-start | bytes 3342344 | tf_op jit(solution)/shard_map/ppermute | solution.py:675
  (39 other events, 515.9 us)
